TPU v7x, 256 devices: a whole 4x4x8 slice. The times are simulated.
256 devices in a mesh: row: 8 (over x, y_lo), col: 32 (over z, y_hi, core).
Axes of the slice: x: 4, y: 4 (y_hi: 2, y_lo: 2; y = y_hi * 2 + y_lo), z: 8, core: 2. Of those that a mesh axis runs over, the one named last changes fastest.
Arguments:
- matrix: bfloat16 [3584, 18432], P('row', 'col'), may hold values from -0.046875 to 0.046875
Outputs:
- update: bfloat16 [3584, 18432], P('row', 'col')
All inputs are finite; a program needn't handle non-finite values.
Results may differ from a plain program's by a relative error of at most 0.0092.
Values may be sent and summed in bfloat16 or wider, within the bound.
No kernel may reach another device: no remote copies, remote signals or barrier semaphores. Data moves between devices by JAX's collectives and lax.ppermute only.
A program may use at most 64 MiB of HBM per device.

v0:
```python
import math

import jax
import jax.numpy as jnp
from jax import lax
from jax.experimental import pallas as pl
from jax.experimental.pallas import tpu as pltpu
from jax.sharding import Mesh
from jax.sharding import PartitionSpec as P


coef_a = 3.4445
coef_b = -4.775
coef_c = 2.0315


SIZES = {"x": 4, "yl": 2, "z": 8, "yh": 2, "c": 2}
AXES = tuple(SIZES)
ROW = ("x", "yl")
COL = ("z", "yh", "c")
RING = SIZES["z"]
PANEL = SIZES["x"] * SIZES["yl"]
FAR = RING // 2
LANES = 128
VMEM_LIMIT = 20 << 20

F32 = jnp.float32
BF16 = jnp.bfloat16
VMEM = pl.BlockSpec(memory_space=pltpu.VMEM)
SMEM = pl.BlockSpec(memory_space=pltpu.SMEM)


def array(shape, kind=BF16):
    return jax.ShapeDtypeStruct(shape, kind)


def shift(value, axis, step):
    size = SIZES[axis]
    return lax.ppermute(value, axis, [((i + step) % size, i) for i in range(size)])


def call(body, place, operands, outs, flops=0, scratch=(), fixed=True, home=False, alias=None):
    if fixed:
        operands = [pltpu.with_memory_space_constraint(a, pltpu.VMEM) for a in operands]
    single = not isinstance(outs, list)
    outs = [outs] if single else outs
    moved = sum(math.prod(a.shape) * 2 for a in (*operands, *outs))
    got = pl.pallas_call(
        body,
        out_shape=outs if home else [pltpu.VMEM(o.shape, o.dtype) for o in outs],
        in_specs=[SMEM] + [VMEM] * len(operands),
        out_specs=[VMEM] * len(outs),
        scratch_shapes=list(scratch),
        input_output_aliases=alias or {},
        cost_estimate=pl.CostEstimate(flops=flops, bytes_accessed=moved, transcendentals=0),
        compiler_params=pltpu.CompilerParams(vmem_limit_bytes=VMEM_LIMIT),
    )(place, *operands)
    return got[0] if single else got


def first_blocks(own):
    return own, shift(own, "x", 1), shift(own, "x", -1), shift(own, "yl", 1)


def more_blocks(first):
    _, _, r30, r01 = first
    return shift(r30, "x", -1), shift(r01, "x", 1), shift(r30, "yl", 1)


def last_block(more):
    _, r11, r31 = more
    half = (r11.shape[0] // 2 + 15) // 16 * 16
    return shift(r11[:half], "x", 1), shift(r31[half:], "x", -1)


def packing(rows, cols):
    width = cols // LANES * LANES
    rest = cols - width
    groups = width // rest
    return width, rest, groups, rows // groups


def pack(block, out):
    rows, cols = block.shape
    width, rest, groups, height = packing(rows, cols)
    out[:rows] = block[:, :width].astype(BF16)
    for g in range(groups):
        out[rows:, g * rest : (g + 1) * rest] = block[g * height : (g + 1) * height, width:].astype(BF16)


def fill(panel, refs):
    half, cols = panel.shape[1:]
    rows = half // 2
    width, rest, groups, height = packing(rows, cols)
    total = rows + height
    at = 0
    for ref in refs:
        size = ref.shape[0]
        block, begin = divmod(at, total)
        i, base = divmod(block * rows, half)
        main = min(size, rows - begin)
        panel[i, base + begin : base + begin + main, :width] = ref[:main]
        if begin + size == total:
            for g in range(groups):
                low = base + g * height
                panel[i, low : low + height, width:] = ref[main:, g * rest : (g + 1) * rest]
        at += size


def pack_body(place, own, packed, copy):
    value = own[...]
    copy[...] = value
    pack(value.astype(F32), packed)


def chunk(z, far, size):
    return pl.ds(pl.multiple_of(lax.rem(z + far, RING) * size, 8), size)


def gram_body(place, own, *refs):
    *blocks, keep, send, panel, rows = refs
    fill(panel, blocks)
    z, c = place[0], place[1]
    dims = (((1,), (1,)), ((), ()))

    @pl.loop(0, 2)
    def _(i):
        rows[i] = lax.dot_general(own[...], panel[i], dims, preferred_element_type=F32)

    size = keep.shape[1]
    for side, out in ((c, keep), (1 - c, send)):
        for far in range(RING):
            out[far] = rows[side, chunk(z, far, size), :].astype(BF16)


def gram_partial(place, own, blocks):
    rows, cols = own.shape
    part = array((RING, rows // RING, 2 * rows))
    panel = array((2, 2 * rows, cols))
    scratch = [pltpu.VMEM((2, rows, 2 * rows), F32)]
    return call(gram_body, place, (own, *blocks), [part, part, panel], 8 * rows * rows * cols, scratch)


def pair_body(place, low, low_other, high, high_other, *outs):
    size = low.shape[1]
    for d in range(RING):
        lower = (low[d].astype(F32) + low_other[d].astype(F32)).astype(BF16)
        upper = (high[d].astype(F32) + high_other[d].astype(F32)).astype(BF16)
        if d == FAR:
            outs[d][...] = lower
            outs[d + 1][...] = upper
        else:
            out = outs[d if d < FAR else d + 1]
            out[:size] = lower
            out[size:] = upper


def add(a, b):
    return (a.astype(F32) + b.astype(F32)).astype(BF16)


def ring_sum(part, up, down):
    size = up.shape[0]
    for step in range(FAR - 1, -1, -1):
        up, down = shift(up, "z", -1), shift(down, "z", 1)
        if step == 0:
            total = part[0].astype(F32) + up.astype(F32) + down.astype(F32)
        elif step == FAR - 1:
            one, two = part[step], part[RING - step]
            up = jnp.concatenate([add(one[:size], up), one[size:]], 0)
            down = jnp.concatenate([two[:size], add(two[size:], down)], 0)
        else:
            up, down = add(part[step], up), add(part[RING - step], down)
    return total.astype(BF16)


def group_body(place, *refs):
    *pieces, out = refs
    for i, ref in enumerate(pieces):
        out[i] = ref[...]


def rows_body(place, low, high, group, other, near, far, total):
    z, c = place[0], place[1]
    size = near.shape[1] // RING
    for side, ref in ((c, group), (1 - c, other)):
        for i in range(RING - 1):
            where = chunk(z, i if i < FAR else i + 1, size)
            near[side, where, :] = ref[i, :size]
            far[side, where, :] = ref[i, size:]
    for side in range(2):
        near[side, chunk(z, FAR, size), :] = jnp.zeros((size, near.shape[2]), BF16)
        far[side, chunk(z, FAR, size), :] = jnp.zeros((size, near.shape[2]), BF16)
    total[...] = jnp.zeros(total.shape, F32)

    @pl.loop(0, 2)
    def _(i):
        total[...] += jnp.dot(near[i], low[i], preferred_element_type=F32) + jnp.dot(
            far[i], high[i], preferred_element_type=F32
        )


def update_body(place, own, low, high, near, far, before, *refs):
    ends, (near_out, far_out, w_high, w_low, total) = refs[:4], refs[4:]
    z, c = place[0], place[1]
    size = near.shape[1] // RING
    where = chunk(z, FAR, size)
    for side, lower, upper in ((c, ends[0], ends[1]), (1 - c, ends[2], ends[3])):
        near_out[side, where, :] = lower[...]
        far_out[side, where, :] = upper[...]
    acc = jnp.zeros((size, own.shape[1]), F32)
    for gram, panel in ((near_out, low), (far_out, high)):
        for i in range(2):
            acc += jnp.dot(gram[i, where, :], panel[i], preferred_element_type=F32)
    total[...] = before[...]
    total[where, :] = acc
    w = coef_b * own[...].astype(F32) + coef_c * total[...]
    pack(w, w_high)
    w_low[...] = (w - w.astype(BF16).astype(F32)).astype(BF16)


def near_body(place, own, w_low, gram, *refs):
    *blocks, total, panel = refs
    rows = own.shape[0]
    fill(panel, blocks)
    acc = coef_a * own[...].astype(F32)
    acc += jnp.dot(gram[0][:, :rows], w_low[...], preferred_element_type=F32)
    total[...] = acc

    @pl.loop(0, 2)
    def _(i):
        total[...] += jnp.dot(gram[i], panel[i], preferred_element_type=F32)


def side_body(place, before, gram, *refs):
    *blocks, total, panel = refs
    fill(panel, blocks)
    total[...] = before[...] + jnp.dot(gram[0], panel[0], preferred_element_type=F32)


def far_body(place, before, gram, *refs):
    *blocks, out, panel = refs
    fill(panel, blocks)
    acc = before[...] + jnp.dot(gram[1], panel[0], preferred_element_type=F32)
    rows, cols = out.shape
    factor = 0.2 * math.sqrt(max(rows * PANEL, cols * math.prod(SIZES[n] for n in COL)))
    out[...] = (acc * factor).astype(BF16)


def newton_step(matrix):
    rows, cols = matrix.shape
    size = rows // RING
    place = jnp.stack([lax.axis_index("z"), lax.axis_index("c")]).astype(jnp.int32)
    width, _, _, height = packing(rows, cols)
    flat = array((rows + height, width))
    block = array((rows, cols))

    packed, own = call(pack_body, place, (matrix,), [flat, block], fixed=False)
    first = lax.optimization_barrier(first_blocks(packed))
    keep, send, low = gram_partial(place, own, first)
    halves = [keep, shift(send, "c", 1)]
    more = lax.optimization_barrier(more_blocks(first))
    last = last_block(more)
    keep, send, high = gram_partial(place, own, (*more, *last))
    halves += [keep, shift(send, "c", 1)]

    one, two = array((size, 2 * rows)), array((2 * size, 2 * rows))
    parts = call(pair_body, place, halves, [two] * FAR + [one] * 2 + [two] * (FAR - 1))
    part = {d: parts[d if d < FAR else d + 1] for d in range(RING) if d != FAR}
    mine = ring_sum(part, parts[FAR], parts[FAR + 1])
    mine = add(mine, shift(mine, "yh", 1))

    ring = {0: mine}
    up, down = mine, mine
    for step in range(1, FAR):
        up, down = lax.optimization_barrier((shift(up, "z", 1), shift(down, "z", -1)))
        ring[step], ring[RING - step] = up, down
    ends = [shift(up[:size], "z", 1)]
    ends.append(shift(down[size:], "z", -1))
    pieces = [ring[d] for d in range(RING) if d != FAR]
    group = call(group_body, place, pieces, array((RING - 1, 2 * size, 2 * rows)))
    ends += [shift(p, "c", 1) for p in ends]

    sums = array((rows, cols), F32)
    wide = array((2, rows, 2 * rows))
    work = 4 * rows * rows * cols
    other = shift(group, "c", 1)
    gram_near, gram_far, total = call(rows_body, place, (low, high, group, other), [wide, wide, sums], 4 * work)
    gram_near, gram_far, w_high, w_low = call(
        update_body,
        place,
        (own, low, high, gram_near, gram_far, total, *ends),
        [wide, wide, flat, block],
        work // 2,
        [pltpu.VMEM((rows, cols), F32)],
        alias={4: 0, 5: 1},
    )

    def panel(count):
        return [pltpu.VMEM((count, 2 * rows, cols), BF16)]

    near = lax.optimization_barrier(first_blocks(w_high))
    total = call(near_body, place, (own, w_low, gram_near, *near), sums, 5 * work // 2, panel(2))
    side = lax.optimization_barrier(more_blocks(near))
    total = call(side_body, place, (total, gram_far, *side[:2]), sums, work, panel(1))
    ends = last_block(side)
    return call(far_body, place, (total, gram_far, side[2], *ends), block, work, panel(1), home=True)


def solution(mesh):
    fine = Mesh(mesh.devices.reshape(tuple(SIZES.values())), AXES)
    return jax.shard_map(newton_step, mesh=fine, in_specs=(P(ROW, COL),), out_specs=P(ROW, COL), check_vma=False)
```

profile of v0, /device:TPU:1, one launch (start us, length us, event | category | flops | bytes accessed | tf_op | source)
XLA Modules:
  0.0 168.6 jit_solution(2904059564731561426)
XLA Ops:
  0.1 1.1 copy-done
  1.1 0.6 shard_map.17
  1.8 2.2 %collective-permute-start.2 = (bf16[504,512]{1,0:T(8,128)(2,1)S(1)}, bf16[504,512]{1,0:T(8,128)(2,1)S(1)}, u32[]{:S(2)}, u32[]{:S(2)}) collective-permute-start(bf16[504,512]{1,0:T(8,128)(2,1)S(1)} %get-tuple-element.51.refs_0_), channel_id=1, source_target_pairs={{32,0},{0,32},{33,1},{1,33},{34,2},{2,34},{35,3},{3,35},{36,4},{4,... | collective-permute-start | bytes 1548296 | tf_op jit(solution)/shard_map/ppermute | solution.py:39
  4.0 1.2 collective-permute-start.1
  5.2 1.5 collective-permute-start
  6.7 7.6 %collective-permute-done.2.refs_3_ = bf16[504,512]{1,0:T(8,128)(2,1)S(1)} collective-permute-done((bf16[504,512]{1,0:T(8,128)(2,1)S(1)}, bf16[504,512]{1,0:T(8,128)(2,1)S(1)}, u32[]{:S(2)}, u32[]{:S(2)}) %collective-permute-start.2) | collective-permute-done | bytes 516128 | tf_op jit(solution)/shard_map/ppermute | solution.py:39
  14.3 3.0 %collective-permute-done.1.refs_2_ = bf16[504,512]{1,0:T(8,128)(2,1)S(1)} collective-permute-done((bf16[504,512]{1,0:T(8,128)(2,1)S(1)}, bf16[504,512]{1,0:T(8,128)(2,1)S(1)}, u32[]{:S(2)}, u32[]{:S(2)}) %collective-permute-start.1) | collective-permute-done | bytes 516128 | tf_op jit(solution)/shard_map/ppermute | solution.py:39
  17.3 2.4 %collective-permute-start.4 = (bf16[504,512]{1,0:T(8,128)(2,1)S(1)}, bf16[504,512]{1,0:T(8,128)(2,1)S(1)}, u32[]{:S(2)}, u32[]{:S(2)}) collective-permute-start(bf16[504,512]{1,0:T(8,128)(2,1)S(1)} %collective-permute-done.2.refs_3_), channel_id=1, source_target_pairs={{64,0},{128,64},{192,128},{0,192},{65,1},{129,65},{193,129},{1,193... | collective-permute-start | bytes 1548296 | tf_op jit(solution)/shard_map/ppermute | solution.py:39
  19.7 8.9 %collective-permute-done.4.refs_1_ = bf16[504,512]{1,0:T(8,128)(2,1)S(1)} collective-permute-done((bf16[504,512]{1,0:T(8,128)(2,1)S(1)}, bf16[504,512]{1,0:T(8,128)(2,1)S(1)}, u32[]{:S(2)}, u32[]{:S(2)}) %collective-permute-start.4) | collective-permute-done | bytes 516128 | tf_op jit(solution)/shard_map/ppermute | solution.py:39
  28.6 1.8 %collective-permute-done.5.refs_2_ = bf16[504,512]{1,0:T(8,128)(2,1)S(1)} collective-permute-done((bf16[504,512]{1,0:T(8,128)(2,1)S(1)}, bf16[504,512]{1,0:T(8,128)(2,1)S(1)}, u32[]{:S(2)}, u32[]{:S(2)}) %collective-permute-start.5) | collective-permute-done | bytes 516128 | tf_op jit(solution)/shard_map/ppermute | solution.py:39
  30.4 0.8 collective-permute-done.3.refs_0_
  31.3 0.7 collective-permute-start.6
  32.0 0.9 collective-permute-start.7
  32.9 2.7 %shard_map.18 = (bf16[8,56,896]{2,1,0:T(8,128)(2,1)S(1)}, bf16[8,56,896]{2,1,0:T(8,128)(2,1)S(1)}, bf16[2,896,576]{2,1,0:T(8,128)(2,1)S(1)}) custom-call(s32[2]{0:T(128)S(1)} %pad_add_fusion.place, bf16[448,576]{1,0:T(8,128)(2,1)S(1)} %get-tuple-element.49.own, bf16[504,512]{1,0:T(8,128)(2,1)S(1)} %get-tuple-element.51.refs_0_, ...), custom_call_target="tpu_custom_call" | custom-call | flops 924844032 | bytes 6250496 | tf_op jit(solution)/shard_map/pallas_call | solution.py:48
  35.7 4.5 %collective-permute-start.8 = (bf16[8,56,896]{2,1,0:T(8,128)(2,1)S(1)}, bf16[8,56,896]{2,1,0:T(8,128)(2,1)S(1)}, u32[]{:S(2)}, u32[]{:S(2)}) collective-permute-start(bf16[8,56,896]{2,1,0:T(8,128)(2,1)S(1)} %get-tuple-element.61), channel_id=1, source_target_pairs={{1,0},{0,1},{3,2},{2,3},{5,4},{4,5},{7,6},{6,7},{9,8},{8,9},{11,10... | collective-permute-start | bytes 2408456 | tf_op jit(solution)/shard_map/ppermute | solution.py:39
  40.1 2.7 %shard_map.19 = (bf16[8,56,896]{2,1,0:T(8,128)(2,1)S(1)}, bf16[8,56,896]{2,1,0:T(8,128)(2,1)S(1)}, bf16[2,896,576]{2,1,0:T(8,128)(2,1)S(1)}) custom-call(s32[2]{0:T(128)S(1)} %pad_add_fusion.place, bf16[448,576]{1,0:T(8,128)(2,1)S(1)} %get-tuple-element.49.own, bf16[504,512]{1,0:T(8,128)(2,1)S(1)} %collective-permute-done.3.refs_0_, ...), custom_call_target="tpu_custom_call" | custom-call | flops 924844032 | bytes 6250496 | tf_op jit(solution)/shard_map/pallas_call | solution.py:48
  42.9 3.0 %collective-permute-start.9 = (bf16[8,56,896]{2,1,0:T(8,128)(2,1)S(1)}, bf16[8,56,896]{2,1,0:T(8,128)(2,1)S(1)}, u32[]{:S(2)}, u32[]{:S(2)}) collective-permute-start(bf16[8,56,896]{2,1,0:T(8,128)(2,1)S(1)} %get-tuple-element.63), channel_id=1, source_target_pairs={{1,0},{0,1},{3,2},{2,3},{5,4},{4,5},{7,6},{6,7},{9,8},{8,9},{11,10... | collective-permute-start | bytes 2408456 | tf_op jit(solution)/shard_map/ppermute | solution.py:39
  45.9 1.9 %collective-permute-done.9.high_other = bf16[8,56,896]{2,1,0:T(8,128)(2,1)S(1)} collective-permute-done((bf16[8,56,896]{2,1,0:T(8,128)(2,1)S(1)}, bf16[8,56,896]{2,1,0:T(8,128)(2,1)S(1)}, u32[]{:S(2)}, u32[]{:S(2)}) %collective-permute-start.9) | collective-permute-done | bytes 802848 | tf_op jit(solution)/shard_map/ppermute | solution.py:39
  47.8 0.9 shard_map.20
  48.7 5.9 %collective-permute-start.14 = (bf16[56,896]{1,0:T(8,128)(2,1)S(1)}, bf16[56,896]{1,0:T(8,128)(2,1)S(1)}, u32[]{:S(2)}, u32[]{:S(2)}) collective-permute-start(bf16[56,896]{1,0:T(8,128)(2,1)S(1)} %get-tuple-element.72), channel_id=1, source_target_pairs={{4,0},{8,4},{12,8},{16,12},{20,16},{24,20},{28,24},{0,28},{5,1},{9... | collective-permute-start | bytes 301064 | tf_op jit(solution)/shard_map/ppermute | solution.py:39
  54.6 0.1 collective-permute-start.10
  54.7 1.7 %collective-permute-done.14 = bf16[56,896]{1,0:T(8,128)(2,1)S(1)} collective-permute-done((bf16[56,896]{1,0:T(8,128)(2,1)S(1)}, bf16[56,896]{1,0:T(8,128)(2,1)S(1)}, u32[]{:S(2)}, u32[]{:S(2)}) %collective-permute-start.14) | collective-permute-done | bytes 100384 | tf_op jit(solution)/shard_map/ppermute | solution.py:39
  56.5 3.5 %collective-permute-start.15 = (bf16[112,896]{1,0:T(8,128)(2,1)S(1)}, bf16[112,896]{1,0:T(8,128)(2,1)S(1)}, u32[]{:S(2)}, u32[]{:S(2)}) collective-permute-start(bf16[112,896]{1,0:T(8,128)(2,1)S(1)} %pad_maximum_fusion.1), channel_id=1, source_target_pairs={{4,0},{8,4},{12,8},{16,12},{20,16},{24,20},{28,24},{0,28},{5,1},{9... | collective-permute-start | bytes 602120 | tf_op jit(solution)/shard_map/ppermute | solution.py:39
  60.0 0.3 collective-permute-start.11
  60.3 2.8 %collective-permute-done.15 = bf16[112,896]{1,0:T(8,128)(2,1)S(1)} collective-permute-done((bf16[112,896]{1,0:T(8,128)(2,1)S(1)}, bf16[112,896]{1,0:T(8,128)(2,1)S(1)}, u32[]{:S(2)}, u32[]{:S(2)}) %collective-permute-start.15) | collective-permute-done | bytes 200736 | tf_op jit(solution)/shard_map/ppermute | solution.py:39
  63.2 3.5 %collective-permute-start.16 = (bf16[112,896]{1,0:T(8,128)(2,1)S(1)}, bf16[112,896]{1,0:T(8,128)(2,1)S(1)}, u32[]{:S(2)}, u32[]{:S(2)}) collective-permute-start(bf16[112,896]{1,0:T(8,128)(2,1)S(1)} %add_convert_fusion.3), channel_id=1, source_target_pairs={{4,0},{8,4},{12,8},{16,12},{20,16},{24,20},{28,24},{0,28},{5,1},{9... | collective-permute-start | bytes 602120 | tf_op jit(solution)/shard_map/ppermute | solution.py:39
  66.8 2.5 %collective-permute-done.16 = bf16[112,896]{1,0:T(8,128)(2,1)S(1)} collective-permute-done((bf16[112,896]{1,0:T(8,128)(2,1)S(1)}, bf16[112,896]{1,0:T(8,128)(2,1)S(1)}, u32[]{:S(2)}, u32[]{:S(2)}) %collective-permute-start.16) | collective-permute-done | bytes 200736 | tf_op jit(solution)/shard_map/ppermute | solution.py:39
  69.4 3.2 %collective-permute-start.17 = (bf16[112,896]{1,0:T(8,128)(2,1)S(1)}, bf16[112,896]{1,0:T(8,128)(2,1)S(1)}, u32[]{:S(2)}, u32[]{:S(2)}) collective-permute-start(bf16[112,896]{1,0:T(8,128)(2,1)S(1)} %add_convert_fusion.2), channel_id=1, source_target_pairs={{4,0},{8,4},{12,8},{16,12},{20,16},{24,20},{28,24},{0,28},{5,1},{9... | collective-permute-start | bytes 602120 | tf_op jit(solution)/shard_map/ppermute | solution.py:39
  72.7 2.5 %collective-permute-done.17 = bf16[112,896]{1,0:T(8,128)(2,1)S(1)} collective-permute-done((bf16[112,896]{1,0:T(8,128)(2,1)S(1)}, bf16[112,896]{1,0:T(8,128)(2,1)S(1)}, u32[]{:S(2)}, u32[]{:S(2)}) %collective-permute-start.17) | collective-permute-done | bytes 200736 | tf_op jit(solution)/shard_map/ppermute | solution.py:39
  75.2 3.3 %collective-permute-done.13 = bf16[112,896]{1,0:T(8,128)(2,1)S(1)} collective-permute-done((bf16[112,896]{1,0:T(8,128)(2,1)S(1)}, bf16[112,896]{1,0:T(8,128)(2,1)S(1)}, u32[]{:S(2)}, u32[]{:S(2)}) %collective-permute-start.13) | collective-permute-done | bytes 200736 | tf_op jit(solution)/shard_map/ppermute | solution.py:39
  78.6 2.9 %collective-permute-start.18 = (bf16[112,896]{1,0:T(8,128)(2,1)S(1)}, bf16[112,896]{1,0:T(8,128)(2,1)S(1)}, u32[]{:S(2)}, u32[]{:S(2)}) collective-permute-start(bf16[112,896]{1,0:T(8,128)(2,1)S(1)} %add_convert_fusion.1), channel_id=1, source_target_pairs={{2,0},{0,2},{3,1},{1,3},{6,4},{4,6},{7,5},{5,7},{10,8},{8,10},{11,... | collective-permute-start | bytes 602120 | tf_op jit(solution)/shard_map/ppermute | solution.py:39
  81.4 3.3 %collective-permute-done.18 = bf16[112,896]{1,0:T(8,128)(2,1)S(1)} collective-permute-done((bf16[112,896]{1,0:T(8,128)(2,1)S(1)}, bf16[112,896]{1,0:T(8,128)(2,1)S(1)}, u32[]{:S(2)}, u32[]{:S(2)}) %collective-permute-start.18) | collective-permute-done | bytes 200736 | tf_op jit(solution)/shard_map/ppermute | solution.py:39
  84.9 2.7 %collective-permute-start.19 = (bf16[112,896]{1,0:T(8,128)(2,1)S(1)}, bf16[112,896]{1,0:T(8,128)(2,1)S(1)}, u32[]{:S(2)}, u32[]{:S(2)}) collective-permute-start(bf16[112,896]{1,0:T(8,128)(2,1)S(1)} %add_convert_fusion.refs_0_), channel_id=1, source_target_pairs={{4,0},{8,4},{12,8},{16,12},{20,16},{24,20},{28,24},{0,28},{5,1},{9... | collective-permute-start | bytes 602120 | tf_op jit(solution)/shard_map/ppermute | solution.py:39
  87.5 3.1 %collective-permute-done.20.refs_6_ = bf16[112,896]{1,0:T(8,128)(2,1)S(1)} collective-permute-done((bf16[112,896]{1,0:T(8,128)(2,1)S(1)}, bf16[112,896]{1,0:T(8,128)(2,1)S(1)}, u32[]{:S(2)}, u32[]{:S(2)}) %collective-permute-start.20) | collective-permute-done | bytes 200736 | tf_op jit(solution)/shard_map/ppermute | solution.py:39
  90.6 2.7 %collective-permute-start.21 = (bf16[112,896]{1,0:T(8,128)(2,1)S(1)}, bf16[112,896]{1,0:T(8,128)(2,1)S(1)}, u32[]{:S(2)}, u32[]{:S(2)}) collective-permute-start(bf16[112,896]{1,0:T(8,128)(2,1)S(1)} %collective-permute-done.19.refs_1_), channel_id=1, source_target_pairs={{4,0},{8,4},{12,8},{16,12},{20,16},{24,20},{28,24},{0,28},{5,1},{9... | collective-permute-start | bytes 602120 | tf_op jit(solution)/shard_map/ppermute | solution.py:39
  93.3 4.0 %collective-permute-done.21.refs_2_ = bf16[112,896]{1,0:T(8,128)(2,1)S(1)} collective-permute-done((bf16[112,896]{1,0:T(8,128)(2,1)S(1)}, bf16[112,896]{1,0:T(8,128)(2,1)S(1)}, u32[]{:S(2)}, u32[]{:S(2)}) %collective-permute-start.21) | collective-permute-done | bytes 200736 | tf_op jit(solution)/shard_map/ppermute | solution.py:39
  97.3 1.7 %collective-permute-done.22.refs_5_ = bf16[112,896]{1,0:T(8,128)(2,1)S(1)} collective-permute-done((bf16[112,896]{1,0:T(8,128)(2,1)S(1)}, bf16[112,896]{1,0:T(8,128)(2,1)S(1)}, u32[]{:S(2)}, u32[]{:S(2)}) %collective-permute-start.22) | collective-permute-done | bytes 200736 | tf_op jit(solution)/shard_map/ppermute | solution.py:39
  99.1 1.7 collective-permute-start.23
  100.7 5.1 %collective-permute-done.23.refs_3_ = bf16[112,896]{1,0:T(8,128)(2,1)S(1)} collective-permute-done((bf16[112,896]{1,0:T(8,128)(2,1)S(1)}, bf16[112,896]{1,0:T(8,128)(2,1)S(1)}, u32[]{:S(2)}, u32[]{:S(2)}) %collective-permute-start.23) | collective-permute-done | bytes 200736 | tf_op jit(solution)/shard_map/ppermute | solution.py:39
  105.9 1.2 collective-permute-done.24.refs_4_
  107.0 0.6 shard_map.21.group
  107.7 9.6 %collective-permute-start.25 = (bf16[7,112,896]{2,1,0:T(8,128)(2,1)S(1)}, bf16[7,112,896]{2,1,0:T(8,128)(2,1)S(1)}, u32[]{:S(2)}, u32[]{:S(2)}) collective-permute-start(bf16[7,112,896]{2,1,0:T(8,128)(2,1)S(1)} %shard_map.21.group), channel_id=1, source_target_pairs={{1,0},{0,1},{3,2},{2,3},{5,4},{4,5},{7,6},{6,7},{9,8},{8,9},{11,10... | collective-permute-start | bytes 4214792 | tf_op jit(solution)/shard_map/ppermute | solution.py:39
  117.3 0.3 collective-permute-start.27
  117.7 2.5 %collective-permute-start.26 = (bf16[56,896]{1,0:T(8,128)(2,1)S(1)}, bf16[56,896]{1,0:T(8,128)(2,1)S(1)}, u32[]{:S(2)}, u32[]{:S(2)}) collective-permute-start(bf16[56,896]{1,0:T(8,128)(2,1)S(1)} %slice.36), channel_id=1, source_target_pairs={{4,0},{8,4},{12,8},{16,12},{20,16},{24,20},{28,24},{0,28},{5,1},{9... | collective-permute-start | bytes 301064 | tf_op jit(solution)/shard_map/ppermute | solution.py:39
  120.2 2.8 %collective-permute-done.27.refs_1_ = bf16[56,896]{1,0:T(8,128)(2,1)S(1)} collective-permute-done((bf16[56,896]{1,0:T(8,128)(2,1)S(1)}, bf16[56,896]{1,0:T(8,128)(2,1)S(1)}, u32[]{:S(2)}, u32[]{:S(2)}) %collective-permute-start.27) | collective-permute-done | bytes 100384 | tf_op jit(solution)/shard_map/ppermute | solution.py:39
  123.0 0.9 collective-permute-start.29
  123.9 4.0 %shard_map.22 = (bf16[2,448,896]{2,1,0:T(8,128)(2,1)S(1)}, bf16[2,448,896]{2,1,0:T(8,128)(2,1)S(1)}, f32[448,576]{1,0:T(8,128)S(1)}) custom-call(s32[2]{0:T(128)S(1)} %pad_add_fusion.place, bf16[2,896,576]{2,1,0:T(8,128)(2,1)S(1)} %get-tuple-element.55.low, bf16[2,896,576]{2,1,0:T(8,128)(2,1)S(1)} %get-tuple-element.59.high, ...), custom_call_target="tpu_custom_call" | custom-call | flops 1849688064 | bytes 10665984 | tf_op jit(solution)/shard_map/pallas_call | solution.py:48
  127.9 1.9 %shard_map.23 = (bf16[2,448,896]{2,1,0:T(8,128)(2,1)S(1)}, bf16[2,448,896]{2,1,0:T(8,128)(2,1)S(1)}, bf16[504,512]{1,0:T(8,128)(2,1)S(1)}, bf16[448,576]{1,0:T(8,128)(2,1)S(1)}) custom-call(s32[2]{0:T(128)S(1)} %pad_add_fusion.place, bf16[448,576]{1,0:T(8,128)(2,1)S(1)} %get-tuple-element.49.own, ...), custom_call_target="tpu_custom_call", output_to_operand_aliasing={{0}: (4, {}), {1}: (5, {})} | custom-call | flops 231211008 | bytes 13017088 | tf_op jit(solution)/shard_map/pallas_call | solution.py:48
  129.8 1.3 collective-permute-start.32
  131.1 0.5 collective-permute-start.31
  131.6 2.2 %collective-permute-start.30 = (bf16[504,512]{1,0:T(8,128)(2,1)S(1)}, bf16[504,512]{1,0:T(8,128)(2,1)S(1)}, u32[]{:S(2)}, u32[]{:S(2)}) collective-permute-start(bf16[504,512]{1,0:T(8,128)(2,1)S(1)} %get-tuple-element.85.refs_0_), channel_id=1, source_target_pairs={{64,0},{128,64},{192,128},{0,192},{65,1},{129,65},{193,129},{1,193... | collective-permute-start | bytes 1548296 | tf_op jit(solution)/shard_map/ppermute | solution.py:39
  133.8 8.9 %collective-permute-done.32.refs_3_ = bf16[504,512]{1,0:T(8,128)(2,1)S(1)} collective-permute-done((bf16[504,512]{1,0:T(8,128)(2,1)S(1)}, bf16[504,512]{1,0:T(8,128)(2,1)S(1)}, u32[]{:S(2)}, u32[]{:S(2)}) %collective-permute-start.32) | collective-permute-done | bytes 516128 | tf_op jit(solution)/shard_map/ppermute | solution.py:39
  142.7 2.1 %collective-permute-done.31.refs_2_ = bf16[504,512]{1,0:T(8,128)(2,1)S(1)} collective-permute-done((bf16[504,512]{1,0:T(8,128)(2,1)S(1)}, bf16[504,512]{1,0:T(8,128)(2,1)S(1)}, u32[]{:S(2)}, u32[]{:S(2)}) %collective-permute-start.31) | collective-permute-done | bytes 516128 | tf_op jit(solution)/shard_map/ppermute | solution.py:39
  144.8 2.4 %collective-permute-start.34 = (bf16[504,512]{1,0:T(8,128)(2,1)S(1)}, bf16[504,512]{1,0:T(8,128)(2,1)S(1)}, u32[]{:S(2)}, u32[]{:S(2)}) collective-permute-start(bf16[504,512]{1,0:T(8,128)(2,1)S(1)} %collective-permute-done.32.refs_3_), channel_id=1, source_target_pairs={{64,0},{128,64},{192,128},{0,192},{65,1},{129,65},{193,129},{1,193... | collective-permute-start | bytes 1548296 | tf_op jit(solution)/shard_map/ppermute | solution.py:39
  147.2 0.3 collective-permute-start.35
  147.5 9.0 %collective-permute-done.34.refs_1_ = bf16[504,512]{1,0:T(8,128)(2,1)S(1)} collective-permute-done((bf16[504,512]{1,0:T(8,128)(2,1)S(1)}, bf16[504,512]{1,0:T(8,128)(2,1)S(1)}, u32[]{:S(2)}, u32[]{:S(2)}) %collective-permute-start.34) | collective-permute-done | bytes 516128 | tf_op jit(solution)/shard_map/ppermute | solution.py:39
  156.5 1.8 %collective-permute-done.35.refs_0_ = bf16[504,512]{1,0:T(8,128)(2,1)S(1)} collective-permute-done((bf16[504,512]{1,0:T(8,128)(2,1)S(1)}, bf16[504,512]{1,0:T(8,128)(2,1)S(1)}, u32[]{:S(2)}, u32[]{:S(2)}) %collective-permute-start.35) | collective-permute-done | bytes 516128 | tf_op jit(solution)/shard_map/ppermute | solution.py:39
  158.3 1.2 collective-permute-done.33.refs_0_
  159.6 0.4 collective-permute-start.36
  160.0 1.3 collective-permute-start.37
  161.2 3.0 %shard_map.24.before = f32[448,576]{1,0:T(8,128)S(1)} custom-call(s32[2]{0:T(128)S(1)} %pad_add_fusion.place, bf16[448,576]{1,0:T(8,128)(2,1)S(1)} %get-tuple-element.49.own, bf16[448,576]{1,0:T(8,128)(2,1)S(1)} %get-tuple-element.82.w_low, bf16[2,448,896]{2,1,0:T(8,128)(2,1)S(1)} %get-tuple-element.83.gram, bf16[504,512]{1,0:T(8,128)(2,1)S(1)} %get-tuple-element.85.refs_0_, ...), custom_call_target="tpu_custom_call" | custom-call | flops 1156055040 | bytes 5218304 | tf_op jit(solution)/shard_map/pallas_call | solution.py:48
  164.2 1.4 shard_map.25.before
  165.7 0.7 collective-permute-done.37.refs_2_
  166.4 2.2 %shard_map.26 = bf16[448,576]{1,0:T(8,128)(2,1)} custom-call(s32[2]{0:T(128)S(1)} %pad_add_fusion.place, f32[448,576]{1,0:T(8,128)S(1)} %shard_map.25.before, bf16[2,448,896]{2,1,0:T(8,128)(2,1)S(1)} %get-tuple-element.89.gram, bf16[504,512]{1,0:T(8,128)(2,1)S(1)} %collective-permute-done.35.refs_0_, bf16[256,512]{1,0:T(8,128)(2,1)S(1)} %collective-permute-done.36.refs_1_, ...), custom_call_target="tpu_custom_call" | custom-call | flops 462422016 | bytes 3670016 | tf_op jit(solution)/shard_map/pallas_call | solution.py:48
  (43 shorter events, 0.9 us)
Async XLA Ops:
  0.1 1.1 copy-start
  1.8 12.5 %collective-permute-start.2 = (bf16[504,512]{1,0:T(8,128)(2,1)S(1)}, bf16[504,512]{1,0:T(8,128)(2,1)S(1)}, u32[]{:S(2)}, u32[]{:S(2)}) collective-permute-start(bf16[504,512]{1,0:T(8,128)(2,1)S(1)} %get-tuple-element.51.refs_0_), channel_id=1, source_target_pairs={{32,0},{0,32},{33,1},{1,33},{34,2},{2,34},{35,3},{3,35},{36,4},{4,... | collective-permute-start | bytes 1548296 | tf_op jit(solution)/shard_map/ppermute | solution.py:39
  4.0 13.3 %collective-permute-start.1 = (bf16[504,512]{1,0:T(8,128)(2,1)S(1)}, bf16[504,512]{1,0:T(8,128)(2,1)S(1)}, u32[]{:S(2)}, u32[]{:S(2)}) collective-permute-start(bf16[504,512]{1,0:T(8,128)(2,1)S(1)} %get-tuple-element.51.refs_0_), channel_id=1, source_target_pairs={{192,0},{0,64},{64,128},{128,192},{193,1},{1,65},{65,129},{129,193... | collective-permute-start | bytes 1548296 | tf_op jit(solution)/shard_map/ppermute | solution.py:39
  5.2 12.1 %collective-permute-start = (bf16[504,512]{1,0:T(8,128)(2,1)S(1)}, bf16[504,512]{1,0:T(8,128)(2,1)S(1)}, u32[]{:S(2)}, u32[]{:S(2)}) collective-permute-start(bf16[504,512]{1,0:T(8,128)(2,1)S(1)} %get-tuple-element.51.refs_0_), channel_id=1, source_target_pairs={{64,0},{128,64},{192,128},{0,192},{65,1},{129,65},{193,129},{1,193... | collective-permute-start | bytes 1548296 | tf_op jit(solution)/shard_map/ppermute | solution.py:39
  17.3 11.3 %collective-permute-start.4 = (bf16[504,512]{1,0:T(8,128)(2,1)S(1)}, bf16[504,512]{1,0:T(8,128)(2,1)S(1)}, u32[]{:S(2)}, u32[]{:S(2)}) collective-permute-start(bf16[504,512]{1,0:T(8,128)(2,1)S(1)} %collective-permute-done.2.refs_3_), channel_id=1, source_target_pairs={{64,0},{128,64},{192,128},{0,192},{65,1},{129,65},{193,129},{1,193... | collective-permute-start | bytes 1548296 | tf_op jit(solution)/shard_map/ppermute | solution.py:39
  19.7 10.7 %collective-permute-start.5 = (bf16[504,512]{1,0:T(8,128)(2,1)S(1)}, bf16[504,512]{1,0:T(8,128)(2,1)S(1)}, u32[]{:S(2)}, u32[]{:S(2)}) collective-permute-start(bf16[504,512]{1,0:T(8,128)(2,1)S(1)} %collective-permute-done.1.refs_2_), channel_id=1, source_target_pairs={{32,0},{0,32},{33,1},{1,33},{34,2},{2,34},{35,3},{3,35},{36,4},{4,... | collective-permute-start | bytes 1548296 | tf_op jit(solution)/shard_map/ppermute | solution.py:39
  19.7 11.6 %collective-permute-start.3 = (bf16[504,512]{1,0:T(8,128)(2,1)S(1)}, bf16[504,512]{1,0:T(8,128)(2,1)S(1)}, u32[]{:S(2)}, u32[]{:S(2)}) collective-permute-start(bf16[504,512]{1,0:T(8,128)(2,1)S(1)} %collective-permute-done.1.refs_2_), channel_id=1, source_target_pairs={{192,0},{0,64},{64,128},{128,192},{193,1},{1,65},{65,129},{129,193... | collective-permute-start | bytes 1548296 | tf_op jit(solution)/shard_map/ppermute | solution.py:39
  31.3 8.8 %collective-permute-start.6 = (bf16[256,512]{1,0:T(8,128)(2,1)S(1)}, bf16[256,512]{1,0:T(8,128)(2,1)S(1)}, u32[]{:S(2)}, u32[]{:S(2)}) collective-permute-start(bf16[256,512]{1,0:T(8,128)(2,1)S(1)} %slice.30), channel_id=1, source_target_pairs={{64,0},{128,64},{192,128},{0,192},{65,1},{129,65},{193,129},{1,193... | collective-permute-start | bytes 786440 | tf_op jit(solution)/shard_map/ppermute | solution.py:39
  32.0 8.1 %collective-permute-start.7 = (bf16[248,512]{1,0:T(8,128)(2,1)S(1)}, bf16[248,512]{1,0:T(8,128)(2,1)S(1)}, u32[]{:S(2)}, u32[]{:S(2)}) collective-permute-start(bf16[248,512]{1,0:T(8,128)(2,1)S(1)} %slice.31), channel_id=1, source_target_pairs={{192,0},{0,64},{64,128},{128,192},{193,1},{1,65},{65,129},{129,193... | collective-permute-start | bytes 761864 | tf_op jit(solution)/shard_map/ppermute | solution.py:39
  35.7 10.2 %collective-permute-start.8 = (bf16[8,56,896]{2,1,0:T(8,128)(2,1)S(1)}, bf16[8,56,896]{2,1,0:T(8,128)(2,1)S(1)}, u32[]{:S(2)}, u32[]{:S(2)}) collective-permute-start(bf16[8,56,896]{2,1,0:T(8,128)(2,1)S(1)} %get-tuple-element.61), channel_id=1, source_target_pairs={{1,0},{0,1},{3,2},{2,3},{5,4},{4,5},{7,6},{6,7},{9,8},{8,9},{11,10... | collective-permute-start | bytes 2408456 | tf_op jit(solution)/shard_map/ppermute | solution.py:39
  42.9 5.0 %collective-permute-start.9 = (bf16[8,56,896]{2,1,0:T(8,128)(2,1)S(1)}, bf16[8,56,896]{2,1,0:T(8,128)(2,1)S(1)}, u32[]{:S(2)}, u32[]{:S(2)}) collective-permute-start(bf16[8,56,896]{2,1,0:T(8,128)(2,1)S(1)} %get-tuple-element.63), channel_id=1, source_target_pairs={{1,0},{0,1},{3,2},{2,3},{5,4},{4,5},{7,6},{6,7},{9,8},{8,9},{11,10... | collective-permute-start | bytes 2408456 | tf_op jit(solution)/shard_map/ppermute | solution.py:39
  48.7 7.7 %collective-permute-start.14 = (bf16[56,896]{1,0:T(8,128)(2,1)S(1)}, bf16[56,896]{1,0:T(8,128)(2,1)S(1)}, u32[]{:S(2)}, u32[]{:S(2)}) collective-permute-start(bf16[56,896]{1,0:T(8,128)(2,1)S(1)} %get-tuple-element.72), channel_id=1, source_target_pairs={{4,0},{8,4},{12,8},{16,12},{20,16},{24,20},{28,24},{0,28},{5,1},{9... | collective-permute-start | bytes 301064 | tf_op jit(solution)/shard_map/ppermute | solution.py:39
  54.6 5.3 %collective-permute-start.10 = (bf16[56,896]{1,0:T(8,128)(2,1)S(1)}, bf16[56,896]{1,0:T(8,128)(2,1)S(1)}, u32[]{:S(2)}, u32[]{:S(2)}) collective-permute-start(bf16[56,896]{1,0:T(8,128)(2,1)S(1)} %get-tuple-element.68), channel_id=1, source_target_pairs={{28,0},{0,4},{4,8},{8,12},{12,16},{16,20},{20,24},{24,28},{29,1},{... | collective-permute-start | bytes 301064 | tf_op jit(solution)/shard_map/ppermute | solution.py:39
  56.5 6.6 %collective-permute-start.15 = (bf16[112,896]{1,0:T(8,128)(2,1)S(1)}, bf16[112,896]{1,0:T(8,128)(2,1)S(1)}, u32[]{:S(2)}, u32[]{:S(2)}) collective-permute-start(bf16[112,896]{1,0:T(8,128)(2,1)S(1)} %pad_maximum_fusion.1), channel_id=1, source_target_pairs={{4,0},{8,4},{12,8},{16,12},{20,16},{24,20},{28,24},{0,28},{5,1},{9... | collective-permute-start | bytes 602120 | tf_op jit(solution)/shard_map/ppermute | solution.py:39
  60.0 6.6 %collective-permute-start.11 = (bf16[112,896]{1,0:T(8,128)(2,1)S(1)}, bf16[112,896]{1,0:T(8,128)(2,1)S(1)}, u32[]{:S(2)}, u32[]{:S(2)}) collective-permute-start(bf16[112,896]{1,0:T(8,128)(2,1)S(1)} %pad_maximum_fusion), channel_id=1, source_target_pairs={{28,0},{0,4},{4,8},{8,12},{12,16},{16,20},{20,24},{24,28},{29,1},{... | collective-permute-start | bytes 602120 | tf_op jit(solution)/shard_map/ppermute | solution.py:39
  63.2 6.1 %collective-permute-start.16 = (bf16[112,896]{1,0:T(8,128)(2,1)S(1)}, bf16[112,896]{1,0:T(8,128)(2,1)S(1)}, u32[]{:S(2)}, u32[]{:S(2)}) collective-permute-start(bf16[112,896]{1,0:T(8,128)(2,1)S(1)} %add_convert_fusion.3), channel_id=1, source_target_pairs={{4,0},{8,4},{12,8},{16,12},{20,16},{24,20},{28,24},{0,28},{5,1},{9... | collective-permute-start | bytes 602120 | tf_op jit(solution)/shard_map/ppermute | solution.py:39
  66.7 5.9 %collective-permute-start.12 = (bf16[112,896]{1,0:T(8,128)(2,1)S(1)}, bf16[112,896]{1,0:T(8,128)(2,1)S(1)}, u32[]{:S(2)}, u32[]{:S(2)}) collective-permute-start(bf16[112,896]{1,0:T(8,128)(2,1)S(1)} %add_convert_fusion.5), channel_id=1, source_target_pairs={{28,0},{0,4},{4,8},{8,12},{12,16},{16,20},{20,24},{24,28},{29,1},{... | collective-permute-start | bytes 602120 | tf_op jit(solution)/shard_map/ppermute | solution.py:39
  69.4 5.9 %collective-permute-start.17 = (bf16[112,896]{1,0:T(8,128)(2,1)S(1)}, bf16[112,896]{1,0:T(8,128)(2,1)S(1)}, u32[]{:S(2)}, u32[]{:S(2)}) collective-permute-start(bf16[112,896]{1,0:T(8,128)(2,1)S(1)} %add_convert_fusion.2), channel_id=1, source_target_pairs={{4,0},{8,4},{12,8},{16,12},{20,16},{24,20},{28,24},{0,28},{5,1},{9... | collective-permute-start | bytes 602120 | tf_op jit(solution)/shard_map/ppermute | solution.py:39
  72.6 5.9 %collective-permute-start.13 = (bf16[112,896]{1,0:T(8,128)(2,1)S(1)}, bf16[112,896]{1,0:T(8,128)(2,1)S(1)}, u32[]{:S(2)}, u32[]{:S(2)}) collective-permute-start(bf16[112,896]{1,0:T(8,128)(2,1)S(1)} %add_convert_fusion.4), channel_id=1, source_target_pairs={{28,0},{0,4},{4,8},{8,12},{12,16},{16,20},{20,24},{24,28},{29,1},{... | collective-permute-start | bytes 602120 | tf_op jit(solution)/shard_map/ppermute | solution.py:39
  78.6 6.2 %collective-permute-start.18 = (bf16[112,896]{1,0:T(8,128)(2,1)S(1)}, bf16[112,896]{1,0:T(8,128)(2,1)S(1)}, u32[]{:S(2)}, u32[]{:S(2)}) collective-permute-start(bf16[112,896]{1,0:T(8,128)(2,1)S(1)} %add_convert_fusion.1), channel_id=1, source_target_pairs={{2,0},{0,2},{3,1},{1,3},{6,4},{4,6},{7,5},{5,7},{10,8},{8,10},{11,... | collective-permute-start | bytes 602120 | tf_op jit(solution)/shard_map/ppermute | solution.py:39
  84.8 5.9 %collective-permute-start.20 = (bf16[112,896]{1,0:T(8,128)(2,1)S(1)}, bf16[112,896]{1,0:T(8,128)(2,1)S(1)}, u32[]{:S(2)}, u32[]{:S(2)}) collective-permute-start(bf16[112,896]{1,0:T(8,128)(2,1)S(1)} %add_convert_fusion.refs_0_), channel_id=1, source_target_pairs={{28,0},{0,4},{4,8},{8,12},{12,16},{16,20},{20,24},{24,28},{29,1},{... | collective-permute-start | bytes 602120 | tf_op jit(solution)/shard_map/ppermute | solution.py:39
  84.9 5.8 %collective-permute-start.19 = (bf16[112,896]{1,0:T(8,128)(2,1)S(1)}, bf16[112,896]{1,0:T(8,128)(2,1)S(1)}, u32[]{:S(2)}, u32[]{:S(2)}) collective-permute-start(bf16[112,896]{1,0:T(8,128)(2,1)S(1)} %add_convert_fusion.refs_0_), channel_id=1, source_target_pairs={{4,0},{8,4},{12,8},{16,12},{20,16},{24,20},{28,24},{0,28},{5,1},{9... | collective-permute-start | bytes 602120 | tf_op jit(solution)/shard_map/ppermute | solution.py:39
  90.6 6.7 %collective-permute-start.21 = (bf16[112,896]{1,0:T(8,128)(2,1)S(1)}, bf16[112,896]{1,0:T(8,128)(2,1)S(1)}, u32[]{:S(2)}, u32[]{:S(2)}) collective-permute-start(bf16[112,896]{1,0:T(8,128)(2,1)S(1)} %collective-permute-done.19.refs_1_), channel_id=1, source_target_pairs={{4,0},{8,4},{12,8},{16,12},{20,16},{24,20},{28,24},{0,28},{5,1},{9... | collective-permute-start | bytes 602120 | tf_op jit(solution)/shard_map/ppermute | solution.py:39
  93.3 5.8 %collective-permute-start.22 = (bf16[112,896]{1,0:T(8,128)(2,1)S(1)}, bf16[112,896]{1,0:T(8,128)(2,1)S(1)}, u32[]{:S(2)}, u32[]{:S(2)}) collective-permute-start(bf16[112,896]{1,0:T(8,128)(2,1)S(1)} %collective-permute-done.20.refs_6_), channel_id=1, source_target_pairs={{28,0},{0,4},{4,8},{8,12},{12,16},{16,20},{20,24},{24,28},{29,1},{... | collective-permute-start | bytes 602120 | tf_op jit(solution)/shard_map/ppermute | solution.py:39
  99.1 6.8 %collective-permute-start.23 = (bf16[112,896]{1,0:T(8,128)(2,1)S(1)}, bf16[112,896]{1,0:T(8,128)(2,1)S(1)}, u32[]{:S(2)}, u32[]{:S(2)}) collective-permute-start(bf16[112,896]{1,0:T(8,128)(2,1)S(1)} %collective-permute-done.21.refs_2_), channel_id=1, source_target_pairs={{4,0},{8,4},{12,8},{16,12},{20,16},{24,20},{28,24},{0,28},{5,1},{9... | collective-permute-start | bytes 602120 | tf_op jit(solution)/shard_map/ppermute | solution.py:39
  100.7 6.3 %collective-permute-start.24 = (bf16[112,896]{1,0:T(8,128)(2,1)S(1)}, bf16[112,896]{1,0:T(8,128)(2,1)S(1)}, u32[]{:S(2)}, u32[]{:S(2)}) collective-permute-start(bf16[112,896]{1,0:T(8,128)(2,1)S(1)} %collective-permute-done.22.refs_5_), channel_id=1, source_target_pairs={{28,0},{0,4},{4,8},{8,12},{12,16},{16,20},{20,24},{24,28},{29,1},{... | collective-permute-start | bytes 602120 | tf_op jit(solution)/shard_map/ppermute | solution.py:39
  107.7 16.2 %collective-permute-start.25 = (bf16[7,112,896]{2,1,0:T(8,128)(2,1)S(1)}, bf16[7,112,896]{2,1,0:T(8,128)(2,1)S(1)}, u32[]{:S(2)}, u32[]{:S(2)}) collective-permute-start(bf16[7,112,896]{2,1,0:T(8,128)(2,1)S(1)} %shard_map.21.group), channel_id=1, source_target_pairs={{1,0},{0,1},{3,2},{2,3},{5,4},{4,5},{7,6},{6,7},{9,8},{8,9},{11,10... | collective-permute-start | bytes 4214792 | tf_op jit(solution)/shard_map/ppermute | solution.py:39
  117.3 5.7 %collective-permute-start.27 = (bf16[56,896]{1,0:T(8,128)(2,1)S(1)}, bf16[56,896]{1,0:T(8,128)(2,1)S(1)}, u32[]{:S(2)}, u32[]{:S(2)}) collective-permute-start(bf16[56,896]{1,0:T(8,128)(2,1)S(1)} %slice.37), channel_id=1, source_target_pairs={{28,0},{0,4},{4,8},{8,12},{12,16},{16,20},{20,24},{24,28},{29,1},{... | collective-permute-start | bytes 301064 | tf_op jit(solution)/shard_map/ppermute | solution.py:39
  117.7 6.2 %collective-permute-start.26 = (bf16[56,896]{1,0:T(8,128)(2,1)S(1)}, bf16[56,896]{1,0:T(8,128)(2,1)S(1)}, u32[]{:S(2)}, u32[]{:S(2)}) collective-permute-start(bf16[56,896]{1,0:T(8,128)(2,1)S(1)} %slice.36), channel_id=1, source_target_pairs={{4,0},{8,4},{12,8},{16,12},{20,16},{24,20},{28,24},{0,28},{5,1},{9... | collective-permute-start | bytes 301064 | tf_op jit(solution)/shard_map/ppermute | solution.py:39
  123.0 4.9 %collective-permute-start.29 = (bf16[56,896]{1,0:T(8,128)(2,1)S(1)}, bf16[56,896]{1,0:T(8,128)(2,1)S(1)}, u32[]{:S(2)}, u32[]{:S(2)}) collective-permute-start(bf16[56,896]{1,0:T(8,128)(2,1)S(1)} %collective-permute-done.27.refs_1_), channel_id=1, source_target_pairs={{1,0},{0,1},{3,2},{2,3},{5,4},{4,5},{7,6},{6,7},{9,8},{8,9},{11,10... | collective-permute-start | bytes 301064 | tf_op jit(solution)/shard_map/ppermute | solution.py:39
  123.9 4.0 %collective-permute-start.28 = (bf16[56,896]{1,0:T(8,128)(2,1)S(1)}, bf16[56,896]{1,0:T(8,128)(2,1)S(1)}, u32[]{:S(2)}, u32[]{:S(2)}) collective-permute-start(bf16[56,896]{1,0:T(8,128)(2,1)S(1)} %collective-permute-done.26.refs_0_), channel_id=1, source_target_pairs={{1,0},{0,1},{3,2},{2,3},{5,4},{4,5},{7,6},{6,7},{9,8},{8,9},{11,10... | collective-permute-start | bytes 301064 | tf_op jit(solution)/shard_map/ppermute | solution.py:39
  129.8 12.9 %collective-permute-start.32 = (bf16[504,512]{1,0:T(8,128)(2,1)S(1)}, bf16[504,512]{1,0:T(8,128)(2,1)S(1)}, u32[]{:S(2)}, u32[]{:S(2)}) collective-permute-start(bf16[504,512]{1,0:T(8,128)(2,1)S(1)} %get-tuple-element.85.refs_0_), channel_id=1, source_target_pairs={{32,0},{0,32},{33,1},{1,33},{34,2},{2,34},{35,3},{3,35},{36,4},{4,... | collective-permute-start | bytes 1548296 | tf_op jit(solution)/shard_map/ppermute | solution.py:39
  131.1 13.7 %collective-permute-start.31 = (bf16[504,512]{1,0:T(8,128)(2,1)S(1)}, bf16[504,512]{1,0:T(8,128)(2,1)S(1)}, u32[]{:S(2)}, u32[]{:S(2)}) collective-permute-start(bf16[504,512]{1,0:T(8,128)(2,1)S(1)} %get-tuple-element.85.refs_0_), channel_id=1, source_target_pairs={{192,0},{0,64},{64,128},{128,192},{193,1},{1,65},{65,129},{129,193... | collective-permute-start | bytes 1548296 | tf_op jit(solution)/shard_map/ppermute | solution.py:39
  131.6 13.2 %collective-permute-start.30 = (bf16[504,512]{1,0:T(8,128)(2,1)S(1)}, bf16[504,512]{1,0:T(8,128)(2,1)S(1)}, u32[]{:S(2)}, u32[]{:S(2)}) collective-permute-start(bf16[504,512]{1,0:T(8,128)(2,1)S(1)} %get-tuple-element.85.refs_0_), channel_id=1, source_target_pairs={{64,0},{128,64},{192,128},{0,192},{65,1},{129,65},{193,129},{1,193... | collective-permute-start | bytes 1548296 | tf_op jit(solution)/shard_map/ppermute | solution.py:39
  144.8 11.7 %collective-permute-start.34 = (bf16[504,512]{1,0:T(8,128)(2,1)S(1)}, bf16[504,512]{1,0:T(8,128)(2,1)S(1)}, u32[]{:S(2)}, u32[]{:S(2)}) collective-permute-start(bf16[504,512]{1,0:T(8,128)(2,1)S(1)} %collective-permute-done.32.refs_3_), channel_id=1, source_target_pairs={{64,0},{128,64},{192,128},{0,192},{65,1},{129,65},{193,129},{1,193... | collective-permute-start | bytes 1548296 | tf_op jit(solution)/shard_map/ppermute | solution.py:39
  147.2 11.1 %collective-permute-start.35 = (bf16[504,512]{1,0:T(8,128)(2,1)S(1)}, bf16[504,512]{1,0:T(8,128)(2,1)S(1)}, u32[]{:S(2)}, u32[]{:S(2)}) collective-permute-start(bf16[504,512]{1,0:T(8,128)(2,1)S(1)} %collective-permute-done.31.refs_2_), channel_id=1, source_target_pairs={{32,0},{0,32},{33,1},{1,33},{34,2},{2,34},{35,3},{3,35},{36,4},{4,... | collective-permute-start | bytes 1548296 | tf_op jit(solution)/shard_map/ppermute | solution.py:39
  147.5 12.0 %collective-permute-start.33 = (bf16[504,512]{1,0:T(8,128)(2,1)S(1)}, bf16[504,512]{1,0:T(8,128)(2,1)S(1)}, u32[]{:S(2)}, u32[]{:S(2)}) collective-permute-start(bf16[504,512]{1,0:T(8,128)(2,1)S(1)} %collective-permute-done.31.refs_2_), channel_id=1, source_target_pairs={{192,0},{0,64},{64,128},{128,192},{193,1},{1,65},{65,129},{129,193... | collective-permute-start | bytes 1548296 | tf_op jit(solution)/shard_map/ppermute | solution.py:39
  159.6 6.8 %collective-permute-start.36 = (bf16[256,512]{1,0:T(8,128)(2,1)S(1)}, bf16[256,512]{1,0:T(8,128)(2,1)S(1)}, u32[]{:S(2)}, u32[]{:S(2)}) collective-permute-start(bf16[256,512]{1,0:T(8,128)(2,1)S(1)} %slice.38), channel_id=1, source_target_pairs={{64,0},{128,64},{192,128},{0,192},{65,1},{129,65},{193,129},{1,193... | collective-permute-start | bytes 786440 | tf_op jit(solution)/shard_map/ppermute | solution.py:39
  160.0 6.4 %collective-permute-start.37 = (bf16[248,512]{1,0:T(8,128)(2,1)S(1)}, bf16[248,512]{1,0:T(8,128)(2,1)S(1)}, u32[]{:S(2)}, u32[]{:S(2)}) collective-permute-start(bf16[248,512]{1,0:T(8,128)(2,1)S(1)} %slice.39), channel_id=1, source_target_pairs={{192,0},{0,64},{64,128},{128,192},{193,1},{1,65},{65,129},{129,193... | collective-permute-start | bytes 761864 | tf_op jit(solution)/shard_map/ppermute | solution.py:39
where the time goes:
time: 171 us; the launch traced here: 169 us
  waiting for transfers between devices  82 us (48%)
  starting transfers between devices  64.5 us (38%)
  Pallas kernels  20.2 us (12%)
    ppermute x38, waiting for transfers between devices, shift(): lax.ppermute(value, axis, [((i + step) % size, i) for i in range(size)])  82 us
    ppermute x38, starting transfers between devices, shift(): lax.ppermute(value, axis, [((i + step) % size, i) for i in range(size)])  64.5 us
    pallas_call x10, Pallas kernels, call(): pl.pallas_call(body, out_shape=outs if home else [pltpu.VMEM(o.shape, o.d...  20.2 us
  transfers between devices with their start and end apart: 38, of which 24 were waited for; matrix products, arithmetic and copies ran while one was open for 0% of the time, Pallas kernels for 8%

commit v1 on v0

--- a/solution.py
+++ b/solution.py
@@ -1,3 +1,4 @@
+import itertools
 import math
 
 import jax
@@ -22,7 +23,7 @@
 PANEL = SIZES["x"] * SIZES["yl"]
 FAR = RING // 2
 LANES = 128
-VMEM_LIMIT = 20 << 20
+VMEM_LIMIT = 14 << 20
 
 F32 = jnp.float32
 BF16 = jnp.bfloat16
@@ -37,6 +38,19 @@
 def shift(value, axis, step):
     size = SIZES[axis]
     return lax.ppermute(value, axis, [((i + step) % size, i) for i in range(size)])
+
+
+def fetch(value, axes, source):
+    sizes = [SIZES[a] for a in axes]
+
+    def flat(position):
+        index = 0
+        for p, n in zip(position, sizes, strict=True):
+            index = index * n + p % n
+        return index
+
+    places = list(itertools.product(*(range(n) for n in sizes)))
+    return lax.ppermute(value, axes, [(flat(source(*p)), flat(p)) for p in places])
 
 
 def call(body, place, operands, outs, flops=0, scratch=(), fixed=True, home=False, alias=None):
@@ -64,7 +78,10 @@
 
 def more_blocks(first):
     _, _, r30, r01 = first
-    return shift(r30, "x", -1), shift(r01, "x", 1), shift(r30, "yl", 1)
+    r20 = shift(r30, "x", -1)
+    r11 = shift(r01, "x", 1)
+    r31 = shift(r30, "yl", 1)
+    return r20, r11, r31
 
 
 def last_block(more):
@@ -117,28 +134,46 @@
     return pl.ds(pl.multiple_of(lax.rem(z + far, RING) * size, 8), size)
 
 
+DIMS = (((1,), (1,)), ((), ()))
+
+
 def gram_body(place, own, *refs):
-    *blocks, keep, send, panel, rows = refs
+    *blocks, keep, send, panel, partner, beside, rows, mixed = refs
     fill(panel, blocks)
     z, c = place[0], place[1]
-    dims = (((1,), (1,)), ((), ()))
+    height = own.shape[0]
+    mixed[:height] = panel[0, height:]
+    mixed[height:] = panel[1, :height]
 
     @pl.loop(0, 2)
     def _(i):
-        rows[i] = lax.dot_general(own[...], panel[i], dims, preferred_element_type=F32)
-
+        rows[i] = lax.dot_general(own[...], panel[i], DIMS, preferred_element_type=F32)
+
+    partner[...] = lax.dot_general(panel[1, height:], mixed[...], DIMS, preferred_element_type=F32)
+    beside[...] = lax.dot_general(panel[0, height:], panel[1, :height], DIMS, preferred_element_type=F32)
+    split_units(z, c, rows, keep, send)
+
+
+def split_units(z, c, rows, keep, send):
     size = keep.shape[1]
     for side, out in ((c, keep), (1 - c, send)):
         for far in range(RING):
             out[far] = rows[side, chunk(z, far, size), :].astype(BF16)
 
 
-def gram_partial(place, own, blocks):
-    rows, cols = own.shape
-    part = array((RING, rows // RING, 2 * rows))
-    panel = array((2, 2 * rows, cols))
-    scratch = [pltpu.VMEM((2, rows, 2 * rows), F32)]
-    return call(gram_body, place, (own, *blocks), [part, part, panel], 8 * rows * rows * cols, scratch)
+def late_body(place, own, partner, beside, block, keep, send, rows, panel):
+    z, c = place[0], place[1]
+    height = own.shape[0]
+    fill(panel, [block])
+    rows[0] = partner[...]
+    rows[1, :, :height] = lax.dot_general(own[...], panel[0, :height], DIMS, preferred_element_type=F32)
+    rows[1, :, height:] = beside[...]
+    split_units(z, c, rows, keep, send)
+
+
+def panel_body(place, *refs):
+    *blocks, panel = refs
+    fill(panel, blocks)
 
 
 def pair_body(place, low, low_other, high, high_other, *outs):
@@ -162,7 +197,8 @@
 def ring_sum(part, up, down):
     size = up.shape[0]
     for step in range(FAR - 1, -1, -1):
-        up, down = shift(up, "z", -1), shift(down, "z", 1)
+        up = shift(up, "z", -1)
+        down = shift(down, "z", 1)
         if step == 0:
             total = part[0].astype(F32) + up.astype(F32) + down.astype(F32)
         elif step == FAR - 1:
@@ -201,13 +237,13 @@
 
 
 def update_body(place, own, low, high, near, far, before, *refs):
-    ends, (near_out, far_out, w_high, w_low, total) = refs[:4], refs[4:]
+    mine, other, near_out, far_out, w_high, w_low, total = refs
     z, c = place[0], place[1]
     size = near.shape[1] // RING
     where = chunk(z, FAR, size)
-    for side, lower, upper in ((c, ends[0], ends[1]), (1 - c, ends[2], ends[3])):
-        near_out[side, where, :] = lower[...]
-        far_out[side, where, :] = upper[...]
+    for side, ref in ((c, mine), (1 - c, other)):
+        near_out[side, where, :] = ref[:size]
+        far_out[side, where, :] = ref[size:]
     acc = jnp.zeros((size, own.shape[1]), F32)
     for gram, panel in ((near_out, low), (far_out, high)):
         for i in range(2):
@@ -257,54 +293,80 @@
 
     packed, own = call(pack_body, place, (matrix,), [flat, block], fixed=False)
     first = lax.optimization_barrier(first_blocks(packed))
-    keep, send, low = gram_partial(place, own, first)
+    r21 = fetch(packed, ("x", "yl"), lambda x, y: (x + 2, y + 1))
+    part = array((RING, size, 2 * rows))
+    wide = array((2, rows, 2 * rows))
+    panel = array((2, 2 * rows, cols))
+    work = 4 * rows * rows * cols
+    keep, send, low, partner, beside = call(
+        gram_body,
+        place,
+        (own, *first),
+        [part, part, panel, array((rows, 2 * rows), F32), array((rows, rows), F32)],
+        7 * work // 2,
+        [pltpu.VMEM(wide.shape, F32), pltpu.VMEM((2 * rows, cols), BF16)],
+    )
     halves = [keep, shift(send, "c", 1)]
-    more = lax.optimization_barrier(more_blocks(first))
-    last = last_block(more)
-    keep, send, high = gram_partial(place, own, (*more, *last))
+    keep, send = call(
+        late_body,
+        place,
+        (own, partner, beside, r21),
+        [part, part],
+        work // 2,
+        [pltpu.VMEM(wide.shape, F32), pltpu.VMEM((1, 2 * rows, cols), BF16)],
+    )
     halves += [keep, shift(send, "c", 1)]
-
+    r20, r11, r31 = more_blocks(first)
+    high = call(panel_body, place, (r11, r31, r21, r20), panel)
     one, two = array((size, 2 * rows)), array((2 * size, 2 * rows))
     parts = call(pair_body, place, halves, [two] * FAR + [one] * 2 + [two] * (FAR - 1))
     part = {d: parts[d if d < FAR else d + 1] for d in range(RING) if d != FAR}
     mine = ring_sum(part, parts[FAR], parts[FAR + 1])
+    ahead = mine[size:]
+    same = fetch(ahead, ("x", "yl", "c"), lambda x, y, c: (x, y + 1, c) if c == 0 else (x - 1, y, c))
+    cross = fetch(
+        ahead, ("x", "yl", "yh", "c"), lambda x, y, h, c: (x, y + 1, h + 1, c) if c == 0 else (x - 1, y, h + 1, c)
+    )
     mine = add(mine, shift(mine, "yh", 1))
+    ahead = add(same, cross)
+    left = lax.broadcasted_iota(jnp.int32, ahead.shape, 1) < rows
+    ahead = jnp.where((place[1] == 1) & left, mine[size:], ahead)
+    mine = jnp.concatenate([mine[:size], ahead], 0)
 
     ring = {0: mine}
     up, down = mine, mine
     for step in range(1, FAR):
-        up, down = lax.optimization_barrier((shift(up, "z", 1), shift(down, "z", -1)))
+        up = shift(up, "z", 1)
+        down = shift(down, "z", -1)
         ring[step], ring[RING - step] = up, down
     ends = [shift(up[:size], "z", 1)]
     ends.append(shift(down[size:], "z", -1))
     pieces = [ring[d] for d in range(RING) if d != FAR]
     group = call(group_body, place, pieces, array((RING - 1, 2 * size, 2 * rows)))
-    ends += [shift(p, "c", 1) for p in ends]
+    ends = jnp.concatenate(ends, 0)
 
     sums = array((rows, cols), F32)
-    wide = array((2, rows, 2 * rows))
-    work = 4 * rows * rows * cols
     other = shift(group, "c", 1)
     gram_near, gram_far, total = call(rows_body, place, (low, high, group, other), [wide, wide, sums], 4 * work)
     gram_near, gram_far, w_high, w_low = call(
         update_body,
         place,
-        (own, low, high, gram_near, gram_far, total, *ends),
+        (own, low, high, gram_near, gram_far, total, ends, shift(ends, "c", 1)),
         [wide, wide, flat, block],
         work // 2,
         [pltpu.VMEM((rows, cols), F32)],
         alias={4: 0, 5: 1},
     )
 
-    def panel(count):
+    def room(count):
         return [pltpu.VMEM((count, 2 * rows, cols), BF16)]
 
     near = lax.optimization_barrier(first_blocks(w_high))
-    total = call(near_body, place, (own, w_low, gram_near, *near), sums, 5 * work // 2, panel(2))
+    total = call(near_body, place, (own, w_low, gram_near, *near), sums, 5 * work // 2, room(2))
     side = lax.optimization_barrier(more_blocks(near))
-    total = call(side_body, place, (total, gram_far, *side[:2]), sums, work, panel(1))
+    total = call(side_body, place, (total, gram_far, *side[1:]), sums, work, room(1))
     ends = last_block(side)
-    return call(far_body, place, (total, gram_far, side[2], *ends), block, work, panel(1), home=True)
+    return call(far_body, place, (total, gram_far, *ends, side[0]), block, work, room(1), home=True)
 
 
 def solution(mesh):

time: 171 us -> 173 us (1.012)
  waiting for transfers between devices: 82 us -> 73.3 us
  starting transfers between devices: 64.5 us -> 71.2 us
  other arithmetic: 0.51 us -> 2.29 us
    ppermute x38 -> x35, waiting for transfers between devices: 82 us -> 70 us  [shift(): lax.ppermute(value, axis, [((i + step) % size, i) for i in range(size)])]
    ppermute x38 -> x35, starting transfers between devices: 64.5 us -> 69.7 us  [shift(): lax.ppermute(value, axis, [((i + step) % size, i) for i in range(size)])]
    ppermute x0 -> x3, waiting for transfers between devices: none -> 3.38 us  [fetch(): lax.ppermute(value, axes, [(flat(source(*p)), flat(p)) for p in places])]
    pallas_call x10 -> x11, Pallas kernels: 20.2 us -> 21.1 us  [call(): pl.pallas_call(body, out_shape=outs if home else [pltpu.VMEM(o.shape, o.d...]
  transfers between devices with their start and end apart: 38 -> 38, of which waited for: 24 -> 24; matrix products, arithmetic and copies ran while one was open for 0% -> 1% of each run, Pallas kernels for 8% -> 9%
where the time goes in v1:
time: 173 us; the launch traced here: 170 us
  waiting for transfers between devices  73.3 us (42%)
  starting transfers between devices  71.2 us (41%)
  Pallas kernels  21.1 us (12%)
  other arithmetic  2.29 us (1%)
  local copies, waits for them, and re-layouts  2.1 us (1%)
    ppermute x35, waiting for transfers between devices, shift(): lax.ppermute(value, axis, [((i + step) % size, i) for i in range(size)])  70 us
    ppermute x35, starting transfers between devices, shift(): lax.ppermute(value, axis, [((i + step) % size, i) for i in range(size)])  69.7 us
    pallas_call x11, Pallas kernels, call(): pl.pallas_call(body, out_shape=outs if home else [pltpu.VMEM(o.shape, o.d...  21.1 us
  transfers between devices with their start and end apart: 38, of which 24 were waited for; matrix products, arithmetic and copies ran while one was open for 1% of the time, Pallas kernels for 9%

profile of v1, /device:TPU:1, one launch (start us, length us, event | category | flops | bytes accessed | tf_op | source)
XLA Modules:
  0.0 170.3 jit_solution(4265686012811396625)
XLA Ops:
  0.1 1.1 copy-done
  1.1 0.6 shard_map.17
  1.8 2.2 %collective-permute-start.2 = (bf16[504,512]{1,0:T(8,128)(2,1)S(1)}, bf16[504,512]{1,0:T(8,128)(2,1)S(1)}, u32[]{:S(2)}, u32[]{:S(2)}) collective-permute-start(bf16[504,512]{1,0:T(8,128)(2,1)S(1)} %get-tuple-element.43.refs_0_), channel_id=1, source_target_pairs={{32,0},{0,32},{33,1},{1,33},{34,2},{2,34},{35,3},{3,35},{36,4},{4,... | collective-permute-start | bytes 1548296 | tf_op jit(solution)/shard_map/ppermute | solution.py:40
  4.0 1.2 collective-permute-start.1
  5.2 1.5 collective-permute-start
  6.7 1.4 collective-permute-start.5
  8.1 6.2 %collective-permute-done.2.refs_3_ = bf16[504,512]{1,0:T(8,128)(2,1)S(1)} collective-permute-done((bf16[504,512]{1,0:T(8,128)(2,1)S(1)}, bf16[504,512]{1,0:T(8,128)(2,1)S(1)}, u32[]{:S(2)}, u32[]{:S(2)}) %collective-permute-start.2) | collective-permute-done | bytes 516128 | tf_op jit(solution)/shard_map/ppermute | solution.py:40
  14.3 3.0 %collective-permute-done.1.refs_2_ = bf16[504,512]{1,0:T(8,128)(2,1)S(1)} collective-permute-done((bf16[504,512]{1,0:T(8,128)(2,1)S(1)}, bf16[504,512]{1,0:T(8,128)(2,1)S(1)}, u32[]{:S(2)}, u32[]{:S(2)}) %collective-permute-start.1) | collective-permute-done | bytes 516128 | tf_op jit(solution)/shard_map/ppermute | solution.py:40
  17.3 4.0 %shard_map.18 = (bf16[8,56,896]{2,1,0:T(8,128)(2,1)S(1)}, bf16[8,56,896]{2,1,0:T(8,128)(2,1)S(1)}, bf16[2,896,576]{2,1,0:T(8,128)(2,1)S(1)}, f32[448,896]{1,0:T(8,128)S(1)}, f32[448,448]{1,0:T(8,128)S(1)}) custom-call(s32[2]{0:T(128)S(1)} %pad_add_fusion.place, bf16[448,576]{1,0:T(8,128)(2,1)S(1)} %get-tuple-element.41.own, ...), custom_call_target="tpu_custom_call" | custom-call | flops 1618477056 | bytes 7454720 | tf_op jit(solution)/shard_map/pallas_call | solution.py:62
  21.3 12.5 %collective-permute-start.7 = (bf16[8,56,896]{2,1,0:T(8,128)(2,1)S(1)}, bf16[8,56,896]{2,1,0:T(8,128)(2,1)S(1)}, u32[]{:S(2)}, u32[]{:S(2)}) collective-permute-start(bf16[8,56,896]{2,1,0:T(8,128)(2,1)S(1)} %get-tuple-element.49), channel_id=1, source_target_pairs={{1,0},{0,1},{3,2},{2,3},{5,4},{4,5},{7,6},{6,7},{9,8},{8,9},{11,10... | collective-permute-start | bytes 2408456 | tf_op jit(solution)/shard_map/ppermute | solution.py:40
  33.8 1.4 shard_map.20
  35.2 0.1 collective-permute-start.8
  35.3 0.4 collective-permute-done.7.low_other
  35.8 1.8 %collective-permute-done.8.high_other = bf16[8,56,896]{2,1,0:T(8,128)(2,1)S(1)} collective-permute-done((bf16[8,56,896]{2,1,0:T(8,128)(2,1)S(1)}, bf16[8,56,896]{2,1,0:T(8,128)(2,1)S(1)}, u32[]{:S(2)}, u32[]{:S(2)}) %collective-permute-start.8) | collective-permute-done | bytes 802848 | tf_op jit(solution)/shard_map/ppermute | solution.py:40
  37.6 0.9 shard_map.21
  38.5 5.6 %collective-permute-start.13 = (bf16[56,896]{1,0:T(8,128)(2,1)S(1)}, bf16[56,896]{1,0:T(8,128)(2,1)S(1)}, u32[]{:S(2)}, u32[]{:S(2)}) collective-permute-start(bf16[56,896]{1,0:T(8,128)(2,1)S(1)} %get-tuple-element.62), channel_id=1, source_target_pairs={{4,0},{8,4},{12,8},{16,12},{20,16},{24,20},{28,24},{0,28},{5,1},{9... | collective-permute-start | bytes 301064 | tf_op jit(solution)/shard_map/ppermute | solution.py:40
  44.2 0.1 collective-permute-start.9
  44.3 1.9 %collective-permute-done.13 = bf16[56,896]{1,0:T(8,128)(2,1)S(1)} collective-permute-done((bf16[56,896]{1,0:T(8,128)(2,1)S(1)}, bf16[56,896]{1,0:T(8,128)(2,1)S(1)}, u32[]{:S(2)}, u32[]{:S(2)}) %collective-permute-start.13) | collective-permute-done | bytes 100384 | tf_op jit(solution)/shard_map/ppermute | solution.py:40
  46.3 3.5 %collective-permute-start.14 = (bf16[112,896]{1,0:T(8,128)(2,1)S(1)}, bf16[112,896]{1,0:T(8,128)(2,1)S(1)}, u32[]{:S(2)}, u32[]{:S(2)}) collective-permute-start(bf16[112,896]{1,0:T(8,128)(2,1)S(1)} %pad_maximum_fusion.1), channel_id=1, source_target_pairs={{4,0},{8,4},{12,8},{16,12},{20,16},{24,20},{28,24},{0,28},{5,1},{9... | collective-permute-start | bytes 602120 | tf_op jit(solution)/shard_map/ppermute | solution.py:40
  49.9 3.2 %collective-permute-done.14 = bf16[112,896]{1,0:T(8,128)(2,1)S(1)} collective-permute-done((bf16[112,896]{1,0:T(8,128)(2,1)S(1)}, bf16[112,896]{1,0:T(8,128)(2,1)S(1)}, u32[]{:S(2)}, u32[]{:S(2)}) %collective-permute-start.14) | collective-permute-done | bytes 200736 | tf_op jit(solution)/shard_map/ppermute | solution.py:40
  53.2 3.5 %collective-permute-start.15 = (bf16[112,896]{1,0:T(8,128)(2,1)S(1)}, bf16[112,896]{1,0:T(8,128)(2,1)S(1)}, u32[]{:S(2)}, u32[]{:S(2)}) collective-permute-start(bf16[112,896]{1,0:T(8,128)(2,1)S(1)} %add_convert_fusion.3), channel_id=1, source_target_pairs={{4,0},{8,4},{12,8},{16,12},{20,16},{24,20},{28,24},{0,28},{5,1},{9... | collective-permute-start | bytes 602120 | tf_op jit(solution)/shard_map/ppermute | solution.py:40
  56.8 2.5 %collective-permute-done.15 = bf16[112,896]{1,0:T(8,128)(2,1)S(1)} collective-permute-done((bf16[112,896]{1,0:T(8,128)(2,1)S(1)}, bf16[112,896]{1,0:T(8,128)(2,1)S(1)}, u32[]{:S(2)}, u32[]{:S(2)}) %collective-permute-start.15) | collective-permute-done | bytes 200736 | tf_op jit(solution)/shard_map/ppermute | solution.py:40
  59.4 3.4 %collective-permute-start.16 = (bf16[112,896]{1,0:T(8,128)(2,1)S(1)}, bf16[112,896]{1,0:T(8,128)(2,1)S(1)}, u32[]{:S(2)}, u32[]{:S(2)}) collective-permute-start(bf16[112,896]{1,0:T(8,128)(2,1)S(1)} %add_convert_fusion.2), channel_id=1, source_target_pairs={{4,0},{8,4},{12,8},{16,12},{20,16},{24,20},{28,24},{0,28},{5,1},{9... | collective-permute-start | bytes 602120 | tf_op jit(solution)/shard_map/ppermute | solution.py:40
  62.9 2.5 %collective-permute-done.16 = bf16[112,896]{1,0:T(8,128)(2,1)S(1)} collective-permute-done((bf16[112,896]{1,0:T(8,128)(2,1)S(1)}, bf16[112,896]{1,0:T(8,128)(2,1)S(1)}, u32[]{:S(2)}, u32[]{:S(2)}) %collective-permute-start.16) | collective-permute-done | bytes 200736 | tf_op jit(solution)/shard_map/ppermute | solution.py:40
  65.4 3.3 %collective-permute-done.12 = bf16[112,896]{1,0:T(8,128)(2,1)S(1)} collective-permute-done((bf16[112,896]{1,0:T(8,128)(2,1)S(1)}, bf16[112,896]{1,0:T(8,128)(2,1)S(1)}, u32[]{:S(2)}, u32[]{:S(2)}) %collective-permute-start.12) | collective-permute-done | bytes 200736 | tf_op jit(solution)/shard_map/ppermute | solution.py:40
  68.7 0.8 add_convert_fusion.1
  69.4 2.6 %collective-permute-start.17 = (bf16[112,896]{1,0:T(8,128)(2,1)}, bf16[112,896]{1,0:T(8,128)(2,1)}, u32[]{:S(2)}, u32[]{:S(2)}) collective-permute-start(bf16[112,896]{1,0:T(8,128)(2,1)} %add_convert_fusion.1), channel_id=1, source_target_pairs={{2,0},{0,2},{3,1},{1,3},{6,4},{4,6},{7,5},{5,7},{10,8},{8,10},{11,... | collective-permute-start | bytes 602120 | tf_op jit(solution)/shard_map/ppermute | solution.py:40
  72.1 0.9 slice.46
  73.2 2.7 %collective-permute-done.17 = bf16[112,896]{1,0:T(8,128)(2,1)} collective-permute-done((bf16[112,896]{1,0:T(8,128)(2,1)}, bf16[112,896]{1,0:T(8,128)(2,1)}, u32[]{:S(2)}, u32[]{:S(2)}) %collective-permute-start.17) | collective-permute-done | bytes 200736 | tf_op jit(solution)/shard_map/ppermute | solution.py:40
  75.8 1.1 add_convert_fusion
  76.9 3.4 %collective-permute-done.19 = bf16[56,896]{1,0:T(8,128)(2,1)S(1)} collective-permute-done((bf16[56,896]{1,0:T(8,128)(2,1)S(1)}, bf16[56,896]{1,0:T(8,128)(2,1)S(1)}, u32[]{:S(2)}, u32[]{:S(2)}) %collective-permute-start.19) | collective-permute-done | bytes 100384 | tf_op jit(solution)/shard_map/ppermute | solution.py:53
  80.5 2.7 %collective-permute-start.20 = (bf16[112,896]{1,0:T(8,128)(2,1)S(1)}, bf16[112,896]{1,0:T(8,128)(2,1)S(1)}, u32[]{:S(2)}, u32[]{:S(2)}) collective-permute-start(bf16[112,896]{1,0:T(8,128)(2,1)S(1)} %pad_maximum_fusion.2.refs_0_), channel_id=1, source_target_pairs={{4,0},{8,4},{12,8},{16,12},{20,16},{24,20},{28,24},{0,28},{5,1},{9... | collective-permute-start | bytes 602120 | tf_op jit(solution)/shard_map/ppermute | solution.py:40
  83.1 3.1 %collective-permute-done.23.refs_6_ = bf16[112,896]{1,0:T(8,128)(2,1)S(1)} collective-permute-done((bf16[112,896]{1,0:T(8,128)(2,1)S(1)}, bf16[112,896]{1,0:T(8,128)(2,1)S(1)}, u32[]{:S(2)}, u32[]{:S(2)}) %collective-permute-start.23) | collective-permute-done | bytes 200736 | tf_op jit(solution)/shard_map/ppermute | solution.py:40
  86.2 2.7 %collective-permute-start.21 = (bf16[112,896]{1,0:T(8,128)(2,1)S(1)}, bf16[112,896]{1,0:T(8,128)(2,1)S(1)}, u32[]{:S(2)}, u32[]{:S(2)}) collective-permute-start(bf16[112,896]{1,0:T(8,128)(2,1)S(1)} %collective-permute-done.20.refs_1_), channel_id=1, source_target_pairs={{4,0},{8,4},{12,8},{16,12},{20,16},{24,20},{28,24},{0,28},{5,1},{9... | collective-permute-start | bytes 602120 | tf_op jit(solution)/shard_map/ppermute | solution.py:40
  88.9 3.3 %collective-permute-done.24.refs_5_ = bf16[112,896]{1,0:T(8,128)(2,1)S(1)} collective-permute-done((bf16[112,896]{1,0:T(8,128)(2,1)S(1)}, bf16[112,896]{1,0:T(8,128)(2,1)S(1)}, u32[]{:S(2)}, u32[]{:S(2)}) %collective-permute-start.24) | collective-permute-done | bytes 200736 | tf_op jit(solution)/shard_map/ppermute | solution.py:40
  92.2 3.0 %collective-permute-start.22 = (bf16[112,896]{1,0:T(8,128)(2,1)S(1)}, bf16[112,896]{1,0:T(8,128)(2,1)S(1)}, u32[]{:S(2)}, u32[]{:S(2)}) collective-permute-start(bf16[112,896]{1,0:T(8,128)(2,1)S(1)} %collective-permute-done.21.refs_2_), channel_id=1, source_target_pairs={{4,0},{8,4},{12,8},{16,12},{20,16},{24,20},{28,24},{0,28},{5,1},{9... | collective-permute-start | bytes 602120 | tf_op jit(solution)/shard_map/ppermute | solution.py:40
  95.1 4.1 %collective-permute-done.25.refs_4_ = bf16[112,896]{1,0:T(8,128)(2,1)S(1)} collective-permute-done((bf16[112,896]{1,0:T(8,128)(2,1)S(1)}, bf16[112,896]{1,0:T(8,128)(2,1)S(1)}, u32[]{:S(2)}, u32[]{:S(2)}) %collective-permute-start.25) | collective-permute-done | bytes 200736 | tf_op jit(solution)/shard_map/ppermute | solution.py:40
  99.3 0.1 collective-permute-done.22.refs_3_
  99.4 0.6 shard_map.22.group
  100.1 6.9 %collective-permute-start.26 = (bf16[7,112,896]{2,1,0:T(8,128)(2,1)S(1)}, bf16[7,112,896]{2,1,0:T(8,128)(2,1)S(1)}, u32[]{:S(2)}, u32[]{:S(2)}) collective-permute-start(bf16[7,112,896]{2,1,0:T(8,128)(2,1)S(1)} %shard_map.22.group), channel_id=1, source_target_pairs={{1,0},{0,1},{3,2},{2,3},{5,4},{4,5},{7,6},{6,7},{9,8},{8,9},{11,10... | collective-permute-start | bytes 4214792 | tf_op jit(solution)/shard_map/ppermute | solution.py:40
  106.9 4.9 %collective-permute-start.3 = (bf16[504,512]{1,0:T(8,128)(2,1)S(1)}, bf16[504,512]{1,0:T(8,128)(2,1)S(1)}, u32[]{:S(2)}, u32[]{:S(2)}) collective-permute-start(bf16[504,512]{1,0:T(8,128)(2,1)S(1)} %copy-done.4), channel_id=1, source_target_pairs={{64,0},{128,64},{192,128},{0,192},{65,1},{129,65},{193,129},{1,193... | collective-permute-start | bytes 1548296 | tf_op jit(solution)/shard_map/ppermute | solution.py:40
  111.9 3.0 %collective-permute-start.27 = (bf16[56,896]{1,0:T(8,128)(2,1)S(1)}, bf16[56,896]{1,0:T(8,128)(2,1)S(1)}, u32[]{:S(2)}, u32[]{:S(2)}) collective-permute-start(bf16[56,896]{1,0:T(8,128)(2,1)S(1)} %slice.47), channel_id=1, source_target_pairs={{4,0},{8,4},{12,8},{16,12},{20,16},{24,20},{28,24},{0,28},{5,1},{9... | collective-permute-start | bytes 301064 | tf_op jit(solution)/shard_map/ppermute | solution.py:40
  114.9 1.6 collective-permute-done.27
  116.6 5.7 %collective-permute-done.28 = bf16[56,896]{1,0:T(8,128)(2,1)S(1)} collective-permute-done((bf16[56,896]{1,0:T(8,128)(2,1)S(1)}, bf16[56,896]{1,0:T(8,128)(2,1)S(1)}, u32[]{:S(2)}, u32[]{:S(2)}) %collective-permute-start.28) | collective-permute-done | bytes 100384 | tf_op jit(solution)/shard_map/ppermute | solution.py:40
  122.3 2.1 %collective-permute-start.29 = (bf16[112,896]{1,0:T(8,128)(2,1)S(1)}, bf16[112,896]{1,0:T(8,128)(2,1)S(1)}, u32[]{:S(2)}, u32[]{:S(2)}) collective-permute-start(bf16[112,896]{1,0:T(8,128)(2,1)S(1)} %constant_dynamic-update-slice_fusion.refs_0_), channel_id=1, source_target_pairs={{1,0},{0,1},{3,2},{2,3},{5,4},{4,5},{7,6},{6,7},{9,8},{8,9},{11,10... | collective-permute-start | bytes 602120 | tf_op jit(solution)/shard_map/ppermute | solution.py:40
  124.4 1.6 collective-permute-done.6.refs_3_
  126.0 0.8 shard_map.19.high
  126.8 4.0 %shard_map.23 = (bf16[2,448,896]{2,1,0:T(8,128)(2,1)S(1)}, bf16[2,448,896]{2,1,0:T(8,128)(2,1)S(1)}, f32[448,576]{1,0:T(8,128)S(1)}) custom-call(s32[2]{0:T(128)S(1)} %pad_add_fusion.place, bf16[2,896,576]{2,1,0:T(8,128)(2,1)S(1)} %get-tuple-element.47.low, bf16[2,896,576]{2,1,0:T(8,128)(2,1)S(1)} %shard_map.19.high, ...), custom_call_target="tpu_custom_call" | custom-call | flops 1849688064 | bytes 10665984 | tf_op jit(solution)/shard_map/pallas_call | solution.py:62
  130.9 1.9 %shard_map.24 = (bf16[2,448,896]{2,1,0:T(8,128)(2,1)S(1)}, bf16[2,448,896]{2,1,0:T(8,128)(2,1)S(1)}, bf16[504,512]{1,0:T(8,128)(2,1)S(1)}, bf16[448,576]{1,0:T(8,128)(2,1)S(1)}) custom-call(s32[2]{0:T(128)S(1)} %pad_add_fusion.place, bf16[448,576]{1,0:T(8,128)(2,1)S(1)} %get-tuple-element.41.own, ...), custom_call_target="tpu_custom_call", output_to_operand_aliasing={{0}: (4, {}), {1}: (5, {})} | custom-call | flops 231211008 | bytes 13017088 | tf_op jit(solution)/shard_map/pallas_call | solution.py:62
  132.8 0.1 collective-permute-start.32
  133.0 2.7 %collective-permute-start.30 = (bf16[504,512]{1,0:T(8,128)(2,1)S(1)}, bf16[504,512]{1,0:T(8,128)(2,1)S(1)}, u32[]{:S(2)}, u32[]{:S(2)}) collective-permute-start(bf16[504,512]{1,0:T(8,128)(2,1)S(1)} %get-tuple-element.69.refs_0_), channel_id=1, source_target_pairs={{64,0},{128,64},{192,128},{0,192},{65,1},{129,65},{193,129},{1,193... | collective-permute-start | bytes 1548296 | tf_op jit(solution)/shard_map/ppermute | solution.py:40
  135.8 9.2 %collective-permute-done.32.refs_3_ = bf16[504,512]{1,0:T(8,128)(2,1)S(1)} collective-permute-done((bf16[504,512]{1,0:T(8,128)(2,1)S(1)}, bf16[504,512]{1,0:T(8,128)(2,1)S(1)}, u32[]{:S(2)}, u32[]{:S(2)}) %collective-permute-start.32) | collective-permute-done | bytes 516128 | tf_op jit(solution)/shard_map/ppermute | solution.py:40
  145.0 1.4 collective-permute-done.31.refs_2_
  146.3 2.4 %collective-permute-start.34 = (bf16[504,512]{1,0:T(8,128)(2,1)S(1)}, bf16[504,512]{1,0:T(8,128)(2,1)S(1)}, u32[]{:S(2)}, u32[]{:S(2)}) collective-permute-start(bf16[504,512]{1,0:T(8,128)(2,1)S(1)} %collective-permute-done.32.refs_3_), channel_id=1, source_target_pairs={{64,0},{128,64},{192,128},{0,192},{65,1},{129,65},{193,129},{1,193... | collective-permute-start | bytes 1548296 | tf_op jit(solution)/shard_map/ppermute | solution.py:40
  148.7 1.0 collective-permute-start.35
  149.8 8.5 %collective-permute-done.34.refs_0_ = bf16[504,512]{1,0:T(8,128)(2,1)S(1)} collective-permute-done((bf16[504,512]{1,0:T(8,128)(2,1)S(1)}, bf16[504,512]{1,0:T(8,128)(2,1)S(1)}, u32[]{:S(2)}, u32[]{:S(2)}) %collective-permute-start.34) | collective-permute-done | bytes 516128 | tf_op jit(solution)/shard_map/ppermute | solution.py:40
  158.2 1.2 collective-permute-done.35.refs_1_
  159.4 1.6 collective-permute-done.33.refs_2_
  161.1 0.5 collective-permute-start.36
  161.6 1.1 collective-permute-start.37
  162.7 3.0 %shard_map.25.before = f32[448,576]{1,0:T(8,128)S(1)} custom-call(s32[2]{0:T(128)S(1)} %pad_add_fusion.place, bf16[448,576]{1,0:T(8,128)(2,1)S(1)} %get-tuple-element.41.own, bf16[448,576]{1,0:T(8,128)(2,1)S(1)} %get-tuple-element.66.w_low, bf16[2,448,896]{2,1,0:T(8,128)(2,1)S(1)} %get-tuple-element.67.gram, bf16[504,512]{1,0:T(8,128)(2,1)S(1)} %get-tuple-element.69.refs_0_, ...), custom_call_target="tpu_custom_call" | custom-call | flops 1156055040 | bytes 5218304 | tf_op jit(solution)/shard_map/pallas_call | solution.py:62
  165.8 1.4 shard_map.26.before
  167.2 0.9 collective-permute-done.37.refs_1_
  168.1 2.3 %shard_map.27 = bf16[448,576]{1,0:T(8,128)(2,1)} custom-call(s32[2]{0:T(128)S(1)} %pad_add_fusion.place, f32[448,576]{1,0:T(8,128)S(1)} %shard_map.26.before, bf16[2,448,896]{2,1,0:T(8,128)(2,1)S(1)} %get-tuple-element.73.gram, bf16[256,512]{1,0:T(8,128)(2,1)S(1)} %collective-permute-done.36.refs_0_, bf16[248,512]{1,0:T(8,128)(2,1)S(1)} %collective-permute-done.37.refs_1_, ...), custom_call_target="tpu_custom_call" | custom-call | flops 462422016 | bytes 3670016 | tf_op jit(solution)/shard_map/pallas_call | solution.py:62
  (56 shorter events, 1.2 us)
Async XLA Ops:
  0.1 1.1 copy-start
  1.8 12.5 %collective-permute-start.2 = (bf16[504,512]{1,0:T(8,128)(2,1)S(1)}, bf16[504,512]{1,0:T(8,128)(2,1)S(1)}, u32[]{:S(2)}, u32[]{:S(2)}) collective-permute-start(bf16[504,512]{1,0:T(8,128)(2,1)S(1)} %get-tuple-element.43.refs_0_), channel_id=1, source_target_pairs={{32,0},{0,32},{33,1},{1,33},{34,2},{2,34},{35,3},{3,35},{36,4},{4,... | collective-permute-start | bytes 1548296 | tf_op jit(solution)/shard_map/ppermute | solution.py:40
  4.0 13.3 %collective-permute-start.1 = (bf16[504,512]{1,0:T(8,128)(2,1)S(1)}, bf16[504,512]{1,0:T(8,128)(2,1)S(1)}, u32[]{:S(2)}, u32[]{:S(2)}) collective-permute-start(bf16[504,512]{1,0:T(8,128)(2,1)S(1)} %get-tuple-element.43.refs_0_), channel_id=1, source_target_pairs={{192,0},{0,64},{64,128},{128,192},{193,1},{1,65},{65,129},{129,193... | collective-permute-start | bytes 1548296 | tf_op jit(solution)/shard_map/ppermute | solution.py:40
  5.2 12.1 %collective-permute-start = (bf16[504,512]{1,0:T(8,128)(2,1)S(1)}, bf16[504,512]{1,0:T(8,128)(2,1)S(1)}, u32[]{:S(2)}, u32[]{:S(2)}) collective-permute-start(bf16[504,512]{1,0:T(8,128)(2,1)S(1)} %get-tuple-element.43.refs_0_), channel_id=1, source_target_pairs={{64,0},{128,64},{192,128},{0,192},{65,1},{129,65},{193,129},{1,193... | collective-permute-start | bytes 1548296 | tf_op jit(solution)/shard_map/ppermute | solution.py:40
  6.7 27.2 %collective-permute-start.5 = (bf16[504,512]{1,0:T(8,128)(2,1)S(1)}, bf16[504,512]{1,0:T(8,128)(2,1)S(1)}, u32[]{:S(2)}, u32[]{:S(2)}) collective-permute-start(bf16[504,512]{1,0:T(8,128)(2,1)S(1)} %get-tuple-element.43.refs_0_), channel_id=1, source_target_pairs={{160,0},{128,32},{224,64},{192,96},{32,128},{0,160},{96,192},{64,2... | collective-permute-start | bytes 1548296 | tf_op jit(solution)/shard_map/ppermute | solution.py:53
  14.3 7.0 %copy-start.3 = (bf16[504,512]{1,0:T(8,128)(2,1)}, bf16[504,512]{1,0:T(8,128)(2,1)S(1)}, u32[]{:S(2)}) copy-start(bf16[504,512]{1,0:T(8,128)(2,1)S(1)} %collective-permute-done.2.refs_3_) | copy-start | bytes 1548292
  17.3 4.0 %copy-start.1 = (bf16[504,512]{1,0:T(8,128)(2,1)}, bf16[504,512]{1,0:T(8,128)(2,1)S(1)}, u32[]{:S(2)}) copy-start(bf16[504,512]{1,0:T(8,128)(2,1)S(1)} %collective-permute-done.1.refs_2_) | copy-start | bytes 1548292
  21.3 14.4 %collective-permute-start.7 = (bf16[8,56,896]{2,1,0:T(8,128)(2,1)S(1)}, bf16[8,56,896]{2,1,0:T(8,128)(2,1)S(1)}, u32[]{:S(2)}, u32[]{:S(2)}) collective-permute-start(bf16[8,56,896]{2,1,0:T(8,128)(2,1)S(1)} %get-tuple-element.49), channel_id=1, source_target_pairs={{1,0},{0,1},{3,2},{2,3},{5,4},{4,5},{7,6},{6,7},{9,8},{8,9},{11,10... | collective-permute-start | bytes 2408456 | tf_op jit(solution)/shard_map/ppermute | solution.py:40
  35.2 2.4 %collective-permute-start.8 = (bf16[8,56,896]{2,1,0:T(8,128)(2,1)S(1)}, bf16[8,56,896]{2,1,0:T(8,128)(2,1)S(1)}, u32[]{:S(2)}, u32[]{:S(2)}) collective-permute-start(bf16[8,56,896]{2,1,0:T(8,128)(2,1)S(1)} %get-tuple-element.53), channel_id=1, source_target_pairs={{1,0},{0,1},{3,2},{2,3},{5,4},{4,5},{7,6},{6,7},{9,8},{8,9},{11,10... | collective-permute-start | bytes 2408456 | tf_op jit(solution)/shard_map/ppermute | solution.py:40
  38.5 7.7 %collective-permute-start.13 = (bf16[56,896]{1,0:T(8,128)(2,1)S(1)}, bf16[56,896]{1,0:T(8,128)(2,1)S(1)}, u32[]{:S(2)}, u32[]{:S(2)}) collective-permute-start(bf16[56,896]{1,0:T(8,128)(2,1)S(1)} %get-tuple-element.62), channel_id=1, source_target_pairs={{4,0},{8,4},{12,8},{16,12},{20,16},{24,20},{28,24},{0,28},{5,1},{9... | collective-permute-start | bytes 301064 | tf_op jit(solution)/shard_map/ppermute | solution.py:40
  44.2 5.6 %collective-permute-start.9 = (bf16[56,896]{1,0:T(8,128)(2,1)S(1)}, bf16[56,896]{1,0:T(8,128)(2,1)S(1)}, u32[]{:S(2)}, u32[]{:S(2)}) collective-permute-start(bf16[56,896]{1,0:T(8,128)(2,1)S(1)} %get-tuple-element.58), channel_id=1, source_target_pairs={{28,0},{0,4},{4,8},{8,12},{12,16},{16,20},{20,24},{24,28},{29,1},{... | collective-permute-start | bytes 301064 | tf_op jit(solution)/shard_map/ppermute | solution.py:40
  46.3 6.8 %collective-permute-start.14 = (bf16[112,896]{1,0:T(8,128)(2,1)S(1)}, bf16[112,896]{1,0:T(8,128)(2,1)S(1)}, u32[]{:S(2)}, u32[]{:S(2)}) collective-permute-start(bf16[112,896]{1,0:T(8,128)(2,1)S(1)} %pad_maximum_fusion.1), channel_id=1, source_target_pairs={{4,0},{8,4},{12,8},{16,12},{20,16},{24,20},{28,24},{0,28},{5,1},{9... | collective-permute-start | bytes 602120 | tf_op jit(solution)/shard_map/ppermute | solution.py:40
  49.8 6.8 %collective-permute-start.10 = (bf16[112,896]{1,0:T(8,128)(2,1)S(1)}, bf16[112,896]{1,0:T(8,128)(2,1)S(1)}, u32[]{:S(2)}, u32[]{:S(2)}) collective-permute-start(bf16[112,896]{1,0:T(8,128)(2,1)S(1)} %pad_maximum_fusion), channel_id=1, source_target_pairs={{28,0},{0,4},{4,8},{8,12},{12,16},{16,20},{20,24},{24,28},{29,1},{... | collective-permute-start | bytes 602120 | tf_op jit(solution)/shard_map/ppermute | solution.py:40
  53.2 6.1 %collective-permute-start.15 = (bf16[112,896]{1,0:T(8,128)(2,1)S(1)}, bf16[112,896]{1,0:T(8,128)(2,1)S(1)}, u32[]{:S(2)}, u32[]{:S(2)}) collective-permute-start(bf16[112,896]{1,0:T(8,128)(2,1)S(1)} %add_convert_fusion.3), channel_id=1, source_target_pairs={{4,0},{8,4},{12,8},{16,12},{20,16},{24,20},{28,24},{0,28},{5,1},{9... | collective-permute-start | bytes 602120 | tf_op jit(solution)/shard_map/ppermute | solution.py:40
  56.7 6.0 %collective-permute-start.11 = (bf16[112,896]{1,0:T(8,128)(2,1)S(1)}, bf16[112,896]{1,0:T(8,128)(2,1)S(1)}, u32[]{:S(2)}, u32[]{:S(2)}) collective-permute-start(bf16[112,896]{1,0:T(8,128)(2,1)S(1)} %add_convert_fusion.5), channel_id=1, source_target_pairs={{28,0},{0,4},{4,8},{8,12},{12,16},{16,20},{20,24},{24,28},{29,1},{... | collective-permute-start | bytes 602120 | tf_op jit(solution)/shard_map/ppermute | solution.py:40
  59.4 6.0 %collective-permute-start.16 = (bf16[112,896]{1,0:T(8,128)(2,1)S(1)}, bf16[112,896]{1,0:T(8,128)(2,1)S(1)}, u32[]{:S(2)}, u32[]{:S(2)}) collective-permute-start(bf16[112,896]{1,0:T(8,128)(2,1)S(1)} %add_convert_fusion.2), channel_id=1, source_target_pairs={{4,0},{8,4},{12,8},{16,12},{20,16},{24,20},{28,24},{0,28},{5,1},{9... | collective-permute-start | bytes 602120 | tf_op jit(solution)/shard_map/ppermute | solution.py:40
  62.8 5.9 %collective-permute-start.12 = (bf16[112,896]{1,0:T(8,128)(2,1)S(1)}, bf16[112,896]{1,0:T(8,128)(2,1)S(1)}, u32[]{:S(2)}, u32[]{:S(2)}) collective-permute-start(bf16[112,896]{1,0:T(8,128)(2,1)S(1)} %add_convert_fusion.4), channel_id=1, source_target_pairs={{28,0},{0,4},{4,8},{8,12},{12,16},{16,20},{20,24},{24,28},{29,1},{... | collective-permute-start | bytes 602120 | tf_op jit(solution)/shard_map/ppermute | solution.py:40
  69.4 6.4 %collective-permute-start.17 = (bf16[112,896]{1,0:T(8,128)(2,1)}, bf16[112,896]{1,0:T(8,128)(2,1)}, u32[]{:S(2)}, u32[]{:S(2)}) collective-permute-start(bf16[112,896]{1,0:T(8,128)(2,1)} %add_convert_fusion.1), channel_id=1, source_target_pairs={{2,0},{0,2},{3,1},{1,3},{6,4},{4,6},{7,5},{5,7},{10,8},{8,10},{11,... | collective-permute-start | bytes 602120 | tf_op jit(solution)/shard_map/ppermute | solution.py:40
  73.0 7.3 %collective-permute-start.19 = (bf16[56,896]{1,0:T(8,128)(2,1)S(1)}, bf16[56,896]{1,0:T(8,128)(2,1)S(1)}, u32[]{:S(2)}, u32[]{:S(2)}) collective-permute-start(bf16[56,896]{1,0:T(8,128)(2,1)S(1)} %slice.46), channel_id=1, source_target_pairs={{34,0},{195,1},{32,2},{193,3},{2,32},{227,33},{0,34},{225,35},{98,... | collective-permute-start | bytes 301064 | tf_op jit(solution)/shard_map/ppermute | solution.py:53
  73.1 7.2 %collective-permute-start.18 = (bf16[56,896]{1,0:T(8,128)(2,1)S(1)}, bf16[56,896]{1,0:T(8,128)(2,1)S(1)}, u32[]{:S(2)}, u32[]{:S(2)}) collective-permute-start(bf16[56,896]{1,0:T(8,128)(2,1)S(1)} %slice.46), channel_id=1, source_target_pairs={{32,0},{193,1},{0,32},{225,33},{96,64},{1,65},{64,96},{33,97},{160... | collective-permute-start | bytes 301064 | tf_op jit(solution)/shard_map/ppermute | solution.py:53
  80.3 26.6 %copy-start.4 = (bf16[504,512]{1,0:T(8,128)(2,1)S(1)}, bf16[504,512]{1,0:T(8,128)(2,1)}, u32[]{:S(2)}) copy-start(bf16[504,512]{1,0:T(8,128)(2,1)} %copy-done.3) | copy-start | bytes 1548292
  80.3 31.5 %copy-start.2 = (bf16[504,512]{1,0:T(8,128)(2,1)S(1)}, bf16[504,512]{1,0:T(8,128)(2,1)}, u32[]{:S(2)}) copy-start(bf16[504,512]{1,0:T(8,128)(2,1)} %copy-done.1) | copy-start | bytes 1548292
  80.4 5.9 %collective-permute-start.23 = (bf16[112,896]{1,0:T(8,128)(2,1)S(1)}, bf16[112,896]{1,0:T(8,128)(2,1)S(1)}, u32[]{:S(2)}, u32[]{:S(2)}) collective-permute-start(bf16[112,896]{1,0:T(8,128)(2,1)S(1)} %pad_maximum_fusion.2.refs_0_), channel_id=1, source_target_pairs={{28,0},{0,4},{4,8},{8,12},{12,16},{16,20},{20,24},{24,28},{29,1},{... | collective-permute-start | bytes 602120 | tf_op jit(solution)/shard_map/ppermute | solution.py:40
  80.5 5.8 %collective-permute-start.20 = (bf16[112,896]{1,0:T(8,128)(2,1)S(1)}, bf16[112,896]{1,0:T(8,128)(2,1)S(1)}, u32[]{:S(2)}, u32[]{:S(2)}) collective-permute-start(bf16[112,896]{1,0:T(8,128)(2,1)S(1)} %pad_maximum_fusion.2.refs_0_), channel_id=1, source_target_pairs={{4,0},{8,4},{12,8},{16,12},{20,16},{24,20},{28,24},{0,28},{5,1},{9... | collective-permute-start | bytes 602120 | tf_op jit(solution)/shard_map/ppermute | solution.py:40
  86.2 6.0 %collective-permute-start.24 = (bf16[112,896]{1,0:T(8,128)(2,1)S(1)}, bf16[112,896]{1,0:T(8,128)(2,1)S(1)}, u32[]{:S(2)}, u32[]{:S(2)}) collective-permute-start(bf16[112,896]{1,0:T(8,128)(2,1)S(1)} %collective-permute-done.23.refs_6_), channel_id=1, source_target_pairs={{28,0},{0,4},{4,8},{8,12},{12,16},{16,20},{20,24},{24,28},{29,1},{... | collective-permute-start | bytes 602120 | tf_op jit(solution)/shard_map/ppermute | solution.py:40
  86.2 6.0 %collective-permute-start.21 = (bf16[112,896]{1,0:T(8,128)(2,1)S(1)}, bf16[112,896]{1,0:T(8,128)(2,1)S(1)}, u32[]{:S(2)}, u32[]{:S(2)}) collective-permute-start(bf16[112,896]{1,0:T(8,128)(2,1)S(1)} %collective-permute-done.20.refs_1_), channel_id=1, source_target_pairs={{4,0},{8,4},{12,8},{16,12},{20,16},{24,20},{28,24},{0,28},{5,1},{9... | collective-permute-start | bytes 602120 | tf_op jit(solution)/shard_map/ppermute | solution.py:40
  92.2 7.1 %collective-permute-start.25 = (bf16[112,896]{1,0:T(8,128)(2,1)S(1)}, bf16[112,896]{1,0:T(8,128)(2,1)S(1)}, u32[]{:S(2)}, u32[]{:S(2)}) collective-permute-start(bf16[112,896]{1,0:T(8,128)(2,1)S(1)} %collective-permute-done.24.refs_5_), channel_id=1, source_target_pairs={{28,0},{0,4},{4,8},{8,12},{12,16},{16,20},{20,24},{24,28},{29,1},{... | collective-permute-start | bytes 602120 | tf_op jit(solution)/shard_map/ppermute | solution.py:40
  92.2 7.2 %collective-permute-start.22 = (bf16[112,896]{1,0:T(8,128)(2,1)S(1)}, bf16[112,896]{1,0:T(8,128)(2,1)S(1)}, u32[]{:S(2)}, u32[]{:S(2)}) collective-permute-start(bf16[112,896]{1,0:T(8,128)(2,1)S(1)} %collective-permute-done.21.refs_2_), channel_id=1, source_target_pairs={{4,0},{8,4},{12,8},{16,12},{20,16},{24,20},{28,24},{0,28},{5,1},{9... | collective-permute-start | bytes 602120 | tf_op jit(solution)/shard_map/ppermute | solution.py:40
  100.1 26.8 %collective-permute-start.26 = (bf16[7,112,896]{2,1,0:T(8,128)(2,1)S(1)}, bf16[7,112,896]{2,1,0:T(8,128)(2,1)S(1)}, u32[]{:S(2)}, u32[]{:S(2)}) collective-permute-start(bf16[7,112,896]{2,1,0:T(8,128)(2,1)S(1)} %shard_map.22.group), channel_id=1, source_target_pairs={{1,0},{0,1},{3,2},{2,3},{5,4},{4,5},{7,6},{6,7},{9,8},{8,9},{11,10... | collective-permute-start | bytes 4214792 | tf_op jit(solution)/shard_map/ppermute | solution.py:40
  106.9 17.5 %collective-permute-start.3 = (bf16[504,512]{1,0:T(8,128)(2,1)S(1)}, bf16[504,512]{1,0:T(8,128)(2,1)S(1)}, u32[]{:S(2)}, u32[]{:S(2)}) collective-permute-start(bf16[504,512]{1,0:T(8,128)(2,1)S(1)} %copy-done.4), channel_id=1, source_target_pairs={{64,0},{128,64},{192,128},{0,192},{65,1},{129,65},{193,129},{1,193... | collective-permute-start | bytes 1548296 | tf_op jit(solution)/shard_map/ppermute | solution.py:40
  111.9 14.1 %collective-permute-start.6 = (bf16[504,512]{1,0:T(8,128)(2,1)S(1)}, bf16[504,512]{1,0:T(8,128)(2,1)S(1)}, u32[]{:S(2)}, u32[]{:S(2)}) collective-permute-start(bf16[504,512]{1,0:T(8,128)(2,1)S(1)} %copy-done.2), channel_id=1, source_target_pairs={{192,0},{0,64},{64,128},{128,192},{193,1},{1,65},{65,129},{129,193... | collective-permute-start | bytes 1548296 | tf_op jit(solution)/shard_map/ppermute | solution.py:40
  111.9 14.1 %collective-permute-start.4 = (bf16[504,512]{1,0:T(8,128)(2,1)S(1)}, bf16[504,512]{1,0:T(8,128)(2,1)S(1)}, u32[]{:S(2)}, u32[]{:S(2)}) collective-permute-start(bf16[504,512]{1,0:T(8,128)(2,1)S(1)} %copy-done.2), channel_id=1, source_target_pairs={{32,0},{0,32},{33,1},{1,33},{34,2},{2,34},{35,3},{3,35},{36,4},{4,... | collective-permute-start | bytes 1548296 | tf_op jit(solution)/shard_map/ppermute | solution.py:40
  111.9 4.7 %collective-permute-start.27 = (bf16[56,896]{1,0:T(8,128)(2,1)S(1)}, bf16[56,896]{1,0:T(8,128)(2,1)S(1)}, u32[]{:S(2)}, u32[]{:S(2)}) collective-permute-start(bf16[56,896]{1,0:T(8,128)(2,1)S(1)} %slice.47), channel_id=1, source_target_pairs={{4,0},{8,4},{12,8},{16,12},{20,16},{24,20},{28,24},{0,28},{5,1},{9... | collective-permute-start | bytes 301064 | tf_op jit(solution)/shard_map/ppermute | solution.py:40
  116.6 5.7 %collective-permute-start.28 = (bf16[56,896]{1,0:T(8,128)(2,1)S(1)}, bf16[56,896]{1,0:T(8,128)(2,1)S(1)}, u32[]{:S(2)}, u32[]{:S(2)}) collective-permute-start(bf16[56,896]{1,0:T(8,128)(2,1)S(1)} %slice.48), channel_id=1, source_target_pairs={{28,0},{0,4},{4,8},{8,12},{12,16},{16,20},{20,24},{24,28},{29,1},{... | collective-permute-start | bytes 301064 | tf_op jit(solution)/shard_map/ppermute | solution.py:40
  122.3 8.5 %collective-permute-start.29 = (bf16[112,896]{1,0:T(8,128)(2,1)S(1)}, bf16[112,896]{1,0:T(8,128)(2,1)S(1)}, u32[]{:S(2)}, u32[]{:S(2)}) collective-permute-start(bf16[112,896]{1,0:T(8,128)(2,1)S(1)} %constant_dynamic-update-slice_fusion.refs_0_), channel_id=1, source_target_pairs={{1,0},{0,1},{3,2},{2,3},{5,4},{4,5},{7,6},{6,7},{9,8},{8,9},{11,10... | collective-permute-start | bytes 602120 | tf_op jit(solution)/shard_map/ppermute | solution.py:40
  132.8 12.1 %collective-permute-start.32 = (bf16[504,512]{1,0:T(8,128)(2,1)S(1)}, bf16[504,512]{1,0:T(8,128)(2,1)S(1)}, u32[]{:S(2)}, u32[]{:S(2)}) collective-permute-start(bf16[504,512]{1,0:T(8,128)(2,1)S(1)} %get-tuple-element.69.refs_0_), channel_id=1, source_target_pairs={{32,0},{0,32},{33,1},{1,33},{34,2},{2,34},{35,3},{3,35},{36,4},{4,... | collective-permute-start | bytes 1548296 | tf_op jit(solution)/shard_map/ppermute | solution.py:40
  132.9 13.4 %collective-permute-start.31 = (bf16[504,512]{1,0:T(8,128)(2,1)S(1)}, bf16[504,512]{1,0:T(8,128)(2,1)S(1)}, u32[]{:S(2)}, u32[]{:S(2)}) collective-permute-start(bf16[504,512]{1,0:T(8,128)(2,1)S(1)} %get-tuple-element.69.refs_0_), channel_id=1, source_target_pairs={{192,0},{0,64},{64,128},{128,192},{193,1},{1,65},{65,129},{129,193... | collective-permute-start | bytes 1548296 | tf_op jit(solution)/shard_map/ppermute | solution.py:40
  133.0 13.3 %collective-permute-start.30 = (bf16[504,512]{1,0:T(8,128)(2,1)S(1)}, bf16[504,512]{1,0:T(8,128)(2,1)S(1)}, u32[]{:S(2)}, u32[]{:S(2)}) collective-permute-start(bf16[504,512]{1,0:T(8,128)(2,1)S(1)} %get-tuple-element.69.refs_0_), channel_id=1, source_target_pairs={{64,0},{128,64},{192,128},{0,192},{65,1},{129,65},{193,129},{1,193... | collective-permute-start | bytes 1548296 | tf_op jit(solution)/shard_map/ppermute | solution.py:40
  146.3 11.9 %collective-permute-start.34 = (bf16[504,512]{1,0:T(8,128)(2,1)S(1)}, bf16[504,512]{1,0:T(8,128)(2,1)S(1)}, u32[]{:S(2)}, u32[]{:S(2)}) collective-permute-start(bf16[504,512]{1,0:T(8,128)(2,1)S(1)} %collective-permute-done.32.refs_3_), channel_id=1, source_target_pairs={{64,0},{128,64},{192,128},{0,192},{65,1},{129,65},{193,129},{1,193... | collective-permute-start | bytes 1548296 | tf_op jit(solution)/shard_map/ppermute | solution.py:40
  148.7 10.6 %collective-permute-start.35 = (bf16[504,512]{1,0:T(8,128)(2,1)S(1)}, bf16[504,512]{1,0:T(8,128)(2,1)S(1)}, u32[]{:S(2)}, u32[]{:S(2)}) collective-permute-start(bf16[504,512]{1,0:T(8,128)(2,1)S(1)} %collective-permute-done.31.refs_2_), channel_id=1, source_target_pairs={{32,0},{0,32},{33,1},{1,33},{34,2},{2,34},{35,3},{3,35},{36,4},{4,... | collective-permute-start | bytes 1548296 | tf_op jit(solution)/shard_map/ppermute | solution.py:40
  149.8 11.3 %collective-permute-start.33 = (bf16[504,512]{1,0:T(8,128)(2,1)S(1)}, bf16[504,512]{1,0:T(8,128)(2,1)S(1)}, u32[]{:S(2)}, u32[]{:S(2)}) collective-permute-start(bf16[504,512]{1,0:T(8,128)(2,1)S(1)} %collective-permute-done.31.refs_2_), channel_id=1, source_target_pairs={{192,0},{0,64},{64,128},{128,192},{193,1},{1,65},{65,129},{129,193... | collective-permute-start | bytes 1548296 | tf_op jit(solution)/shard_map/ppermute | solution.py:40
  161.1 7.0 %collective-permute-start.36 = (bf16[256,512]{1,0:T(8,128)(2,1)S(1)}, bf16[256,512]{1,0:T(8,128)(2,1)S(1)}, u32[]{:S(2)}, u32[]{:S(2)}) collective-permute-start(bf16[256,512]{1,0:T(8,128)(2,1)S(1)} %slice.42), channel_id=1, source_target_pairs={{64,0},{128,64},{192,128},{0,192},{65,1},{129,65},{193,129},{1,193... | collective-permute-start | bytes 786440 | tf_op jit(solution)/shard_map/ppermute | solution.py:40
  161.6 6.4 %collective-permute-start.37 = (bf16[248,512]{1,0:T(8,128)(2,1)S(1)}, bf16[248,512]{1,0:T(8,128)(2,1)S(1)}, u32[]{:S(2)}, u32[]{:S(2)}) collective-permute-start(bf16[248,512]{1,0:T(8,128)(2,1)S(1)} %slice.43), channel_id=1, source_target_pairs={{192,0},{0,64},{64,128},{128,192},{193,1},{1,65},{65,129},{129,193... | collective-permute-start | bytes 761864 | tf_op jit(solution)/shard_map/ppermute | solution.py:40

commit v2 on v1

--- a/solution.py
+++ b/solution.py
@@ -73,21 +73,16 @@
 
 
 def first_blocks(own):
-    return own, shift(own, "x", 1), shift(own, "x", -1), shift(own, "yl", 1)
-
-
-def more_blocks(first):
-    _, _, r30, r01 = first
-    r20 = shift(r30, "x", -1)
+    near = shift(own, "x", 1), shift(own, "x", -1), shift(own, "yl", 1)
+    return lax.optimization_barrier(near), shift(own, "x", 2)
+
+
+def more_blocks(near, r20):
+    _, _, r01 = near
     r11 = shift(r01, "x", 1)
-    r31 = shift(r30, "yl", 1)
-    return r20, r11, r31
-
-
-def last_block(more):
-    _, r11, r31 = more
-    half = (r11.shape[0] // 2 + 15) // 16 * 16
-    return shift(r11[:half], "x", 1), shift(r31[half:], "x", -1)
+    r31 = shift(r01, "x", -1)
+    r21 = shift(r20, "yl", 1)
+    return r11, r31, r21
 
 
 def packing(rows, cols):
@@ -138,7 +133,7 @@
 
 
 def gram_body(place, own, *refs):
-    *blocks, keep, send, panel, partner, beside, rows, mixed = refs
+    *blocks, keep, send, panel, partner, rows, mixed = refs
     fill(panel, blocks)
     z, c = place[0], place[1]
     height = own.shape[0]
@@ -150,7 +145,6 @@
         rows[i] = lax.dot_general(own[...], panel[i], DIMS, preferred_element_type=F32)
 
     partner[...] = lax.dot_general(panel[1, height:], mixed[...], DIMS, preferred_element_type=F32)
-    beside[...] = lax.dot_general(panel[0, height:], panel[1, :height], DIMS, preferred_element_type=F32)
     split_units(z, c, rows, keep, send)
 
 
@@ -161,19 +155,22 @@
             out[far] = rows[side, chunk(z, far, size), :].astype(BF16)
 
 
-def late_body(place, own, partner, beside, block, keep, send, rows, panel):
+def late_body(place, own, low, partner, block, keep, send, rows, panel):
     z, c = place[0], place[1]
     height = own.shape[0]
     fill(panel, [block])
     rows[0] = partner[...]
-    rows[1, :, :height] = lax.dot_general(own[...], panel[0, :height], DIMS, preferred_element_type=F32)
-    rows[1, :, height:] = beside[...]
+    rows[1, :, :height] = lax.dot_general(low[1, height:], panel[0, :height], DIMS, preferred_element_type=F32)
+    rows[1, :, height:] = lax.dot_general(own[...], panel[0, :height], DIMS, preferred_element_type=F32)
     split_units(z, c, rows, keep, send)
 
 
-def panel_body(place, *refs):
-    *blocks, panel = refs
-    fill(panel, blocks)
+def panel_body(place, low, *refs):
+    *blocks, panel, high = refs
+    fill(high, blocks)
+    for i in range(2):
+        panel[i] = low[i]
+        panel[i + 2] = high[i]
 
 
 def pair_body(place, low, low_other, high, high_other, *outs):
@@ -216,40 +213,50 @@
         out[i] = ref[...]
 
 
-def rows_body(place, low, high, group, other, near, far, total):
+def lay(gram, side, group, z):
+    size = gram.shape[1] // RING
+    for i in range(RING - 1):
+        where = chunk(z, i if i < FAR else i + 1, size)
+        gram[side, where, :] = group[i, :size]
+        gram[side + 2, where, :] = group[i, size:]
+    for half in (side, side + 2):
+        gram[half, chunk(z, FAR, size), :] = jnp.zeros((size, gram.shape[2]), BF16)
+
+
+def own_rows_body(place, panel, group, gram, total):
     z, c = place[0], place[1]
-    size = near.shape[1] // RING
-    for side, ref in ((c, group), (1 - c, other)):
-        for i in range(RING - 1):
-            where = chunk(z, i if i < FAR else i + 1, size)
-            near[side, where, :] = ref[i, :size]
-            far[side, where, :] = ref[i, size:]
-    for side in range(2):
-        near[side, chunk(z, FAR, size), :] = jnp.zeros((size, near.shape[2]), BF16)
-        far[side, chunk(z, FAR, size), :] = jnp.zeros((size, near.shape[2]), BF16)
+    lay(gram, c, group, z)
     total[...] = jnp.zeros(total.shape, F32)
 
     @pl.loop(0, 2)
     def _(i):
-        total[...] += jnp.dot(near[i], low[i], preferred_element_type=F32) + jnp.dot(
-            far[i], high[i], preferred_element_type=F32
-        )
-
-
-def update_body(place, own, low, high, near, far, before, *refs):
-    mine, other, near_out, far_out, w_high, w_low, total = refs
+        total[...] += jnp.dot(gram[c + 2 * i], panel[c + 2 * i], preferred_element_type=F32)
+
+
+def other_rows_body(place, panel, group, before_gram, before, gram, total):
+    z, side = place[0], 1 - place[1]
+    lay(gram, side, group, z)
+
+    @pl.loop(0, 2)
+    def _(i):
+        total[...] += jnp.dot(gram[side + 2 * i], panel[side + 2 * i], preferred_element_type=F32)
+
+
+def update_body(place, own, panel, before_gram, before, mine, other, gram, w_high, w_low, total, acc):
     z, c = place[0], place[1]
-    size = near.shape[1] // RING
+    size = gram.shape[1] // RING
     where = chunk(z, FAR, size)
     for side, ref in ((c, mine), (1 - c, other)):
-        near_out[side, where, :] = ref[:size]
-        far_out[side, where, :] = ref[size:]
-    acc = jnp.zeros((size, own.shape[1]), F32)
-    for gram, panel in ((near_out, low), (far_out, high)):
-        for i in range(2):
-            acc += jnp.dot(gram[i, where, :], panel[i], preferred_element_type=F32)
+        gram[side, where, :] = ref[:size]
+        gram[side + 2, where, :] = ref[size:]
+    acc[...] = jnp.zeros(acc.shape, F32)
+
+    @pl.loop(0, 4)
+    def _(i):
+        acc[...] += jnp.dot(gram[i, where, :], panel[i], preferred_element_type=F32)
+
     total[...] = before[...]
-    total[where, :] = acc
+    total[where, :] = acc[...]
     w = coef_b * own[...].astype(F32) + coef_c * total[...]
     pack(w, w_high)
     w_low[...] = (w - w.astype(BF16).astype(F32)).astype(BF16)
@@ -260,25 +267,24 @@
     rows = own.shape[0]
     fill(panel, blocks)
     acc = coef_a * own[...].astype(F32)
-    acc += jnp.dot(gram[0][:, :rows], w_low[...], preferred_element_type=F32)
-    total[...] = acc
+    total[...] = acc + jnp.dot(gram[0][:, :rows], w_low[...], preferred_element_type=F32)
 
     @pl.loop(0, 2)
     def _(i):
         total[...] += jnp.dot(gram[i], panel[i], preferred_element_type=F32)
 
 
-def side_body(place, before, gram, *refs):
-    *blocks, total, panel = refs
-    fill(panel, blocks)
-    total[...] = before[...] + jnp.dot(gram[0], panel[0], preferred_element_type=F32)
-
-
-def far_body(place, before, gram, *refs):
-    *blocks, out, panel = refs
-    fill(panel, blocks)
-    acc = before[...] + jnp.dot(gram[1], panel[0], preferred_element_type=F32)
+def side_body(place, before, gram, block, total, panel):
+    rows = total.shape[0]
+    fill(panel, [block])
+    total[...] = before[...] + jnp.dot(gram[3][:, rows:], panel[0, :rows], preferred_element_type=F32)
+
+
+def far_body(place, before, gram, r11, r31, r21, out, panel):
     rows, cols = out.shape
+    fill(panel, (r11, r31, r21))
+    acc = before[...] + jnp.dot(gram[2], panel[0], preferred_element_type=F32)
+    acc += jnp.dot(gram[3][:, :rows], panel[1, :rows], preferred_element_type=F32)
     factor = 0.2 * math.sqrt(max(rows * PANEL, cols * math.prod(SIZES[n] for n in COL)))
     out[...] = (acc * factor).astype(BF16)
 
@@ -292,45 +298,40 @@
     block = array((rows, cols))
 
     packed, own = call(pack_body, place, (matrix,), [flat, block], fixed=False)
-    first = lax.optimization_barrier(first_blocks(packed))
-    r21 = fetch(packed, ("x", "yl"), lambda x, y: (x + 2, y + 1))
+    near, r20 = first_blocks(packed)
     part = array((RING, size, 2 * rows))
-    wide = array((2, rows, 2 * rows))
-    panel = array((2, 2 * rows, cols))
+    wide = array((4, rows, 2 * rows))
+    sums = array((rows, cols), F32)
     work = 4 * rows * rows * cols
-    keep, send, low, partner, beside = call(
+
+    def room(count, kind=BF16, width=cols):
+        return pltpu.VMEM((count, 2 * rows, width), kind)
+
+    pairs = pltpu.VMEM((2, rows, 2 * rows), F32)
+    keep, send, low, partner = call(
         gram_body,
         place,
-        (own, *first),
-        [part, part, panel, array((rows, 2 * rows), F32), array((rows, rows), F32)],
-        7 * work // 2,
-        [pltpu.VMEM(wide.shape, F32), pltpu.VMEM((2 * rows, cols), BF16)],
+        (own, packed, *near),
+        [part, part, array((2, 2 * rows, cols)), array((rows, 2 * rows), F32)],
+        3 * work,
+        [pairs, pltpu.VMEM((2 * rows, cols), BF16)],
     )
     halves = [keep, shift(send, "c", 1)]
-    keep, send = call(
-        late_body,
-        place,
-        (own, partner, beside, r21),
-        [part, part],
-        work // 2,
-        [pltpu.VMEM(wide.shape, F32), pltpu.VMEM((1, 2 * rows, cols), BF16)],
-    )
+    keep, send = call(late_body, place, (own, low, partner, r20), [part, part], work, [pairs, room(1)])
     halves += [keep, shift(send, "c", 1)]
-    r20, r11, r31 = more_blocks(first)
-    high = call(panel_body, place, (r11, r31, r21, r20), panel)
+    r11, r31, r21 = more_blocks(near, r20)
+    panel = call(panel_body, place, (low, r11, r31, r21, r20), array((4, 2 * rows, cols)), 0, [room(2)])
     one, two = array((size, 2 * rows)), array((2 * size, 2 * rows))
     parts = call(pair_body, place, halves, [two] * FAR + [one] * 2 + [two] * (FAR - 1))
     part = {d: parts[d if d < FAR else d + 1] for d in range(RING) if d != FAR}
     mine = ring_sum(part, parts[FAR], parts[FAR + 1])
     ahead = mine[size:]
-    same = fetch(ahead, ("x", "yl", "c"), lambda x, y, c: (x, y + 1, c) if c == 0 else (x - 1, y, c))
-    cross = fetch(
-        ahead, ("x", "yl", "yh", "c"), lambda x, y, h, c: (x, y + 1, h + 1, c) if c == 0 else (x - 1, y, h + 1, c)
-    )
+    same = shift(ahead, "yl", 1)
+    cross = fetch(ahead, ("yl", "yh"), lambda y, h: (y + 1, h + 1))
     mine = add(mine, shift(mine, "yh", 1))
     ahead = add(same, cross)
-    left = lax.broadcasted_iota(jnp.int32, ahead.shape, 1) < rows
-    ahead = jnp.where((place[1] == 1) & left, mine[size:], ahead)
+    right = lax.broadcasted_iota(jnp.int32, ahead.shape, 1) >= rows
+    ahead = jnp.where((place[1] == 1) & right, mine[size:], ahead)
     mine = jnp.concatenate([mine[:size], ahead], 0)
 
     ring = {0: mine}
@@ -345,28 +346,24 @@
     group = call(group_body, place, pieces, array((RING - 1, 2 * size, 2 * rows)))
     ends = jnp.concatenate(ends, 0)
 
-    sums = array((rows, cols), F32)
     other = shift(group, "c", 1)
-    gram_near, gram_far, total = call(rows_body, place, (low, high, group, other), [wide, wide, sums], 4 * work)
-    gram_near, gram_far, w_high, w_low = call(
+    gram, total = call(own_rows_body, place, (panel, group), [wide, sums], 2 * work)
+    gram, total = call(other_rows_body, place, (panel, other, gram, total), [wide, sums], 2 * work, alias={3: 0, 4: 1})
+    gram, w_high, w_low = call(
         update_body,
         place,
-        (own, low, high, gram_near, gram_far, total, ends, shift(ends, "c", 1)),
-        [wide, wide, flat, block],
+        (own, panel, gram, total, ends, shift(ends, "c", 1)),
+        [wide, flat, block],
         work // 2,
-        [pltpu.VMEM((rows, cols), F32)],
-        alias={4: 0, 5: 1},
+        [pltpu.VMEM((rows, cols), F32), pltpu.VMEM((size, cols), F32)],
+        alias={3: 0},
     )
 
-    def room(count):
-        return [pltpu.VMEM((count, 2 * rows, cols), BF16)]
-
-    near = lax.optimization_barrier(first_blocks(w_high))
-    total = call(near_body, place, (own, w_low, gram_near, *near), sums, 5 * work // 2, room(2))
-    side = lax.optimization_barrier(more_blocks(near))
-    total = call(side_body, place, (total, gram_far, *side[1:]), sums, work, room(1))
-    ends = last_block(side)
-    return call(far_body, place, (total, gram_far, *ends, side[0]), block, work, room(1), home=True)
+    near, r20 = first_blocks(w_high)
+    total = call(near_body, place, (own, w_low, gram, w_high, *near), sums, 5 * work // 2, [room(2)])
+    ends = more_blocks(near, r20)
+    total = call(side_body, place, (total, gram, r20), sums, work // 2, [room(1)])
+    return call(far_body, place, (total, gram, *ends), block, 3 * work // 2, [room(2)], home=True)
 
 
 def solution(mesh):

time: 173 us -> 176 us (1.017)
  Pallas kernels: 21.1 us -> 23 us
    ppermute x35 -> x36, waiting for transfers between devices: 70 us -> 74.2 us  [shift(): lax.ppermute(value, axis, [((i + step) % size, i) for i in range(size)])]
    ppermute x3 -> x1, waiting for transfers between devices: 3.38 us -> 0.87 us  [fetch(): lax.ppermute(value, axes, [(flat(source(*p)), flat(p)) for p in places])]
    pallas_call x11 -> x12, Pallas kernels: 21.1 us -> 23 us  [call(): pl.pallas_call(body, out_shape=outs if home else [pltpu.VMEM(o.shape, o.d...]
    ppermute x35 -> x36, starting transfers between devices: 69.7 us -> 71.6 us  [shift(): lax.ppermute(value, axis, [((i + step) % size, i) for i in range(size)])]
  transfers between devices with their start and end apart: 38 -> 37, of which waited for: 24 -> 22; matrix products, arithmetic and copies ran while one was open for 1% -> 1% of each run, Pallas kernels for 9% -> 9%
where the time goes in v2:
time: 176 us; the launch traced here: 174 us
  waiting for transfers between devices  75 us (43%)
  starting transfers between devices  71.7 us (41%)
  Pallas kernels  23 us (13%)
  other arithmetic  2.28 us (1%)
  local copies, waits for them, and re-layouts  2.06 us (1%)
    ppermute x36, waiting for transfers between devices, shift(): lax.ppermute(value, axis, [((i + step) % size, i) for i in range(size)])  74.2 us
    ppermute x36, starting transfers between devices, shift(): lax.ppermute(value, axis, [((i + step) % size, i) for i in range(size)])  71.6 us
    pallas_call x12, Pallas kernels, call(): pl.pallas_call(body, out_shape=outs if home else [pltpu.VMEM(o.shape, o.d...  23 us
  transfers between devices with their start and end apart: 37, of which 22 were waited for; matrix products, arithmetic and copies ran while one was open for 1% of the time, Pallas kernels for 9%

profile of v2, /device:TPU:1, one launch (start us, length us, event | category | flops | bytes accessed | tf_op | source)
XLA Modules:
  0.0 174.3 jit_solution(13962305671154183672)
XLA Ops:
  0.1 1.1 copy-done
  1.1 0.6 shard_map.17
  1.8 2.2 %collective-permute-start.2 = (bf16[504,512]{1,0:T(8,128)(2,1)S(1)}, bf16[504,512]{1,0:T(8,128)(2,1)S(1)}, u32[]{:S(2)}, u32[]{:S(2)}) collective-permute-start(bf16[504,512]{1,0:T(8,128)(2,1)S(1)} %get-tuple-element.36.refs_0_), channel_id=1, source_target_pairs={{32,0},{0,32},{33,1},{1,33},{34,2},{2,34},{35,3},{3,35},{36,4},{4,... | collective-permute-start | bytes 1548296 | tf_op jit(solution)/shard_map/ppermute | solution.py:40
  4.0 1.2 collective-permute-start.1
  5.2 1.5 collective-permute-start
  6.7 1.5 collective-permute-start.5
  8.2 6.1 %collective-permute-done.2.refs_3_ = bf16[504,512]{1,0:T(8,128)(2,1)S(1)} collective-permute-done((bf16[504,512]{1,0:T(8,128)(2,1)S(1)}, bf16[504,512]{1,0:T(8,128)(2,1)S(1)}, u32[]{:S(2)}, u32[]{:S(2)}) %collective-permute-start.2) | collective-permute-done | bytes 516128 | tf_op jit(solution)/shard_map/ppermute | solution.py:40
  14.3 3.0 %collective-permute-done.1.refs_2_ = bf16[504,512]{1,0:T(8,128)(2,1)S(1)} collective-permute-done((bf16[504,512]{1,0:T(8,128)(2,1)S(1)}, bf16[504,512]{1,0:T(8,128)(2,1)S(1)}, u32[]{:S(2)}, u32[]{:S(2)}) %collective-permute-start.1) | collective-permute-done | bytes 516128 | tf_op jit(solution)/shard_map/ppermute | solution.py:40
  17.3 3.6 %shard_map.18 = (bf16[8,56,896]{2,1,0:T(8,128)(2,1)S(1)}, bf16[8,56,896]{2,1,0:T(8,128)(2,1)S(1)}, bf16[2,896,576]{2,1,0:T(8,128)(2,1)S(1)}, f32[448,896]{1,0:T(8,128)S(1)}) custom-call(s32[2]{0:T(128)S(1)} %pad_add_fusion.place, bf16[448,576]{1,0:T(8,128)(2,1)S(1)} %get-tuple-element.35.own, bf16[504,512]{1,0:T(8,128)(2,1)S(1)} %get-tuple-element.36.refs_0_, ...), custom_call_target="tpu_custom_call" | custom-call | flops 1387266048 | bytes 7053312 | tf_op jit(solution)/shard_map/pallas_call | solution.py:62
  21.0 12.5 %collective-permute-start.7 = (bf16[8,56,896]{2,1,0:T(8,128)(2,1)S(1)}, bf16[8,56,896]{2,1,0:T(8,128)(2,1)S(1)}, u32[]{:S(2)}, u32[]{:S(2)}) collective-permute-start(bf16[8,56,896]{2,1,0:T(8,128)(2,1)S(1)} %get-tuple-element.42), channel_id=1, source_target_pairs={{1,0},{0,1},{3,2},{2,3},{5,4},{4,5},{7,6},{6,7},{9,8},{8,9},{11,10... | collective-permute-start | bytes 2408456 | tf_op jit(solution)/shard_map/ppermute | solution.py:40
  33.5 1.9 %shard_map.20 = (bf16[8,56,896]{2,1,0:T(8,128)(2,1)S(1)}, bf16[8,56,896]{2,1,0:T(8,128)(2,1)S(1)}) custom-call(s32[2]{0:T(128)S(1)} %pad_add_fusion.place, bf16[448,576]{1,0:T(8,128)(2,1)S(1)} %get-tuple-element.35.own, bf16[2,896,576]{2,1,0:T(8,128)(2,1)S(1)} %get-tuple-element.40.low, f32[448,896]{1,0:T(8,128)S(1)} %get-tuple-element.43.partner, ...), custom_call_target="tpu_custom_call" | custom-call | flops 462422016 | bytes 5505024 | tf_op jit(solution)/shard_map/pallas_call | solution.py:62
  35.3 0.1 collective-permute-start.8
  35.5 2.3 %collective-permute-done.8.high_other = bf16[8,56,896]{2,1,0:T(8,128)(2,1)S(1)} collective-permute-done((bf16[8,56,896]{2,1,0:T(8,128)(2,1)S(1)}, bf16[8,56,896]{2,1,0:T(8,128)(2,1)S(1)}, u32[]{:S(2)}, u32[]{:S(2)}) %collective-permute-start.8) | collective-permute-done | bytes 802848 | tf_op jit(solution)/shard_map/ppermute | solution.py:40
  37.7 0.9 shard_map.21
  38.7 5.7 %collective-permute-start.13 = (bf16[56,896]{1,0:T(8,128)(2,1)S(1)}, bf16[56,896]{1,0:T(8,128)(2,1)S(1)}, u32[]{:S(2)}, u32[]{:S(2)}) collective-permute-start(bf16[56,896]{1,0:T(8,128)(2,1)S(1)} %get-tuple-element.54), channel_id=1, source_target_pairs={{4,0},{8,4},{12,8},{16,12},{20,16},{24,20},{28,24},{0,28},{5,1},{9... | collective-permute-start | bytes 301064 | tf_op jit(solution)/shard_map/ppermute | solution.py:40
  44.4 1.9 %collective-permute-done.13 = bf16[56,896]{1,0:T(8,128)(2,1)S(1)} collective-permute-done((bf16[56,896]{1,0:T(8,128)(2,1)S(1)}, bf16[56,896]{1,0:T(8,128)(2,1)S(1)}, u32[]{:S(2)}, u32[]{:S(2)}) %collective-permute-start.13) | collective-permute-done | bytes 100384 | tf_op jit(solution)/shard_map/ppermute | solution.py:40
  46.4 3.5 %collective-permute-start.14 = (bf16[112,896]{1,0:T(8,128)(2,1)S(1)}, bf16[112,896]{1,0:T(8,128)(2,1)S(1)}, u32[]{:S(2)}, u32[]{:S(2)}) collective-permute-start(bf16[112,896]{1,0:T(8,128)(2,1)S(1)} %pad_maximum_fusion.1), channel_id=1, source_target_pairs={{4,0},{8,4},{12,8},{16,12},{20,16},{24,20},{28,24},{0,28},{5,1},{9... | collective-permute-start | bytes 602120 | tf_op jit(solution)/shard_map/ppermute | solution.py:40
  50.1 3.2 %collective-permute-done.14 = bf16[112,896]{1,0:T(8,128)(2,1)S(1)} collective-permute-done((bf16[112,896]{1,0:T(8,128)(2,1)S(1)}, bf16[112,896]{1,0:T(8,128)(2,1)S(1)}, u32[]{:S(2)}, u32[]{:S(2)}) %collective-permute-start.14) | collective-permute-done | bytes 200736 | tf_op jit(solution)/shard_map/ppermute | solution.py:40
  53.3 3.5 %collective-permute-start.15 = (bf16[112,896]{1,0:T(8,128)(2,1)S(1)}, bf16[112,896]{1,0:T(8,128)(2,1)S(1)}, u32[]{:S(2)}, u32[]{:S(2)}) collective-permute-start(bf16[112,896]{1,0:T(8,128)(2,1)S(1)} %add_convert_fusion.3), channel_id=1, source_target_pairs={{4,0},{8,4},{12,8},{16,12},{20,16},{24,20},{28,24},{0,28},{5,1},{9... | collective-permute-start | bytes 602120 | tf_op jit(solution)/shard_map/ppermute | solution.py:40
  56.9 0.3 collective-permute-start.11
  57.2 2.3 %collective-permute-done.15 = bf16[112,896]{1,0:T(8,128)(2,1)S(1)} collective-permute-done((bf16[112,896]{1,0:T(8,128)(2,1)S(1)}, bf16[112,896]{1,0:T(8,128)(2,1)S(1)}, u32[]{:S(2)}, u32[]{:S(2)}) %collective-permute-start.15) | collective-permute-done | bytes 200736 | tf_op jit(solution)/shard_map/ppermute | solution.py:40
  59.5 3.2 %collective-permute-start.16 = (bf16[112,896]{1,0:T(8,128)(2,1)S(1)}, bf16[112,896]{1,0:T(8,128)(2,1)S(1)}, u32[]{:S(2)}, u32[]{:S(2)}) collective-permute-start(bf16[112,896]{1,0:T(8,128)(2,1)S(1)} %add_convert_fusion.2), channel_id=1, source_target_pairs={{4,0},{8,4},{12,8},{16,12},{20,16},{24,20},{28,24},{0,28},{5,1},{9... | collective-permute-start | bytes 602120 | tf_op jit(solution)/shard_map/ppermute | solution.py:40
  62.7 0.2 collective-permute-done.11
  63.1 2.3 %collective-permute-done.16 = bf16[112,896]{1,0:T(8,128)(2,1)S(1)} collective-permute-done((bf16[112,896]{1,0:T(8,128)(2,1)S(1)}, bf16[112,896]{1,0:T(8,128)(2,1)S(1)}, u32[]{:S(2)}, u32[]{:S(2)}) %collective-permute-start.16) | collective-permute-done | bytes 200736 | tf_op jit(solution)/shard_map/ppermute | solution.py:40
  65.4 3.4 %collective-permute-done.12 = bf16[112,896]{1,0:T(8,128)(2,1)S(1)} collective-permute-done((bf16[112,896]{1,0:T(8,128)(2,1)S(1)}, bf16[112,896]{1,0:T(8,128)(2,1)S(1)}, u32[]{:S(2)}, u32[]{:S(2)}) %collective-permute-start.12) | collective-permute-done | bytes 200736 | tf_op jit(solution)/shard_map/ppermute | solution.py:40
  68.8 0.8 add_convert_fusion.1
  69.6 2.6 %collective-permute-start.17 = (bf16[112,896]{1,0:T(8,128)(2,1)}, bf16[112,896]{1,0:T(8,128)(2,1)}, u32[]{:S(2)}, u32[]{:S(2)}) collective-permute-start(bf16[112,896]{1,0:T(8,128)(2,1)} %add_convert_fusion.1), channel_id=1, source_target_pairs={{2,0},{0,2},{3,1},{1,3},{6,4},{4,6},{7,5},{5,7},{10,8},{8,10},{11,... | collective-permute-start | bytes 602120 | tf_op jit(solution)/shard_map/ppermute | solution.py:40
  72.2 0.9 slice.38
  73.3 2.6 %collective-permute-done.17 = bf16[112,896]{1,0:T(8,128)(2,1)} collective-permute-done((bf16[112,896]{1,0:T(8,128)(2,1)}, bf16[112,896]{1,0:T(8,128)(2,1)}, u32[]{:S(2)}, u32[]{:S(2)}) %collective-permute-start.17) | collective-permute-done | bytes 200736 | tf_op jit(solution)/shard_map/ppermute | solution.py:40
  76.0 1.1 add_convert_fusion
  77.0 0.9 collective-permute-done.19
  78.1 2.7 %collective-permute-start.20 = (bf16[112,896]{1,0:T(8,128)(2,1)S(1)}, bf16[112,896]{1,0:T(8,128)(2,1)S(1)}, u32[]{:S(2)}, u32[]{:S(2)}) collective-permute-start(bf16[112,896]{1,0:T(8,128)(2,1)S(1)} %pad_maximum_fusion.2.refs_0_), channel_id=1, source_target_pairs={{4,0},{8,4},{12,8},{16,12},{20,16},{24,20},{28,24},{0,28},{5,1},{9... | collective-permute-start | bytes 602120 | tf_op jit(solution)/shard_map/ppermute | solution.py:40
  80.8 3.1 %collective-permute-done.23.refs_6_ = bf16[112,896]{1,0:T(8,128)(2,1)S(1)} collective-permute-done((bf16[112,896]{1,0:T(8,128)(2,1)S(1)}, bf16[112,896]{1,0:T(8,128)(2,1)S(1)}, u32[]{:S(2)}, u32[]{:S(2)}) %collective-permute-start.23) | collective-permute-done | bytes 200736 | tf_op jit(solution)/shard_map/ppermute | solution.py:40
  83.9 2.7 %collective-permute-start.21 = (bf16[112,896]{1,0:T(8,128)(2,1)S(1)}, bf16[112,896]{1,0:T(8,128)(2,1)S(1)}, u32[]{:S(2)}, u32[]{:S(2)}) collective-permute-start(bf16[112,896]{1,0:T(8,128)(2,1)S(1)} %collective-permute-done.20.refs_1_), channel_id=1, source_target_pairs={{4,0},{8,4},{12,8},{16,12},{20,16},{24,20},{28,24},{0,28},{5,1},{9... | collective-permute-start | bytes 602120 | tf_op jit(solution)/shard_map/ppermute | solution.py:40
  86.5 5.0 %collective-permute-done.24.refs_5_ = bf16[112,896]{1,0:T(8,128)(2,1)S(1)} collective-permute-done((bf16[112,896]{1,0:T(8,128)(2,1)S(1)}, bf16[112,896]{1,0:T(8,128)(2,1)S(1)}, u32[]{:S(2)}, u32[]{:S(2)}) %collective-permute-start.24) | collective-permute-done | bytes 200736 | tf_op jit(solution)/shard_map/ppermute | solution.py:40
  91.5 2.7 %collective-permute-start.22 = (bf16[112,896]{1,0:T(8,128)(2,1)S(1)}, bf16[112,896]{1,0:T(8,128)(2,1)S(1)}, u32[]{:S(2)}, u32[]{:S(2)}) collective-permute-start(bf16[112,896]{1,0:T(8,128)(2,1)S(1)} %collective-permute-done.21.refs_2_), channel_id=1, source_target_pairs={{4,0},{8,4},{12,8},{16,12},{20,16},{24,20},{28,24},{0,28},{5,1},{9... | collective-permute-start | bytes 602120 | tf_op jit(solution)/shard_map/ppermute | solution.py:40
  94.2 4.1 %collective-permute-done.25.refs_4_ = bf16[112,896]{1,0:T(8,128)(2,1)S(1)} collective-permute-done((bf16[112,896]{1,0:T(8,128)(2,1)S(1)}, bf16[112,896]{1,0:T(8,128)(2,1)S(1)}, u32[]{:S(2)}, u32[]{:S(2)}) %collective-permute-start.25) | collective-permute-done | bytes 200736 | tf_op jit(solution)/shard_map/ppermute | solution.py:40
  98.4 0.6 shard_map.22.group
  99.0 8.8 %collective-permute-start.26 = (bf16[7,112,896]{2,1,0:T(8,128)(2,1)S(1)}, bf16[7,112,896]{2,1,0:T(8,128)(2,1)S(1)}, u32[]{:S(2)}, u32[]{:S(2)}) collective-permute-start(bf16[7,112,896]{2,1,0:T(8,128)(2,1)S(1)} %shard_map.22.group), channel_id=1, source_target_pairs={{1,0},{0,1},{3,2},{2,3},{5,4},{4,5},{7,6},{6,7},{9,8},{8,9},{11,10... | collective-permute-start | bytes 4214792 | tf_op jit(solution)/shard_map/ppermute | solution.py:40
  107.8 0.5 collective-permute-start.6
  108.3 3.4 %collective-permute-start.3 = (bf16[504,512]{1,0:T(8,128)(2,1)S(1)}, bf16[504,512]{1,0:T(8,128)(2,1)S(1)}, u32[]{:S(2)}, u32[]{:S(2)}) collective-permute-start(bf16[504,512]{1,0:T(8,128)(2,1)S(1)} %copy-done.2), channel_id=1, source_target_pairs={{64,0},{128,64},{192,128},{0,192},{65,1},{129,65},{193,129},{1,193... | collective-permute-start | bytes 1548296 | tf_op jit(solution)/shard_map/ppermute | solution.py:40
  111.7 3.0 %collective-permute-start.27 = (bf16[56,896]{1,0:T(8,128)(2,1)S(1)}, bf16[56,896]{1,0:T(8,128)(2,1)S(1)}, u32[]{:S(2)}, u32[]{:S(2)}) collective-permute-start(bf16[56,896]{1,0:T(8,128)(2,1)S(1)} %slice.39), channel_id=1, source_target_pairs={{4,0},{8,4},{12,8},{16,12},{20,16},{24,20},{28,24},{0,28},{5,1},{9... | collective-permute-start | bytes 301064 | tf_op jit(solution)/shard_map/ppermute | solution.py:40
  114.7 1.6 collective-permute-done.27
  116.4 5.6 %collective-permute-done.28 = bf16[56,896]{1,0:T(8,128)(2,1)S(1)} collective-permute-done((bf16[56,896]{1,0:T(8,128)(2,1)S(1)}, bf16[56,896]{1,0:T(8,128)(2,1)S(1)}, u32[]{:S(2)}, u32[]{:S(2)}) %collective-permute-start.28) | collective-permute-done | bytes 100384 | tf_op jit(solution)/shard_map/ppermute | solution.py:40
  122.0 2.2 %collective-permute-start.29 = (bf16[112,896]{1,0:T(8,128)(2,1)S(1)}, bf16[112,896]{1,0:T(8,128)(2,1)S(1)}, u32[]{:S(2)}, u32[]{:S(2)}) collective-permute-start(bf16[112,896]{1,0:T(8,128)(2,1)S(1)} %constant_dynamic-update-slice_fusion.mine), channel_id=1, source_target_pairs={{1,0},{0,1},{3,2},{2,3},{5,4},{4,5},{7,6},{6,7},{9,8},{8,9},{11,10... | collective-permute-start | bytes 602120 | tf_op jit(solution)/shard_map/ppermute | solution.py:40
  124.2 1.2 shard_map.19.panel
  125.5 2.5 %shard_map.23 = (bf16[4,448,896]{2,1,0:T(8,128)(2,1)S(1)}, f32[448,576]{1,0:T(8,128)S(1)}) custom-call(s32[2]{0:T(128)S(1)} %pad_add_fusion.place, bf16[4,896,576]{2,1,0:T(8,128)(2,1)S(1)} %shard_map.19.panel, bf16[7,112,896]{2,1,0:T(8,128)(2,1)S(1)} %shard_map.22.group), custom_call_target="tpu_custom_call" | custom-call | flops 924844032 | bytes 9261056 | tf_op jit(solution)/shard_map/pallas_call | solution.py:62
  128.0 2.4 %shard_map.24 = (bf16[4,448,896]{2,1,0:T(8,128)(2,1)S(1)}, f32[448,576]{1,0:T(8,128)S(1)}) custom-call(s32[2]{0:T(128)S(1)} %pad_add_fusion.place, bf16[4,896,576]{2,1,0:T(8,128)(2,1)S(1)} %shard_map.19.panel, bf16[7,112,896]{2,1,0:T(8,128)(2,1)S(1)} %collective-permute-done.26.group, ...), custom_call_target="tpu_custom_call", output_to_operand_aliasing={{0}: (3, {}), {1}: (4, {})} | custom-call | flops 924844032 | bytes 12988416 | tf_op jit(solution)/shard_map/pallas_call | solution.py:62
  130.4 2.5 %shard_map.25 = (bf16[4,448,896]{2,1,0:T(8,128)(2,1)S(1)}, bf16[504,512]{1,0:T(8,128)(2,1)S(1)}, bf16[448,576]{1,0:T(8,128)(2,1)S(1)}) custom-call(s32[2]{0:T(128)S(1)} %pad_add_fusion.place, bf16[448,576]{1,0:T(8,128)(2,1)S(1)} %get-tuple-element.35.own, bf16[4,896,576]{2,1,0:T(8,128)(2,1)S(1)} %shard_map.19.panel, ...), custom_call_target="tpu_custom_call", output_to_operand_aliasing={{0}: (3, {})} | custom-call | flops 231211008 | bytes 13017088 | tf_op jit(solution)/shard_map/pallas_call | solution.py:62
  132.9 1.1 collective-permute-start.32
  134.0 2.7 %collective-permute-start.30 = (bf16[504,512]{1,0:T(8,128)(2,1)S(1)}, bf16[504,512]{1,0:T(8,128)(2,1)S(1)}, u32[]{:S(2)}, u32[]{:S(2)}) collective-permute-start(bf16[504,512]{1,0:T(8,128)(2,1)S(1)} %get-tuple-element.61.refs_0_), channel_id=1, source_target_pairs={{64,0},{128,64},{192,128},{0,192},{65,1},{129,65},{193,129},{1,193... | collective-permute-start | bytes 1548296 | tf_op jit(solution)/shard_map/ppermute | solution.py:40
  136.6 0.2 collective-permute-start.33
  136.9 9.2 %collective-permute-done.32.refs_3_ = bf16[504,512]{1,0:T(8,128)(2,1)S(1)} collective-permute-done((bf16[504,512]{1,0:T(8,128)(2,1)S(1)}, bf16[504,512]{1,0:T(8,128)(2,1)S(1)}, u32[]{:S(2)}, u32[]{:S(2)}) %collective-permute-start.32) | collective-permute-done | bytes 516128 | tf_op jit(solution)/shard_map/ppermute | solution.py:40
  146.1 2.6 %collective-permute-done.31.refs_2_ = bf16[504,512]{1,0:T(8,128)(2,1)S(1)} collective-permute-done((bf16[504,512]{1,0:T(8,128)(2,1)S(1)}, bf16[504,512]{1,0:T(8,128)(2,1)S(1)}, u32[]{:S(2)}, u32[]{:S(2)}) %collective-permute-start.31) | collective-permute-done | bytes 516128 | tf_op jit(solution)/shard_map/ppermute | solution.py:40
  148.7 0.1 collective-permute-done.30.refs_1_
  148.9 9.5 %collective-permute-done.33.block = bf16[504,512]{1,0:T(8,128)(2,1)S(1)} collective-permute-done((bf16[504,512]{1,0:T(8,128)(2,1)S(1)}, bf16[504,512]{1,0:T(8,128)(2,1)S(1)}, u32[]{:S(2)}, u32[]{:S(2)}) %collective-permute-start.33) | collective-permute-done | bytes 516128 | tf_op jit(solution)/shard_map/ppermute | solution.py:40
  158.4 0.5 collective-permute-start.36
  158.9 0.6 collective-permute-start.35
  159.5 2.5 %collective-permute-start.34 = (bf16[504,512]{1,0:T(8,128)(2,1)S(1)}, bf16[504,512]{1,0:T(8,128)(2,1)S(1)}, u32[]{:S(2)}, u32[]{:S(2)}) collective-permute-start(bf16[504,512]{1,0:T(8,128)(2,1)S(1)} %collective-permute-done.32.refs_3_), channel_id=1, source_target_pairs={{64,0},{128,64},{192,128},{0,192},{65,1},{129,65},{193,129},{1,193... | collective-permute-start | bytes 1548296 | tf_op jit(solution)/shard_map/ppermute | solution.py:40
  162.0 3.0 %shard_map.26.before = f32[448,576]{1,0:T(8,128)S(1)} custom-call(s32[2]{0:T(128)S(1)} %pad_add_fusion.place, bf16[448,576]{1,0:T(8,128)(2,1)S(1)} %get-tuple-element.35.own, bf16[448,576]{1,0:T(8,128)(2,1)S(1)} %get-tuple-element.59.w_low, bf16[4,448,896]{2,1,0:T(8,128)(2,1)S(1)} %get-tuple-element.60.gram, bf16[504,512]{1,0:T(8,128)(2,1)S(1)} %get-tuple-element.61.refs_0_, ...), custom_call_target="tpu_custom_call" | custom-call | flops 1156055040 | bytes 6823936 | tf_op jit(solution)/shard_map/pallas_call | solution.py:62
  165.0 1.1 shard_map.27.before
  166.1 3.4 %collective-permute-done.36.r21 = bf16[504,512]{1,0:T(8,128)(2,1)S(1)} collective-permute-done((bf16[504,512]{1,0:T(8,128)(2,1)S(1)}, bf16[504,512]{1,0:T(8,128)(2,1)S(1)}, u32[]{:S(2)}, u32[]{:S(2)}) %collective-permute-start.36) | collective-permute-done | bytes 516128 | tf_op jit(solution)/shard_map/ppermute | solution.py:40
  169.5 2.2 %collective-permute-done.35.r31 = bf16[504,512]{1,0:T(8,128)(2,1)S(1)} collective-permute-done((bf16[504,512]{1,0:T(8,128)(2,1)S(1)}, bf16[504,512]{1,0:T(8,128)(2,1)S(1)}, u32[]{:S(2)}, u32[]{:S(2)}) %collective-permute-start.35) | collective-permute-done | bytes 516128 | tf_op jit(solution)/shard_map/ppermute | solution.py:40
  171.7 2.6 %shard_map.28 = bf16[448,576]{1,0:T(8,128)(2,1)} custom-call(s32[2]{0:T(128)S(1)} %pad_add_fusion.place, f32[448,576]{1,0:T(8,128)S(1)} %shard_map.27.before, bf16[4,448,896]{2,1,0:T(8,128)(2,1)S(1)} %get-tuple-element.60.gram, bf16[504,512]{1,0:T(8,128)(2,1)S(1)} %collective-permute-done.34.r11, bf16[504,512]{1,0:T(8,128)(2,1)S(1)} %collective-permute-done.35.r31, ...), custom_call_target="tpu_custom_call" | custom-call | flops 693633024 | bytes 5791744 | tf_op jit(solution)/shard_map/pallas_call | solution.py:62
  (49 shorter events, 1.1 us)
Async XLA Ops:
  0.1 1.1 copy-start
  1.8 12.5 %collective-permute-start.2 = (bf16[504,512]{1,0:T(8,128)(2,1)S(1)}, bf16[504,512]{1,0:T(8,128)(2,1)S(1)}, u32[]{:S(2)}, u32[]{:S(2)}) collective-permute-start(bf16[504,512]{1,0:T(8,128)(2,1)S(1)} %get-tuple-element.36.refs_0_), channel_id=1, source_target_pairs={{32,0},{0,32},{33,1},{1,33},{34,2},{2,34},{35,3},{3,35},{36,4},{4,... | collective-permute-start | bytes 1548296 | tf_op jit(solution)/shard_map/ppermute | solution.py:40
  4.0 13.3 %collective-permute-start.1 = (bf16[504,512]{1,0:T(8,128)(2,1)S(1)}, bf16[504,512]{1,0:T(8,128)(2,1)S(1)}, u32[]{:S(2)}, u32[]{:S(2)}) collective-permute-start(bf16[504,512]{1,0:T(8,128)(2,1)S(1)} %get-tuple-element.36.refs_0_), channel_id=1, source_target_pairs={{192,0},{0,64},{64,128},{128,192},{193,1},{1,65},{65,129},{129,193... | collective-permute-start | bytes 1548296 | tf_op jit(solution)/shard_map/ppermute | solution.py:40
  5.2 12.1 %collective-permute-start = (bf16[504,512]{1,0:T(8,128)(2,1)S(1)}, bf16[504,512]{1,0:T(8,128)(2,1)S(1)}, u32[]{:S(2)}, u32[]{:S(2)}) collective-permute-start(bf16[504,512]{1,0:T(8,128)(2,1)S(1)} %get-tuple-element.36.refs_0_), channel_id=1, source_target_pairs={{64,0},{128,64},{192,128},{0,192},{65,1},{129,65},{193,129},{1,193... | collective-permute-start | bytes 1548296 | tf_op jit(solution)/shard_map/ppermute | solution.py:40
  6.7 26.8 %collective-permute-start.5 = (bf16[504,512]{1,0:T(8,128)(2,1)S(1)}, bf16[504,512]{1,0:T(8,128)(2,1)S(1)}, u32[]{:S(2)}, u32[]{:S(2)}) collective-permute-start(bf16[504,512]{1,0:T(8,128)(2,1)S(1)} %get-tuple-element.36.refs_0_), channel_id=1, source_target_pairs={{128,0},{192,64},{0,128},{64,192},{129,1},{193,65},{1,129},{65,193... | collective-permute-start | bytes 1548296 | tf_op jit(solution)/shard_map/ppermute | solution.py:40
  14.3 6.7 %copy-start.1 = (bf16[504,512]{1,0:T(8,128)(2,1)}, bf16[504,512]{1,0:T(8,128)(2,1)S(1)}, u32[]{:S(2)}) copy-start(bf16[504,512]{1,0:T(8,128)(2,1)S(1)} %collective-permute-done.2.refs_3_) | copy-start | bytes 1548292
  21.0 14.5 %collective-permute-start.7 = (bf16[8,56,896]{2,1,0:T(8,128)(2,1)S(1)}, bf16[8,56,896]{2,1,0:T(8,128)(2,1)S(1)}, u32[]{:S(2)}, u32[]{:S(2)}) collective-permute-start(bf16[8,56,896]{2,1,0:T(8,128)(2,1)S(1)} %get-tuple-element.42), channel_id=1, source_target_pairs={{1,0},{0,1},{3,2},{2,3},{5,4},{4,5},{7,6},{6,7},{9,8},{8,9},{11,10... | collective-permute-start | bytes 2408456 | tf_op jit(solution)/shard_map/ppermute | solution.py:40
  35.3 2.4 %collective-permute-start.8 = (bf16[8,56,896]{2,1,0:T(8,128)(2,1)S(1)}, bf16[8,56,896]{2,1,0:T(8,128)(2,1)S(1)}, u32[]{:S(2)}, u32[]{:S(2)}) collective-permute-start(bf16[8,56,896]{2,1,0:T(8,128)(2,1)S(1)} %get-tuple-element.45), channel_id=1, source_target_pairs={{1,0},{0,1},{3,2},{2,3},{5,4},{4,5},{7,6},{6,7},{9,8},{8,9},{11,10... | collective-permute-start | bytes 2408456 | tf_op jit(solution)/shard_map/ppermute | solution.py:40
  38.7 7.7 %collective-permute-start.13 = (bf16[56,896]{1,0:T(8,128)(2,1)S(1)}, bf16[56,896]{1,0:T(8,128)(2,1)S(1)}, u32[]{:S(2)}, u32[]{:S(2)}) collective-permute-start(bf16[56,896]{1,0:T(8,128)(2,1)S(1)} %get-tuple-element.54), channel_id=1, source_target_pairs={{4,0},{8,4},{12,8},{16,12},{20,16},{24,20},{28,24},{0,28},{5,1},{9... | collective-permute-start | bytes 301064 | tf_op jit(solution)/shard_map/ppermute | solution.py:40
  44.3 5.6 %collective-permute-start.9 = (bf16[56,896]{1,0:T(8,128)(2,1)S(1)}, bf16[56,896]{1,0:T(8,128)(2,1)S(1)}, u32[]{:S(2)}, u32[]{:S(2)}) collective-permute-start(bf16[56,896]{1,0:T(8,128)(2,1)S(1)} %get-tuple-element.50), channel_id=1, source_target_pairs={{28,0},{0,4},{4,8},{8,12},{12,16},{16,20},{20,24},{24,28},{29,1},{... | collective-permute-start | bytes 301064 | tf_op jit(solution)/shard_map/ppermute | solution.py:40
  46.4 6.8 %collective-permute-start.14 = (bf16[112,896]{1,0:T(8,128)(2,1)S(1)}, bf16[112,896]{1,0:T(8,128)(2,1)S(1)}, u32[]{:S(2)}, u32[]{:S(2)}) collective-permute-start(bf16[112,896]{1,0:T(8,128)(2,1)S(1)} %pad_maximum_fusion.1), channel_id=1, source_target_pairs={{4,0},{8,4},{12,8},{16,12},{20,16},{24,20},{28,24},{0,28},{5,1},{9... | collective-permute-start | bytes 602120 | tf_op jit(solution)/shard_map/ppermute | solution.py:40
  50.0 6.8 %collective-permute-start.10 = (bf16[112,896]{1,0:T(8,128)(2,1)S(1)}, bf16[112,896]{1,0:T(8,128)(2,1)S(1)}, u32[]{:S(2)}, u32[]{:S(2)}) collective-permute-start(bf16[112,896]{1,0:T(8,128)(2,1)S(1)} %pad_maximum_fusion), channel_id=1, source_target_pairs={{28,0},{0,4},{4,8},{8,12},{12,16},{16,20},{20,24},{24,28},{29,1},{... | collective-permute-start | bytes 602120 | tf_op jit(solution)/shard_map/ppermute | solution.py:40
  53.3 6.1 %collective-permute-start.15 = (bf16[112,896]{1,0:T(8,128)(2,1)S(1)}, bf16[112,896]{1,0:T(8,128)(2,1)S(1)}, u32[]{:S(2)}, u32[]{:S(2)}) collective-permute-start(bf16[112,896]{1,0:T(8,128)(2,1)S(1)} %add_convert_fusion.3), channel_id=1, source_target_pairs={{4,0},{8,4},{12,8},{16,12},{20,16},{24,20},{28,24},{0,28},{5,1},{9... | collective-permute-start | bytes 602120 | tf_op jit(solution)/shard_map/ppermute | solution.py:40
  56.9 6.0 %collective-permute-start.11 = (bf16[112,896]{1,0:T(8,128)(2,1)S(1)}, bf16[112,896]{1,0:T(8,128)(2,1)S(1)}, u32[]{:S(2)}, u32[]{:S(2)}) collective-permute-start(bf16[112,896]{1,0:T(8,128)(2,1)S(1)} %add_convert_fusion.5), channel_id=1, source_target_pairs={{28,0},{0,4},{4,8},{8,12},{12,16},{16,20},{20,24},{24,28},{29,1},{... | collective-permute-start | bytes 602120 | tf_op jit(solution)/shard_map/ppermute | solution.py:40
  59.5 5.9 %collective-permute-start.16 = (bf16[112,896]{1,0:T(8,128)(2,1)S(1)}, bf16[112,896]{1,0:T(8,128)(2,1)S(1)}, u32[]{:S(2)}, u32[]{:S(2)}) collective-permute-start(bf16[112,896]{1,0:T(8,128)(2,1)S(1)} %add_convert_fusion.2), channel_id=1, source_target_pairs={{4,0},{8,4},{12,8},{16,12},{20,16},{24,20},{28,24},{0,28},{5,1},{9... | collective-permute-start | bytes 602120 | tf_op jit(solution)/shard_map/ppermute | solution.py:40
  63.0 5.9 %collective-permute-start.12 = (bf16[112,896]{1,0:T(8,128)(2,1)S(1)}, bf16[112,896]{1,0:T(8,128)(2,1)S(1)}, u32[]{:S(2)}, u32[]{:S(2)}) collective-permute-start(bf16[112,896]{1,0:T(8,128)(2,1)S(1)} %add_convert_fusion.4), channel_id=1, source_target_pairs={{28,0},{0,4},{4,8},{8,12},{12,16},{16,20},{20,24},{24,28},{29,1},{... | collective-permute-start | bytes 602120 | tf_op jit(solution)/shard_map/ppermute | solution.py:40
  69.6 6.4 %collective-permute-start.17 = (bf16[112,896]{1,0:T(8,128)(2,1)}, bf16[112,896]{1,0:T(8,128)(2,1)}, u32[]{:S(2)}, u32[]{:S(2)}) collective-permute-start(bf16[112,896]{1,0:T(8,128)(2,1)} %add_convert_fusion.1), channel_id=1, source_target_pairs={{2,0},{0,2},{3,1},{1,3},{6,4},{4,6},{7,5},{5,7},{10,8},{8,10},{11,... | collective-permute-start | bytes 602120 | tf_op jit(solution)/shard_map/ppermute | solution.py:40
  73.1 4.8 %collective-permute-start.19 = (bf16[56,896]{1,0:T(8,128)(2,1)S(1)}, bf16[56,896]{1,0:T(8,128)(2,1)S(1)}, u32[]{:S(2)}, u32[]{:S(2)}) collective-permute-start(bf16[56,896]{1,0:T(8,128)(2,1)S(1)} %slice.38), channel_id=1, source_target_pairs={{34,0},{32,2},{2,32},{0,34},{35,1},{33,3},{3,33},{1,35},{38,4},{36... | collective-permute-start | bytes 301064 | tf_op jit(solution)/shard_map/ppermute | solution.py:53
  73.2 4.7 %collective-permute-start.18 = (bf16[56,896]{1,0:T(8,128)(2,1)S(1)}, bf16[56,896]{1,0:T(8,128)(2,1)S(1)}, u32[]{:S(2)}, u32[]{:S(2)}) collective-permute-start(bf16[56,896]{1,0:T(8,128)(2,1)S(1)} %slice.38), channel_id=1, source_target_pairs={{32,0},{0,32},{33,1},{1,33},{34,2},{2,34},{35,3},{3,35},{36,4},{4,... | collective-permute-start | bytes 301064 | tf_op jit(solution)/shard_map/ppermute | solution.py:40
  78.0 30.3 %copy-start.2 = (bf16[504,512]{1,0:T(8,128)(2,1)S(1)}, bf16[504,512]{1,0:T(8,128)(2,1)}, u32[]{:S(2)}) copy-start(bf16[504,512]{1,0:T(8,128)(2,1)} %copy-done.1) | copy-start | bytes 1548292
  78.0 5.9 %collective-permute-start.23 = (bf16[112,896]{1,0:T(8,128)(2,1)S(1)}, bf16[112,896]{1,0:T(8,128)(2,1)S(1)}, u32[]{:S(2)}, u32[]{:S(2)}) collective-permute-start(bf16[112,896]{1,0:T(8,128)(2,1)S(1)} %pad_maximum_fusion.2.refs_0_), channel_id=1, source_target_pairs={{28,0},{0,4},{4,8},{8,12},{12,16},{16,20},{20,24},{24,28},{29,1},{... | collective-permute-start | bytes 602120 | tf_op jit(solution)/shard_map/ppermute | solution.py:40
  78.1 5.8 %collective-permute-start.20 = (bf16[112,896]{1,0:T(8,128)(2,1)S(1)}, bf16[112,896]{1,0:T(8,128)(2,1)S(1)}, u32[]{:S(2)}, u32[]{:S(2)}) collective-permute-start(bf16[112,896]{1,0:T(8,128)(2,1)S(1)} %pad_maximum_fusion.2.refs_0_), channel_id=1, source_target_pairs={{4,0},{8,4},{12,8},{16,12},{20,16},{24,20},{28,24},{0,28},{5,1},{9... | collective-permute-start | bytes 602120 | tf_op jit(solution)/shard_map/ppermute | solution.py:40
  83.9 7.7 %collective-permute-start.24 = (bf16[112,896]{1,0:T(8,128)(2,1)S(1)}, bf16[112,896]{1,0:T(8,128)(2,1)S(1)}, u32[]{:S(2)}, u32[]{:S(2)}) collective-permute-start(bf16[112,896]{1,0:T(8,128)(2,1)S(1)} %collective-permute-done.23.refs_6_), channel_id=1, source_target_pairs={{28,0},{0,4},{4,8},{8,12},{12,16},{16,20},{20,24},{24,28},{29,1},{... | collective-permute-start | bytes 602120 | tf_op jit(solution)/shard_map/ppermute | solution.py:40
  83.9 7.7 %collective-permute-start.21 = (bf16[112,896]{1,0:T(8,128)(2,1)S(1)}, bf16[112,896]{1,0:T(8,128)(2,1)S(1)}, u32[]{:S(2)}, u32[]{:S(2)}) collective-permute-start(bf16[112,896]{1,0:T(8,128)(2,1)S(1)} %collective-permute-done.20.refs_1_), channel_id=1, source_target_pairs={{4,0},{8,4},{12,8},{16,12},{20,16},{24,20},{28,24},{0,28},{5,1},{9... | collective-permute-start | bytes 602120 | tf_op jit(solution)/shard_map/ppermute | solution.py:40
  91.5 6.8 %collective-permute-start.25 = (bf16[112,896]{1,0:T(8,128)(2,1)S(1)}, bf16[112,896]{1,0:T(8,128)(2,1)S(1)}, u32[]{:S(2)}, u32[]{:S(2)}) collective-permute-start(bf16[112,896]{1,0:T(8,128)(2,1)S(1)} %collective-permute-done.24.refs_5_), channel_id=1, source_target_pairs={{28,0},{0,4},{4,8},{8,12},{12,16},{16,20},{20,24},{24,28},{29,1},{... | collective-permute-start | bytes 602120 | tf_op jit(solution)/shard_map/ppermute | solution.py:40
  91.5 6.8 %collective-permute-start.22 = (bf16[112,896]{1,0:T(8,128)(2,1)S(1)}, bf16[112,896]{1,0:T(8,128)(2,1)S(1)}, u32[]{:S(2)}, u32[]{:S(2)}) collective-permute-start(bf16[112,896]{1,0:T(8,128)(2,1)S(1)} %collective-permute-done.21.refs_2_), channel_id=1, source_target_pairs={{4,0},{8,4},{12,8},{16,12},{20,16},{24,20},{28,24},{0,28},{5,1},{9... | collective-permute-start | bytes 602120 | tf_op jit(solution)/shard_map/ppermute | solution.py:40
  99.0 28.9 %collective-permute-start.26 = (bf16[7,112,896]{2,1,0:T(8,128)(2,1)S(1)}, bf16[7,112,896]{2,1,0:T(8,128)(2,1)S(1)}, u32[]{:S(2)}, u32[]{:S(2)}) collective-permute-start(bf16[7,112,896]{2,1,0:T(8,128)(2,1)S(1)} %shard_map.22.group), channel_id=1, source_target_pairs={{1,0},{0,1},{3,2},{2,3},{5,4},{4,5},{7,6},{6,7},{9,8},{8,9},{11,10... | collective-permute-start | bytes 4214792 | tf_op jit(solution)/shard_map/ppermute | solution.py:40
  107.8 16.4 %collective-permute-start.6 = (bf16[504,512]{1,0:T(8,128)(2,1)S(1)}, bf16[504,512]{1,0:T(8,128)(2,1)S(1)}, u32[]{:S(2)}, u32[]{:S(2)}) collective-permute-start(bf16[504,512]{1,0:T(8,128)(2,1)S(1)} %collective-permute-done.5.refs_3_.block), channel_id=1, source_target_pairs={{32,0},{0,32},{33,1},{1,33},{34,2},{2,34},{35,3},{3,35},{36,4},{4,... | collective-permute-start | bytes 1548296 | tf_op jit(solution)/shard_map/ppermute | solution.py:40
  108.3 16.0 %collective-permute-start.4 = (bf16[504,512]{1,0:T(8,128)(2,1)S(1)}, bf16[504,512]{1,0:T(8,128)(2,1)S(1)}, u32[]{:S(2)}, u32[]{:S(2)}) collective-permute-start(bf16[504,512]{1,0:T(8,128)(2,1)S(1)} %copy-done.2), channel_id=1, source_target_pairs={{192,0},{0,64},{64,128},{128,192},{193,1},{1,65},{65,129},{129,193... | collective-permute-start | bytes 1548296 | tf_op jit(solution)/shard_map/ppermute | solution.py:40
  108.3 16.0 %collective-permute-start.3 = (bf16[504,512]{1,0:T(8,128)(2,1)S(1)}, bf16[504,512]{1,0:T(8,128)(2,1)S(1)}, u32[]{:S(2)}, u32[]{:S(2)}) collective-permute-start(bf16[504,512]{1,0:T(8,128)(2,1)S(1)} %copy-done.2), channel_id=1, source_target_pairs={{64,0},{128,64},{192,128},{0,192},{65,1},{129,65},{193,129},{1,193... | collective-permute-start | bytes 1548296 | tf_op jit(solution)/shard_map/ppermute | solution.py:40
  111.7 4.7 %collective-permute-start.27 = (bf16[56,896]{1,0:T(8,128)(2,1)S(1)}, bf16[56,896]{1,0:T(8,128)(2,1)S(1)}, u32[]{:S(2)}, u32[]{:S(2)}) collective-permute-start(bf16[56,896]{1,0:T(8,128)(2,1)S(1)} %slice.39), channel_id=1, source_target_pairs={{4,0},{8,4},{12,8},{16,12},{20,16},{24,20},{28,24},{0,28},{5,1},{9... | collective-permute-start | bytes 301064 | tf_op jit(solution)/shard_map/ppermute | solution.py:40
  116.4 5.7 %collective-permute-start.28 = (bf16[56,896]{1,0:T(8,128)(2,1)S(1)}, bf16[56,896]{1,0:T(8,128)(2,1)S(1)}, u32[]{:S(2)}, u32[]{:S(2)}) collective-permute-start(bf16[56,896]{1,0:T(8,128)(2,1)S(1)} %slice.40), channel_id=1, source_target_pairs={{28,0},{0,4},{4,8},{8,12},{12,16},{16,20},{20,24},{24,28},{29,1},{... | collective-permute-start | bytes 301064 | tf_op jit(solution)/shard_map/ppermute | solution.py:40
  122.0 8.3 %collective-permute-start.29 = (bf16[112,896]{1,0:T(8,128)(2,1)S(1)}, bf16[112,896]{1,0:T(8,128)(2,1)S(1)}, u32[]{:S(2)}, u32[]{:S(2)}) collective-permute-start(bf16[112,896]{1,0:T(8,128)(2,1)S(1)} %constant_dynamic-update-slice_fusion.mine), channel_id=1, source_target_pairs={{1,0},{0,1},{3,2},{2,3},{5,4},{4,5},{7,6},{6,7},{9,8},{8,9},{11,10... | collective-permute-start | bytes 602120 | tf_op jit(solution)/shard_map/ppermute | solution.py:40
  132.9 13.3 %collective-permute-start.32 = (bf16[504,512]{1,0:T(8,128)(2,1)S(1)}, bf16[504,512]{1,0:T(8,128)(2,1)S(1)}, u32[]{:S(2)}, u32[]{:S(2)}) collective-permute-start(bf16[504,512]{1,0:T(8,128)(2,1)S(1)} %get-tuple-element.61.refs_0_), channel_id=1, source_target_pairs={{32,0},{0,32},{33,1},{1,33},{34,2},{2,34},{35,3},{3,35},{36,4},{4,... | collective-permute-start | bytes 1548296 | tf_op jit(solution)/shard_map/ppermute | solution.py:40
  134.0 14.8 %collective-permute-start.31 = (bf16[504,512]{1,0:T(8,128)(2,1)S(1)}, bf16[504,512]{1,0:T(8,128)(2,1)S(1)}, u32[]{:S(2)}, u32[]{:S(2)}) collective-permute-start(bf16[504,512]{1,0:T(8,128)(2,1)S(1)} %get-tuple-element.61.refs_0_), channel_id=1, source_target_pairs={{192,0},{0,64},{64,128},{128,192},{193,1},{1,65},{65,129},{129,193... | collective-permute-start | bytes 1548296 | tf_op jit(solution)/shard_map/ppermute | solution.py:40
  134.0 14.9 %collective-permute-start.30 = (bf16[504,512]{1,0:T(8,128)(2,1)S(1)}, bf16[504,512]{1,0:T(8,128)(2,1)S(1)}, u32[]{:S(2)}, u32[]{:S(2)}) collective-permute-start(bf16[504,512]{1,0:T(8,128)(2,1)S(1)} %get-tuple-element.61.refs_0_), channel_id=1, source_target_pairs={{64,0},{128,64},{192,128},{0,192},{65,1},{129,65},{193,129},{1,193... | collective-permute-start | bytes 1548296 | tf_op jit(solution)/shard_map/ppermute | solution.py:40
  136.6 21.8 %collective-permute-start.33 = (bf16[504,512]{1,0:T(8,128)(2,1)S(1)}, bf16[504,512]{1,0:T(8,128)(2,1)S(1)}, u32[]{:S(2)}, u32[]{:S(2)}) collective-permute-start(bf16[504,512]{1,0:T(8,128)(2,1)S(1)} %get-tuple-element.61.refs_0_), channel_id=1, source_target_pairs={{128,0},{192,64},{0,128},{64,192},{129,1},{193,65},{1,129},{65,193... | collective-permute-start | bytes 1548296 | tf_op jit(solution)/shard_map/ppermute | solution.py:40
  158.4 11.1 %collective-permute-start.36 = (bf16[504,512]{1,0:T(8,128)(2,1)S(1)}, bf16[504,512]{1,0:T(8,128)(2,1)S(1)}, u32[]{:S(2)}, u32[]{:S(2)}) collective-permute-start(bf16[504,512]{1,0:T(8,128)(2,1)S(1)} %collective-permute-done.33.block), channel_id=1, source_target_pairs={{32,0},{0,32},{33,1},{1,33},{34,2},{2,34},{35,3},{3,35},{36,4},{4,... | collective-permute-start | bytes 1548296 | tf_op jit(solution)/shard_map/ppermute | solution.py:40
  158.9 12.9 %collective-permute-start.35 = (bf16[504,512]{1,0:T(8,128)(2,1)S(1)}, bf16[504,512]{1,0:T(8,128)(2,1)S(1)}, u32[]{:S(2)}, u32[]{:S(2)}) collective-permute-start(bf16[504,512]{1,0:T(8,128)(2,1)S(1)} %collective-permute-done.32.refs_3_), channel_id=1, source_target_pairs={{192,0},{0,64},{64,128},{128,192},{193,1},{1,65},{65,129},{129,193... | collective-permute-start | bytes 1548296 | tf_op jit(solution)/shard_map/ppermute | solution.py:40
  159.5 12.3 %collective-permute-start.34 = (bf16[504,512]{1,0:T(8,128)(2,1)S(1)}, bf16[504,512]{1,0:T(8,128)(2,1)S(1)}, u32[]{:S(2)}, u32[]{:S(2)}) collective-permute-start(bf16[504,512]{1,0:T(8,128)(2,1)S(1)} %collective-permute-done.32.refs_3_), channel_id=1, source_target_pairs={{64,0},{128,64},{192,128},{0,192},{65,1},{129,65},{193,129},{1,193... | collective-permute-start | bytes 1548296 | tf_op jit(solution)/shard_map/ppermute | solution.py:40

commit v3 on v2

--- a/solution.py
+++ b/solution.py
@@ -77,10 +77,10 @@
     return lax.optimization_barrier(near), shift(own, "x", 2)
 
 
-def more_blocks(near, r20):
-    _, _, r01 = near
-    r11 = shift(r01, "x", 1)
-    r31 = shift(r01, "x", -1)
+def more_blocks(near, r20, spare):
+    r10, r30, r01 = near
+    r11 = shift(r10, "yl", 1) if spare else shift(r01, "x", 1)
+    r31 = shift(r30, "yl", 1) if spare else shift(r01, "x", -1)
     r21 = shift(r20, "yl", 1)
     return r11, r31, r21
 
@@ -280,11 +280,15 @@
     total[...] = before[...] + jnp.dot(gram[3][:, rows:], panel[0, :rows], preferred_element_type=F32)
 
 
-def far_body(place, before, gram, r11, r31, r21, out, panel):
+def mid_body(place, before, gram, r11, r31, total, panel):
+    fill(panel, (r11, r31))
+    total[...] = before[...] + jnp.dot(gram[2], panel[0], preferred_element_type=F32)
+
+
+def far_body(place, before, gram, r21, out, panel):
     rows, cols = out.shape
-    fill(panel, (r11, r31, r21))
-    acc = before[...] + jnp.dot(gram[2], panel[0], preferred_element_type=F32)
-    acc += jnp.dot(gram[3][:, :rows], panel[1, :rows], preferred_element_type=F32)
+    fill(panel, [r21])
+    acc = before[...] + jnp.dot(gram[3][:, :rows], panel[0, :rows], preferred_element_type=F32)
     factor = 0.2 * math.sqrt(max(rows * PANEL, cols * math.prod(SIZES[n] for n in COL)))
     out[...] = (acc * factor).astype(BF16)
 
@@ -319,7 +323,7 @@
     halves = [keep, shift(send, "c", 1)]
     keep, send = call(late_body, place, (own, low, partner, r20), [part, part], work, [pairs, room(1)])
     halves += [keep, shift(send, "c", 1)]
-    r11, r31, r21 = more_blocks(near, r20)
+    r11, r31, r21 = more_blocks(near, r20, True)
     panel = call(panel_body, place, (low, r11, r31, r21, r20), array((4, 2 * rows, cols)), 0, [room(2)])
     one, two = array((size, 2 * rows)), array((2 * size, 2 * rows))
     parts = call(pair_body, place, halves, [two] * FAR + [one] * 2 + [two] * (FAR - 1))
@@ -360,10 +364,12 @@
     )
 
     near, r20 = first_blocks(w_high)
+    ends = more_blocks(near, r20, False)
     total = call(near_body, place, (own, w_low, gram, w_high, *near), sums, 5 * work // 2, [room(2)])
-    ends = more_blocks(near, r20)
     total = call(side_body, place, (total, gram, r20), sums, work // 2, [room(1)])
-    return call(far_body, place, (total, gram, *ends), block, 3 * work // 2, [room(2)], home=True)
+    r11, r31, r21 = ends
+    total = call(mid_body, place, (total, gram, r11, r31), sums, work, [room(1)])
+    return call(far_body, place, (total, gram, r21), block, work // 2, [room(1)], home=True)
 
 
 def solution(mesh):

time: 176 us -> 195 us (1.11)
  waiting for transfers between devices: 75 us -> 92.1 us
    ppermute x36, waiting for transfers between devices: 74.2 us -> 91.2 us  [shift(): lax.ppermute(value, axis, [((i + step) % size, i) for i in range(size)])]
    pallas_call x12 -> x13, Pallas kernels: 23 us -> 23.7 us  [call(): pl.pallas_call(body, out_shape=outs if home else [pltpu.VMEM(o.shape, o.d...]
where the time goes in v3:
time: 195 us; the launch traced here: 193 us
  waiting for transfers between devices  92.1 us (47%)
  starting transfers between devices  72.9 us (37%)
  Pallas kernels  23.7 us (12%)
  other arithmetic  2.3 us (1%)
  local copies, waits for them, and re-layouts  2.07 us (1%)
    ppermute x36, waiting for transfers between devices, shift(): lax.ppermute(value, axis, [((i + step) % size, i) for i in range(size)])  91.2 us
    ppermute x36, starting transfers between devices, shift(): lax.ppermute(value, axis, [((i + step) % size, i) for i in range(size)])  72.8 us
    pallas_call x13, Pallas kernels, call(): pl.pallas_call(body, out_shape=outs if home else [pltpu.VMEM(o.shape, o.d...  23.7 us
  transfers between devices with their start and end apart: 37, of which 22 were waited for; matrix products, arithmetic and copies ran while one was open for 1% of the time, Pallas kernels for 9%

profile of v3, /device:TPU:1, one launch (start us, length us, event | category | flops | bytes accessed | tf_op | source)
XLA Modules:
  0.0 193.4 jit_solution(16998398433780001311)
XLA Ops:
  0.1 1.1 copy-done
  1.1 0.6 shard_map.17
  1.8 2.2 %collective-permute-start.2 = (bf16[504,512]{1,0:T(8,128)(2,1)S(1)}, bf16[504,512]{1,0:T(8,128)(2,1)S(1)}, u32[]{:S(2)}, u32[]{:S(2)}) collective-permute-start(bf16[504,512]{1,0:T(8,128)(2,1)S(1)} %get-tuple-element.36.refs_0_), channel_id=1, source_target_pairs={{32,0},{0,32},{33,1},{1,33},{34,2},{2,34},{35,3},{3,35},{36,4},{4,... | collective-permute-start | bytes 1548296 | tf_op jit(solution)/shard_map/ppermute | solution.py:40
  4.0 1.2 collective-permute-start.1
  5.2 1.5 collective-permute-start
  6.7 1.5 collective-permute-start.5
  8.2 6.1 %collective-permute-done.2.refs_3_ = bf16[504,512]{1,0:T(8,128)(2,1)S(1)} collective-permute-done((bf16[504,512]{1,0:T(8,128)(2,1)S(1)}, bf16[504,512]{1,0:T(8,128)(2,1)S(1)}, u32[]{:S(2)}, u32[]{:S(2)}) %collective-permute-start.2) | collective-permute-done | bytes 516128 | tf_op jit(solution)/shard_map/ppermute | solution.py:40
  14.3 3.0 %collective-permute-done.1.refs_2_ = bf16[504,512]{1,0:T(8,128)(2,1)S(1)} collective-permute-done((bf16[504,512]{1,0:T(8,128)(2,1)S(1)}, bf16[504,512]{1,0:T(8,128)(2,1)S(1)}, u32[]{:S(2)}, u32[]{:S(2)}) %collective-permute-start.1) | collective-permute-done | bytes 516128 | tf_op jit(solution)/shard_map/ppermute | solution.py:40
  17.3 3.6 %shard_map.18 = (bf16[8,56,896]{2,1,0:T(8,128)(2,1)S(1)}, bf16[8,56,896]{2,1,0:T(8,128)(2,1)S(1)}, bf16[2,896,576]{2,1,0:T(8,128)(2,1)S(1)}, f32[448,896]{1,0:T(8,128)S(1)}) custom-call(s32[2]{0:T(128)S(1)} %pad_add_fusion.place, bf16[448,576]{1,0:T(8,128)(2,1)S(1)} %get-tuple-element.35.own, bf16[504,512]{1,0:T(8,128)(2,1)S(1)} %get-tuple-element.36.refs_0_, ...), custom_call_target="tpu_custom_call" | custom-call | flops 1387266048 | bytes 7053312 | tf_op jit(solution)/shard_map/pallas_call | solution.py:62
  21.0 12.5 %collective-permute-start.7 = (bf16[8,56,896]{2,1,0:T(8,128)(2,1)S(1)}, bf16[8,56,896]{2,1,0:T(8,128)(2,1)S(1)}, u32[]{:S(2)}, u32[]{:S(2)}) collective-permute-start(bf16[8,56,896]{2,1,0:T(8,128)(2,1)S(1)} %get-tuple-element.42), channel_id=1, source_target_pairs={{1,0},{0,1},{3,2},{2,3},{5,4},{4,5},{7,6},{6,7},{9,8},{8,9},{11,10... | collective-permute-start | bytes 2408456 | tf_op jit(solution)/shard_map/ppermute | solution.py:40
  33.5 1.9 shard_map.20
  35.5 2.3 %collective-permute-done.8.high_other = bf16[8,56,896]{2,1,0:T(8,128)(2,1)S(1)} collective-permute-done((bf16[8,56,896]{2,1,0:T(8,128)(2,1)S(1)}, bf16[8,56,896]{2,1,0:T(8,128)(2,1)S(1)}, u32[]{:S(2)}, u32[]{:S(2)}) %collective-permute-start.8) | collective-permute-done | bytes 802848 | tf_op jit(solution)/shard_map/ppermute | solution.py:40
  37.8 0.9 shard_map.21
  38.7 5.6 %collective-permute-start.13 = (bf16[56,896]{1,0:T(8,128)(2,1)S(1)}, bf16[56,896]{1,0:T(8,128)(2,1)S(1)}, u32[]{:S(2)}, u32[]{:S(2)}) collective-permute-start(bf16[56,896]{1,0:T(8,128)(2,1)S(1)} %get-tuple-element.54), channel_id=1, source_target_pairs={{4,0},{8,4},{12,8},{16,12},{20,16},{24,20},{28,24},{0,28},{5,1},{9... | collective-permute-start | bytes 301064 | tf_op jit(solution)/shard_map/ppermute | solution.py:40
  44.4 1.9 %collective-permute-done.13 = bf16[56,896]{1,0:T(8,128)(2,1)S(1)} collective-permute-done((bf16[56,896]{1,0:T(8,128)(2,1)S(1)}, bf16[56,896]{1,0:T(8,128)(2,1)S(1)}, u32[]{:S(2)}, u32[]{:S(2)}) %collective-permute-start.13) | collective-permute-done | bytes 100384 | tf_op jit(solution)/shard_map/ppermute | solution.py:40
  46.4 3.5 %collective-permute-start.14 = (bf16[112,896]{1,0:T(8,128)(2,1)S(1)}, bf16[112,896]{1,0:T(8,128)(2,1)S(1)}, u32[]{:S(2)}, u32[]{:S(2)}) collective-permute-start(bf16[112,896]{1,0:T(8,128)(2,1)S(1)} %pad_maximum_fusion.1), channel_id=1, source_target_pairs={{4,0},{8,4},{12,8},{16,12},{20,16},{24,20},{28,24},{0,28},{5,1},{9... | collective-permute-start | bytes 602120 | tf_op jit(solution)/shard_map/ppermute | solution.py:40
  50.1 3.2 %collective-permute-done.14 = bf16[112,896]{1,0:T(8,128)(2,1)S(1)} collective-permute-done((bf16[112,896]{1,0:T(8,128)(2,1)S(1)}, bf16[112,896]{1,0:T(8,128)(2,1)S(1)}, u32[]{:S(2)}, u32[]{:S(2)}) %collective-permute-start.14) | collective-permute-done | bytes 200736 | tf_op jit(solution)/shard_map/ppermute | solution.py:40
  53.3 3.5 %collective-permute-start.15 = (bf16[112,896]{1,0:T(8,128)(2,1)S(1)}, bf16[112,896]{1,0:T(8,128)(2,1)S(1)}, u32[]{:S(2)}, u32[]{:S(2)}) collective-permute-start(bf16[112,896]{1,0:T(8,128)(2,1)S(1)} %add_convert_fusion.3), channel_id=1, source_target_pairs={{4,0},{8,4},{12,8},{16,12},{20,16},{24,20},{28,24},{0,28},{5,1},{9... | collective-permute-start | bytes 602120 | tf_op jit(solution)/shard_map/ppermute | solution.py:40
  56.9 0.3 collective-permute-start.11
  57.2 2.3 %collective-permute-done.15 = bf16[112,896]{1,0:T(8,128)(2,1)S(1)} collective-permute-done((bf16[112,896]{1,0:T(8,128)(2,1)S(1)}, bf16[112,896]{1,0:T(8,128)(2,1)S(1)}, u32[]{:S(2)}, u32[]{:S(2)}) %collective-permute-start.15) | collective-permute-done | bytes 200736 | tf_op jit(solution)/shard_map/ppermute | solution.py:40
  59.5 3.2 %collective-permute-start.16 = (bf16[112,896]{1,0:T(8,128)(2,1)S(1)}, bf16[112,896]{1,0:T(8,128)(2,1)S(1)}, u32[]{:S(2)}, u32[]{:S(2)}) collective-permute-start(bf16[112,896]{1,0:T(8,128)(2,1)S(1)} %add_convert_fusion.2), channel_id=1, source_target_pairs={{4,0},{8,4},{12,8},{16,12},{20,16},{24,20},{28,24},{0,28},{5,1},{9... | collective-permute-start | bytes 602120 | tf_op jit(solution)/shard_map/ppermute | solution.py:40
  62.7 0.2 collective-permute-done.11
  63.1 2.3 %collective-permute-done.16 = bf16[112,896]{1,0:T(8,128)(2,1)S(1)} collective-permute-done((bf16[112,896]{1,0:T(8,128)(2,1)S(1)}, bf16[112,896]{1,0:T(8,128)(2,1)S(1)}, u32[]{:S(2)}, u32[]{:S(2)}) %collective-permute-start.16) | collective-permute-done | bytes 200736 | tf_op jit(solution)/shard_map/ppermute | solution.py:40
  65.4 3.4 %collective-permute-done.12 = bf16[112,896]{1,0:T(8,128)(2,1)S(1)} collective-permute-done((bf16[112,896]{1,0:T(8,128)(2,1)S(1)}, bf16[112,896]{1,0:T(8,128)(2,1)S(1)}, u32[]{:S(2)}, u32[]{:S(2)}) %collective-permute-start.12) | collective-permute-done | bytes 200736 | tf_op jit(solution)/shard_map/ppermute | solution.py:40
  68.8 0.8 add_convert_fusion.1
  69.6 2.6 %collective-permute-start.17 = (bf16[112,896]{1,0:T(8,128)(2,1)}, bf16[112,896]{1,0:T(8,128)(2,1)}, u32[]{:S(2)}, u32[]{:S(2)}) collective-permute-start(bf16[112,896]{1,0:T(8,128)(2,1)} %add_convert_fusion.1), channel_id=1, source_target_pairs={{2,0},{0,2},{3,1},{1,3},{6,4},{4,6},{7,5},{5,7},{10,8},{8,10},{11,... | collective-permute-start | bytes 602120 | tf_op jit(solution)/shard_map/ppermute | solution.py:40
  72.2 0.9 slice.38
  73.4 2.6 %collective-permute-done.17 = bf16[112,896]{1,0:T(8,128)(2,1)} collective-permute-done((bf16[112,896]{1,0:T(8,128)(2,1)}, bf16[112,896]{1,0:T(8,128)(2,1)}, u32[]{:S(2)}, u32[]{:S(2)}) %collective-permute-start.17) | collective-permute-done | bytes 200736 | tf_op jit(solution)/shard_map/ppermute | solution.py:40
  76.0 1.1 add_convert_fusion
  77.1 0.9 collective-permute-done.19
  78.1 2.7 %collective-permute-start.20 = (bf16[112,896]{1,0:T(8,128)(2,1)S(1)}, bf16[112,896]{1,0:T(8,128)(2,1)S(1)}, u32[]{:S(2)}, u32[]{:S(2)}) collective-permute-start(bf16[112,896]{1,0:T(8,128)(2,1)S(1)} %pad_maximum_fusion.2.refs_0_), channel_id=1, source_target_pairs={{4,0},{8,4},{12,8},{16,12},{20,16},{24,20},{28,24},{0,28},{5,1},{9... | collective-permute-start | bytes 602120 | tf_op jit(solution)/shard_map/ppermute | solution.py:40
  80.8 3.1 %collective-permute-done.23.refs_6_ = bf16[112,896]{1,0:T(8,128)(2,1)S(1)} collective-permute-done((bf16[112,896]{1,0:T(8,128)(2,1)S(1)}, bf16[112,896]{1,0:T(8,128)(2,1)S(1)}, u32[]{:S(2)}, u32[]{:S(2)}) %collective-permute-start.23) | collective-permute-done | bytes 200736 | tf_op jit(solution)/shard_map/ppermute | solution.py:40
  83.9 2.7 %collective-permute-start.21 = (bf16[112,896]{1,0:T(8,128)(2,1)S(1)}, bf16[112,896]{1,0:T(8,128)(2,1)S(1)}, u32[]{:S(2)}, u32[]{:S(2)}) collective-permute-start(bf16[112,896]{1,0:T(8,128)(2,1)S(1)} %collective-permute-done.20.refs_1_), channel_id=1, source_target_pairs={{4,0},{8,4},{12,8},{16,12},{20,16},{24,20},{28,24},{0,28},{5,1},{9... | collective-permute-start | bytes 602120 | tf_op jit(solution)/shard_map/ppermute | solution.py:40
  86.6 5.0 %collective-permute-done.24.refs_5_ = bf16[112,896]{1,0:T(8,128)(2,1)S(1)} collective-permute-done((bf16[112,896]{1,0:T(8,128)(2,1)S(1)}, bf16[112,896]{1,0:T(8,128)(2,1)S(1)}, u32[]{:S(2)}, u32[]{:S(2)}) %collective-permute-start.24) | collective-permute-done | bytes 200736 | tf_op jit(solution)/shard_map/ppermute | solution.py:40
  91.6 2.7 %collective-permute-start.22 = (bf16[112,896]{1,0:T(8,128)(2,1)S(1)}, bf16[112,896]{1,0:T(8,128)(2,1)S(1)}, u32[]{:S(2)}, u32[]{:S(2)}) collective-permute-start(bf16[112,896]{1,0:T(8,128)(2,1)S(1)} %collective-permute-done.21.refs_2_), channel_id=1, source_target_pairs={{4,0},{8,4},{12,8},{16,12},{20,16},{24,20},{28,24},{0,28},{5,1},{9... | collective-permute-start | bytes 602120 | tf_op jit(solution)/shard_map/ppermute | solution.py:40
  94.3 4.1 %collective-permute-done.25.refs_4_ = bf16[112,896]{1,0:T(8,128)(2,1)S(1)} collective-permute-done((bf16[112,896]{1,0:T(8,128)(2,1)S(1)}, bf16[112,896]{1,0:T(8,128)(2,1)S(1)}, u32[]{:S(2)}, u32[]{:S(2)}) %collective-permute-start.25) | collective-permute-done | bytes 200736 | tf_op jit(solution)/shard_map/ppermute | solution.py:40
  98.4 0.6 shard_map.22.group
  99.1 8.8 %collective-permute-start.26 = (bf16[7,112,896]{2,1,0:T(8,128)(2,1)S(1)}, bf16[7,112,896]{2,1,0:T(8,128)(2,1)S(1)}, u32[]{:S(2)}, u32[]{:S(2)}) collective-permute-start(bf16[7,112,896]{2,1,0:T(8,128)(2,1)S(1)} %shard_map.22.group), channel_id=1, source_target_pairs={{1,0},{0,1},{3,2},{2,3},{5,4},{4,5},{7,6},{6,7},{9,8},{8,9},{11,10... | collective-permute-start | bytes 4214792 | tf_op jit(solution)/shard_map/ppermute | solution.py:40
  107.9 0.5 collective-permute-start.6
  108.3 1.0 collective-permute-start.3
  109.3 0.5 collective-permute-start.4
  109.8 3.0 %collective-permute-start.27 = (bf16[56,896]{1,0:T(8,128)(2,1)S(1)}, bf16[56,896]{1,0:T(8,128)(2,1)S(1)}, u32[]{:S(2)}, u32[]{:S(2)}) collective-permute-start(bf16[56,896]{1,0:T(8,128)(2,1)S(1)} %slice.39), channel_id=1, source_target_pairs={{4,0},{8,4},{12,8},{16,12},{20,16},{24,20},{28,24},{0,28},{5,1},{9... | collective-permute-start | bytes 301064 | tf_op jit(solution)/shard_map/ppermute | solution.py:40
  112.8 1.6 collective-permute-done.27
  114.5 5.0 %collective-permute-done.28 = bf16[56,896]{1,0:T(8,128)(2,1)S(1)} collective-permute-done((bf16[56,896]{1,0:T(8,128)(2,1)S(1)}, bf16[56,896]{1,0:T(8,128)(2,1)S(1)}, u32[]{:S(2)}, u32[]{:S(2)}) %collective-permute-start.28) | collective-permute-done | bytes 100384 | tf_op jit(solution)/shard_map/ppermute | solution.py:40
  119.6 3.3 %collective-permute-start.29 = (bf16[112,896]{1,0:T(8,128)(2,1)S(1)}, bf16[112,896]{1,0:T(8,128)(2,1)S(1)}, u32[]{:S(2)}, u32[]{:S(2)}) collective-permute-start(bf16[112,896]{1,0:T(8,128)(2,1)S(1)} %constant_dynamic-update-slice_fusion.mine), channel_id=1, source_target_pairs={{1,0},{0,1},{3,2},{2,3},{5,4},{4,5},{7,6},{6,7},{9,8},{8,9},{11,10... | collective-permute-start | bytes 602120 | tf_op jit(solution)/shard_map/ppermute | solution.py:40
  122.8 9.3 %collective-permute-done.3.refs_0_ = bf16[504,512]{1,0:T(8,128)(2,1)S(1)} collective-permute-done((bf16[504,512]{1,0:T(8,128)(2,1)S(1)}, bf16[504,512]{1,0:T(8,128)(2,1)S(1)}, u32[]{:S(2)}, u32[]{:S(2)}) %collective-permute-start.3) | collective-permute-done | bytes 516128 | tf_op jit(solution)/shard_map/ppermute | solution.py:40
  132.1 11.1 %collective-permute-done.4.refs_1_ = bf16[504,512]{1,0:T(8,128)(2,1)S(1)} collective-permute-done((bf16[504,512]{1,0:T(8,128)(2,1)S(1)}, bf16[504,512]{1,0:T(8,128)(2,1)S(1)}, u32[]{:S(2)}, u32[]{:S(2)}) %collective-permute-start.4) | collective-permute-done | bytes 516128 | tf_op jit(solution)/shard_map/ppermute | solution.py:40
  143.2 1.2 shard_map.19.panel
  144.4 2.5 %shard_map.23 = (bf16[4,448,896]{2,1,0:T(8,128)(2,1)S(1)}, f32[448,576]{1,0:T(8,128)S(1)}) custom-call(s32[2]{0:T(128)S(1)} %pad_add_fusion.place, bf16[4,896,576]{2,1,0:T(8,128)(2,1)S(1)} %shard_map.19.panel, bf16[7,112,896]{2,1,0:T(8,128)(2,1)S(1)} %shard_map.22.group), custom_call_target="tpu_custom_call" | custom-call | flops 924844032 | bytes 9261056 | tf_op jit(solution)/shard_map/pallas_call | solution.py:62
  146.9 2.4 %shard_map.24 = (bf16[4,448,896]{2,1,0:T(8,128)(2,1)S(1)}, f32[448,576]{1,0:T(8,128)S(1)}) custom-call(s32[2]{0:T(128)S(1)} %pad_add_fusion.place, bf16[4,896,576]{2,1,0:T(8,128)(2,1)S(1)} %shard_map.19.panel, bf16[7,112,896]{2,1,0:T(8,128)(2,1)S(1)} %collective-permute-done.26.group, ...), custom_call_target="tpu_custom_call", output_to_operand_aliasing={{0}: (3, {}), {1}: (4, {})} | custom-call | flops 924844032 | bytes 12988416 | tf_op jit(solution)/shard_map/pallas_call | solution.py:62
  149.3 2.5 %shard_map.25 = (bf16[4,448,896]{2,1,0:T(8,128)(2,1)S(1)}, bf16[504,512]{1,0:T(8,128)(2,1)S(1)}, bf16[448,576]{1,0:T(8,128)(2,1)S(1)}) custom-call(s32[2]{0:T(128)S(1)} %pad_add_fusion.place, bf16[448,576]{1,0:T(8,128)(2,1)S(1)} %get-tuple-element.35.own, bf16[4,896,576]{2,1,0:T(8,128)(2,1)S(1)} %shard_map.19.panel, ...), custom_call_target="tpu_custom_call", output_to_operand_aliasing={{0}: (3, {})} | custom-call | flops 231211008 | bytes 13017088 | tf_op jit(solution)/shard_map/pallas_call | solution.py:62
  151.8 0.5 collective-permute-start.32
  152.3 3.4 %collective-permute-start.30 = (bf16[504,512]{1,0:T(8,128)(2,1)S(1)}, bf16[504,512]{1,0:T(8,128)(2,1)S(1)}, u32[]{:S(2)}, u32[]{:S(2)}) collective-permute-start(bf16[504,512]{1,0:T(8,128)(2,1)S(1)} %get-tuple-element.61.refs_0_), channel_id=1, source_target_pairs={{64,0},{128,64},{192,128},{0,192},{65,1},{129,65},{193,129},{1,193... | collective-permute-start | bytes 1548296 | tf_op jit(solution)/shard_map/ppermute | solution.py:40
  155.7 1.2 collective-permute-start.33
  156.9 7.3 %collective-permute-done.32.refs_3_ = bf16[504,512]{1,0:T(8,128)(2,1)S(1)} collective-permute-done((bf16[504,512]{1,0:T(8,128)(2,1)S(1)}, bf16[504,512]{1,0:T(8,128)(2,1)S(1)}, u32[]{:S(2)}, u32[]{:S(2)}) %collective-permute-start.32) | collective-permute-done | bytes 516128 | tf_op jit(solution)/shard_map/ppermute | solution.py:40
  164.2 2.4 %collective-permute-done.31.refs_2_ = bf16[504,512]{1,0:T(8,128)(2,1)S(1)} collective-permute-done((bf16[504,512]{1,0:T(8,128)(2,1)S(1)}, bf16[504,512]{1,0:T(8,128)(2,1)S(1)}, u32[]{:S(2)}, u32[]{:S(2)}) %collective-permute-start.31) | collective-permute-done | bytes 516128 | tf_op jit(solution)/shard_map/ppermute | solution.py:40
  166.6 9.9 %collective-permute-done.30.refs_1_ = bf16[504,512]{1,0:T(8,128)(2,1)S(1)} collective-permute-done((bf16[504,512]{1,0:T(8,128)(2,1)S(1)}, bf16[504,512]{1,0:T(8,128)(2,1)S(1)}, u32[]{:S(2)}, u32[]{:S(2)}) %collective-permute-start.30) | collective-permute-done | bytes 516128 | tf_op jit(solution)/shard_map/ppermute | solution.py:40
  176.5 3.6 %collective-permute-start.34 = (bf16[504,512]{1,0:T(8,128)(2,1)S(1)}, bf16[504,512]{1,0:T(8,128)(2,1)S(1)}, u32[]{:S(2)}, u32[]{:S(2)}) collective-permute-start(bf16[504,512]{1,0:T(8,128)(2,1)S(1)} %collective-permute-done.32.refs_3_), channel_id=1, source_target_pairs={{64,0},{128,64},{192,128},{0,192},{65,1},{129,65},{193,129},{1,193... | collective-permute-start | bytes 1548296 | tf_op jit(solution)/shard_map/ppermute | solution.py:40
  180.1 1.0 collective-permute-start.36
  181.1 3.0 %shard_map.26.before = f32[448,576]{1,0:T(8,128)S(1)} custom-call(s32[2]{0:T(128)S(1)} %pad_add_fusion.place, bf16[448,576]{1,0:T(8,128)(2,1)S(1)} %get-tuple-element.35.own, bf16[448,576]{1,0:T(8,128)(2,1)S(1)} %get-tuple-element.59.w_low, bf16[4,448,896]{2,1,0:T(8,128)(2,1)S(1)} %get-tuple-element.60.gram, bf16[504,512]{1,0:T(8,128)(2,1)S(1)} %get-tuple-element.61.refs_0_, ...), custom_call_target="tpu_custom_call" | custom-call | flops 1156055040 | bytes 6823936 | tf_op jit(solution)/shard_map/pallas_call | solution.py:62
  184.1 1.1 shard_map.27.before
  185.2 4.9 %collective-permute-done.35.r31 = bf16[504,512]{1,0:T(8,128)(2,1)S(1)} collective-permute-done((bf16[504,512]{1,0:T(8,128)(2,1)S(1)}, bf16[504,512]{1,0:T(8,128)(2,1)S(1)}, u32[]{:S(2)}, u32[]{:S(2)}) %collective-permute-start.35) | collective-permute-done | bytes 516128 | tf_op jit(solution)/shard_map/ppermute | solution.py:40
  190.1 1.4 shard_map.28.before
  191.5 1.9 shard_map.29
  (54 shorter events, 1.2 us)
Async XLA Ops:
  0.1 1.1 copy-start
  1.8 12.5 %collective-permute-start.2 = (bf16[504,512]{1,0:T(8,128)(2,1)S(1)}, bf16[504,512]{1,0:T(8,128)(2,1)S(1)}, u32[]{:S(2)}, u32[]{:S(2)}) collective-permute-start(bf16[504,512]{1,0:T(8,128)(2,1)S(1)} %get-tuple-element.36.refs_0_), channel_id=1, source_target_pairs={{32,0},{0,32},{33,1},{1,33},{34,2},{2,34},{35,3},{3,35},{36,4},{4,... | collective-permute-start | bytes 1548296 | tf_op jit(solution)/shard_map/ppermute | solution.py:40
  4.0 13.3 %collective-permute-start.1 = (bf16[504,512]{1,0:T(8,128)(2,1)S(1)}, bf16[504,512]{1,0:T(8,128)(2,1)S(1)}, u32[]{:S(2)}, u32[]{:S(2)}) collective-permute-start(bf16[504,512]{1,0:T(8,128)(2,1)S(1)} %get-tuple-element.36.refs_0_), channel_id=1, source_target_pairs={{192,0},{0,64},{64,128},{128,192},{193,1},{1,65},{65,129},{129,193... | collective-permute-start | bytes 1548296 | tf_op jit(solution)/shard_map/ppermute | solution.py:40
  5.2 12.1 %collective-permute-start = (bf16[504,512]{1,0:T(8,128)(2,1)S(1)}, bf16[504,512]{1,0:T(8,128)(2,1)S(1)}, u32[]{:S(2)}, u32[]{:S(2)}) collective-permute-start(bf16[504,512]{1,0:T(8,128)(2,1)S(1)} %get-tuple-element.36.refs_0_), channel_id=1, source_target_pairs={{64,0},{128,64},{192,128},{0,192},{65,1},{129,65},{193,129},{1,193... | collective-permute-start | bytes 1548296 | tf_op jit(solution)/shard_map/ppermute | solution.py:40
  6.7 26.8 %collective-permute-start.5 = (bf16[504,512]{1,0:T(8,128)(2,1)S(1)}, bf16[504,512]{1,0:T(8,128)(2,1)S(1)}, u32[]{:S(2)}, u32[]{:S(2)}) collective-permute-start(bf16[504,512]{1,0:T(8,128)(2,1)S(1)} %get-tuple-element.36.refs_0_), channel_id=1, source_target_pairs={{128,0},{192,64},{0,128},{64,192},{129,1},{193,65},{1,129},{65,193... | collective-permute-start | bytes 1548296 | tf_op jit(solution)/shard_map/ppermute | solution.py:40
  17.3 3.6 %copy-start.1 = (bf16[504,512]{1,0:T(8,128)(2,1)}, bf16[504,512]{1,0:T(8,128)(2,1)S(1)}, u32[]{:S(2)}) copy-start(bf16[504,512]{1,0:T(8,128)(2,1)S(1)} %collective-permute-done.1.refs_2_) | copy-start | bytes 1548292
  17.3 3.7 %copy-start.3 = (bf16[504,512]{1,0:T(8,128)(2,1)}, bf16[504,512]{1,0:T(8,128)(2,1)S(1)}, u32[]{:S(2)}) copy-start(bf16[504,512]{1,0:T(8,128)(2,1)S(1)} %collective-permute-done.refs_1_) | copy-start | bytes 1548292
  21.0 14.5 %collective-permute-start.7 = (bf16[8,56,896]{2,1,0:T(8,128)(2,1)S(1)}, bf16[8,56,896]{2,1,0:T(8,128)(2,1)S(1)}, u32[]{:S(2)}, u32[]{:S(2)}) collective-permute-start(bf16[8,56,896]{2,1,0:T(8,128)(2,1)S(1)} %get-tuple-element.42), channel_id=1, source_target_pairs={{1,0},{0,1},{3,2},{2,3},{5,4},{4,5},{7,6},{6,7},{9,8},{8,9},{11,10... | collective-permute-start | bytes 2408456 | tf_op jit(solution)/shard_map/ppermute | solution.py:40
  35.4 2.4 %collective-permute-start.8 = (bf16[8,56,896]{2,1,0:T(8,128)(2,1)S(1)}, bf16[8,56,896]{2,1,0:T(8,128)(2,1)S(1)}, u32[]{:S(2)}, u32[]{:S(2)}) collective-permute-start(bf16[8,56,896]{2,1,0:T(8,128)(2,1)S(1)} %get-tuple-element.45), channel_id=1, source_target_pairs={{1,0},{0,1},{3,2},{2,3},{5,4},{4,5},{7,6},{6,7},{9,8},{8,9},{11,10... | collective-permute-start | bytes 2408456 | tf_op jit(solution)/shard_map/ppermute | solution.py:40
  38.7 7.7 %collective-permute-start.13 = (bf16[56,896]{1,0:T(8,128)(2,1)S(1)}, bf16[56,896]{1,0:T(8,128)(2,1)S(1)}, u32[]{:S(2)}, u32[]{:S(2)}) collective-permute-start(bf16[56,896]{1,0:T(8,128)(2,1)S(1)} %get-tuple-element.54), channel_id=1, source_target_pairs={{4,0},{8,4},{12,8},{16,12},{20,16},{24,20},{28,24},{0,28},{5,1},{9... | collective-permute-start | bytes 301064 | tf_op jit(solution)/shard_map/ppermute | solution.py:40
  44.4 5.6 %collective-permute-start.9 = (bf16[56,896]{1,0:T(8,128)(2,1)S(1)}, bf16[56,896]{1,0:T(8,128)(2,1)S(1)}, u32[]{:S(2)}, u32[]{:S(2)}) collective-permute-start(bf16[56,896]{1,0:T(8,128)(2,1)S(1)} %get-tuple-element.50), channel_id=1, source_target_pairs={{28,0},{0,4},{4,8},{8,12},{12,16},{16,20},{20,24},{24,28},{29,1},{... | collective-permute-start | bytes 301064 | tf_op jit(solution)/shard_map/ppermute | solution.py:40
  46.4 6.8 %collective-permute-start.14 = (bf16[112,896]{1,0:T(8,128)(2,1)S(1)}, bf16[112,896]{1,0:T(8,128)(2,1)S(1)}, u32[]{:S(2)}, u32[]{:S(2)}) collective-permute-start(bf16[112,896]{1,0:T(8,128)(2,1)S(1)} %pad_maximum_fusion.1), channel_id=1, source_target_pairs={{4,0},{8,4},{12,8},{16,12},{20,16},{24,20},{28,24},{0,28},{5,1},{9... | collective-permute-start | bytes 602120 | tf_op jit(solution)/shard_map/ppermute | solution.py:40
  50.0 6.8 %collective-permute-start.10 = (bf16[112,896]{1,0:T(8,128)(2,1)S(1)}, bf16[112,896]{1,0:T(8,128)(2,1)S(1)}, u32[]{:S(2)}, u32[]{:S(2)}) collective-permute-start(bf16[112,896]{1,0:T(8,128)(2,1)S(1)} %pad_maximum_fusion), channel_id=1, source_target_pairs={{28,0},{0,4},{4,8},{8,12},{12,16},{16,20},{20,24},{24,28},{29,1},{... | collective-permute-start | bytes 602120 | tf_op jit(solution)/shard_map/ppermute | solution.py:40
  53.3 6.1 %collective-permute-start.15 = (bf16[112,896]{1,0:T(8,128)(2,1)S(1)}, bf16[112,896]{1,0:T(8,128)(2,1)S(1)}, u32[]{:S(2)}, u32[]{:S(2)}) collective-permute-start(bf16[112,896]{1,0:T(8,128)(2,1)S(1)} %add_convert_fusion.3), channel_id=1, source_target_pairs={{4,0},{8,4},{12,8},{16,12},{20,16},{24,20},{28,24},{0,28},{5,1},{9... | collective-permute-start | bytes 602120 | tf_op jit(solution)/shard_map/ppermute | solution.py:40
  56.9 6.0 %collective-permute-start.11 = (bf16[112,896]{1,0:T(8,128)(2,1)S(1)}, bf16[112,896]{1,0:T(8,128)(2,1)S(1)}, u32[]{:S(2)}, u32[]{:S(2)}) collective-permute-start(bf16[112,896]{1,0:T(8,128)(2,1)S(1)} %add_convert_fusion.5), channel_id=1, source_target_pairs={{28,0},{0,4},{4,8},{8,12},{12,16},{16,20},{20,24},{24,28},{29,1},{... | collective-permute-start | bytes 602120 | tf_op jit(solution)/shard_map/ppermute | solution.py:40
  59.5 5.9 %collective-permute-start.16 = (bf16[112,896]{1,0:T(8,128)(2,1)S(1)}, bf16[112,896]{1,0:T(8,128)(2,1)S(1)}, u32[]{:S(2)}, u32[]{:S(2)}) collective-permute-start(bf16[112,896]{1,0:T(8,128)(2,1)S(1)} %add_convert_fusion.2), channel_id=1, source_target_pairs={{4,0},{8,4},{12,8},{16,12},{20,16},{24,20},{28,24},{0,28},{5,1},{9... | collective-permute-start | bytes 602120 | tf_op jit(solution)/shard_map/ppermute | solution.py:40
  63.0 5.9 %collective-permute-start.12 = (bf16[112,896]{1,0:T(8,128)(2,1)S(1)}, bf16[112,896]{1,0:T(8,128)(2,1)S(1)}, u32[]{:S(2)}, u32[]{:S(2)}) collective-permute-start(bf16[112,896]{1,0:T(8,128)(2,1)S(1)} %add_convert_fusion.4), channel_id=1, source_target_pairs={{28,0},{0,4},{4,8},{8,12},{12,16},{16,20},{20,24},{24,28},{29,1},{... | collective-permute-start | bytes 602120 | tf_op jit(solution)/shard_map/ppermute | solution.py:40
  69.6 6.4 %collective-permute-start.17 = (bf16[112,896]{1,0:T(8,128)(2,1)}, bf16[112,896]{1,0:T(8,128)(2,1)}, u32[]{:S(2)}, u32[]{:S(2)}) collective-permute-start(bf16[112,896]{1,0:T(8,128)(2,1)} %add_convert_fusion.1), channel_id=1, source_target_pairs={{2,0},{0,2},{3,1},{1,3},{6,4},{4,6},{7,5},{5,7},{10,8},{8,10},{11,... | collective-permute-start | bytes 602120 | tf_op jit(solution)/shard_map/ppermute | solution.py:40
  73.2 4.8 %collective-permute-start.19 = (bf16[56,896]{1,0:T(8,128)(2,1)S(1)}, bf16[56,896]{1,0:T(8,128)(2,1)S(1)}, u32[]{:S(2)}, u32[]{:S(2)}) collective-permute-start(bf16[56,896]{1,0:T(8,128)(2,1)S(1)} %slice.38), channel_id=1, source_target_pairs={{34,0},{32,2},{2,32},{0,34},{35,1},{33,3},{3,33},{1,35},{38,4},{36... | collective-permute-start | bytes 301064 | tf_op jit(solution)/shard_map/ppermute | solution.py:53
  73.3 4.7 %collective-permute-start.18 = (bf16[56,896]{1,0:T(8,128)(2,1)S(1)}, bf16[56,896]{1,0:T(8,128)(2,1)S(1)}, u32[]{:S(2)}, u32[]{:S(2)}) collective-permute-start(bf16[56,896]{1,0:T(8,128)(2,1)S(1)} %slice.38), channel_id=1, source_target_pairs={{32,0},{0,32},{33,1},{1,33},{34,2},{2,34},{35,3},{3,35},{36,4},{4,... | collective-permute-start | bytes 301064 | tf_op jit(solution)/shard_map/ppermute | solution.py:40
  78.0 30.3 %copy-start.4 = (bf16[504,512]{1,0:T(8,128)(2,1)S(1)}, bf16[504,512]{1,0:T(8,128)(2,1)}, u32[]{:S(2)}) copy-start(bf16[504,512]{1,0:T(8,128)(2,1)} %copy-done.3) | copy-start | bytes 1548292
  78.0 31.3 %copy-start.2 = (bf16[504,512]{1,0:T(8,128)(2,1)S(1)}, bf16[504,512]{1,0:T(8,128)(2,1)}, u32[]{:S(2)}) copy-start(bf16[504,512]{1,0:T(8,128)(2,1)} %copy-done.1) | copy-start | bytes 1548292
  78.0 5.9 %collective-permute-start.23 = (bf16[112,896]{1,0:T(8,128)(2,1)S(1)}, bf16[112,896]{1,0:T(8,128)(2,1)S(1)}, u32[]{:S(2)}, u32[]{:S(2)}) collective-permute-start(bf16[112,896]{1,0:T(8,128)(2,1)S(1)} %pad_maximum_fusion.2.refs_0_), channel_id=1, source_target_pairs={{28,0},{0,4},{4,8},{8,12},{12,16},{16,20},{20,24},{24,28},{29,1},{... | collective-permute-start | bytes 602120 | tf_op jit(solution)/shard_map/ppermute | solution.py:40
  78.1 5.8 %collective-permute-start.20 = (bf16[112,896]{1,0:T(8,128)(2,1)S(1)}, bf16[112,896]{1,0:T(8,128)(2,1)S(1)}, u32[]{:S(2)}, u32[]{:S(2)}) collective-permute-start(bf16[112,896]{1,0:T(8,128)(2,1)S(1)} %pad_maximum_fusion.2.refs_0_), channel_id=1, source_target_pairs={{4,0},{8,4},{12,8},{16,12},{20,16},{24,20},{28,24},{0,28},{5,1},{9... | collective-permute-start | bytes 602120 | tf_op jit(solution)/shard_map/ppermute | solution.py:40
  83.9 7.7 %collective-permute-start.24 = (bf16[112,896]{1,0:T(8,128)(2,1)S(1)}, bf16[112,896]{1,0:T(8,128)(2,1)S(1)}, u32[]{:S(2)}, u32[]{:S(2)}) collective-permute-start(bf16[112,896]{1,0:T(8,128)(2,1)S(1)} %collective-permute-done.23.refs_6_), channel_id=1, source_target_pairs={{28,0},{0,4},{4,8},{8,12},{12,16},{16,20},{20,24},{24,28},{29,1},{... | collective-permute-start | bytes 602120 | tf_op jit(solution)/shard_map/ppermute | solution.py:40
  83.9 7.7 %collective-permute-start.21 = (bf16[112,896]{1,0:T(8,128)(2,1)S(1)}, bf16[112,896]{1,0:T(8,128)(2,1)S(1)}, u32[]{:S(2)}, u32[]{:S(2)}) collective-permute-start(bf16[112,896]{1,0:T(8,128)(2,1)S(1)} %collective-permute-done.20.refs_1_), channel_id=1, source_target_pairs={{4,0},{8,4},{12,8},{16,12},{20,16},{24,20},{28,24},{0,28},{5,1},{9... | collective-permute-start | bytes 602120 | tf_op jit(solution)/shard_map/ppermute | solution.py:40
  91.6 6.8 %collective-permute-start.25 = (bf16[112,896]{1,0:T(8,128)(2,1)S(1)}, bf16[112,896]{1,0:T(8,128)(2,1)S(1)}, u32[]{:S(2)}, u32[]{:S(2)}) collective-permute-start(bf16[112,896]{1,0:T(8,128)(2,1)S(1)} %collective-permute-done.24.refs_5_), channel_id=1, source_target_pairs={{28,0},{0,4},{4,8},{8,12},{12,16},{16,20},{20,24},{24,28},{29,1},{... | collective-permute-start | bytes 602120 | tf_op jit(solution)/shard_map/ppermute | solution.py:40
  91.6 6.8 %collective-permute-start.22 = (bf16[112,896]{1,0:T(8,128)(2,1)S(1)}, bf16[112,896]{1,0:T(8,128)(2,1)S(1)}, u32[]{:S(2)}, u32[]{:S(2)}) collective-permute-start(bf16[112,896]{1,0:T(8,128)(2,1)S(1)} %collective-permute-done.21.refs_2_), channel_id=1, source_target_pairs={{4,0},{8,4},{12,8},{16,12},{20,16},{24,20},{28,24},{0,28},{5,1},{9... | collective-permute-start | bytes 602120 | tf_op jit(solution)/shard_map/ppermute | solution.py:40
  99.1 47.8 %collective-permute-start.26 = (bf16[7,112,896]{2,1,0:T(8,128)(2,1)S(1)}, bf16[7,112,896]{2,1,0:T(8,128)(2,1)S(1)}, u32[]{:S(2)}, u32[]{:S(2)}) collective-permute-start(bf16[7,112,896]{2,1,0:T(8,128)(2,1)S(1)} %shard_map.22.group), channel_id=1, source_target_pairs={{1,0},{0,1},{3,2},{2,3},{5,4},{4,5},{7,6},{6,7},{9,8},{8,9},{11,10... | collective-permute-start | bytes 4214792 | tf_op jit(solution)/shard_map/ppermute | solution.py:40
  107.9 15.0 %collective-permute-start.6 = (bf16[504,512]{1,0:T(8,128)(2,1)S(1)}, bf16[504,512]{1,0:T(8,128)(2,1)S(1)}, u32[]{:S(2)}, u32[]{:S(2)}) collective-permute-start(bf16[504,512]{1,0:T(8,128)(2,1)S(1)} %collective-permute-done.5.refs_3_.block), channel_id=1, source_target_pairs={{32,0},{0,32},{33,1},{1,33},{34,2},{2,34},{35,3},{3,35},{36,4},{4,... | collective-permute-start | bytes 1548296 | tf_op jit(solution)/shard_map/ppermute | solution.py:40
  108.3 23.8 %collective-permute-start.3 = (bf16[504,512]{1,0:T(8,128)(2,1)S(1)}, bf16[504,512]{1,0:T(8,128)(2,1)S(1)}, u32[]{:S(2)}, u32[]{:S(2)}) collective-permute-start(bf16[504,512]{1,0:T(8,128)(2,1)S(1)} %copy-done.4), channel_id=1, source_target_pairs={{32,0},{0,32},{33,1},{1,33},{34,2},{2,34},{35,3},{3,35},{36,4},{4,... | collective-permute-start | bytes 1548296 | tf_op jit(solution)/shard_map/ppermute | solution.py:40
  109.3 33.9 %collective-permute-start.4 = (bf16[504,512]{1,0:T(8,128)(2,1)S(1)}, bf16[504,512]{1,0:T(8,128)(2,1)S(1)}, u32[]{:S(2)}, u32[]{:S(2)}) collective-permute-start(bf16[504,512]{1,0:T(8,128)(2,1)S(1)} %copy-done.2), channel_id=1, source_target_pairs={{32,0},{0,32},{33,1},{1,33},{34,2},{2,34},{35,3},{3,35},{36,4},{4,... | collective-permute-start | bytes 1548296 | tf_op jit(solution)/shard_map/ppermute | solution.py:40
  109.8 4.7 %collective-permute-start.27 = (bf16[56,896]{1,0:T(8,128)(2,1)S(1)}, bf16[56,896]{1,0:T(8,128)(2,1)S(1)}, u32[]{:S(2)}, u32[]{:S(2)}) collective-permute-start(bf16[56,896]{1,0:T(8,128)(2,1)S(1)} %slice.39), channel_id=1, source_target_pairs={{4,0},{8,4},{12,8},{16,12},{20,16},{24,20},{28,24},{0,28},{5,1},{9... | collective-permute-start | bytes 301064 | tf_op jit(solution)/shard_map/ppermute | solution.py:40
  114.5 5.1 %collective-permute-start.28 = (bf16[56,896]{1,0:T(8,128)(2,1)S(1)}, bf16[56,896]{1,0:T(8,128)(2,1)S(1)}, u32[]{:S(2)}, u32[]{:S(2)}) collective-permute-start(bf16[56,896]{1,0:T(8,128)(2,1)S(1)} %slice.40), channel_id=1, source_target_pairs={{28,0},{0,4},{4,8},{8,12},{12,16},{16,20},{20,24},{24,28},{29,1},{... | collective-permute-start | bytes 301064 | tf_op jit(solution)/shard_map/ppermute | solution.py:40
  119.6 29.7 %collective-permute-start.29 = (bf16[112,896]{1,0:T(8,128)(2,1)S(1)}, bf16[112,896]{1,0:T(8,128)(2,1)S(1)}, u32[]{:S(2)}, u32[]{:S(2)}) collective-permute-start(bf16[112,896]{1,0:T(8,128)(2,1)S(1)} %constant_dynamic-update-slice_fusion.mine), channel_id=1, source_target_pairs={{1,0},{0,1},{3,2},{2,3},{5,4},{4,5},{7,6},{6,7},{9,8},{8,9},{11,10... | collective-permute-start | bytes 602120 | tf_op jit(solution)/shard_map/ppermute | solution.py:40
  151.8 12.4 %collective-permute-start.32 = (bf16[504,512]{1,0:T(8,128)(2,1)S(1)}, bf16[504,512]{1,0:T(8,128)(2,1)S(1)}, u32[]{:S(2)}, u32[]{:S(2)}) collective-permute-start(bf16[504,512]{1,0:T(8,128)(2,1)S(1)} %get-tuple-element.61.refs_0_), channel_id=1, source_target_pairs={{32,0},{0,32},{33,1},{1,33},{34,2},{2,34},{35,3},{3,35},{36,4},{4,... | collective-permute-start | bytes 1548296 | tf_op jit(solution)/shard_map/ppermute | solution.py:40
  152.3 14.3 %collective-permute-start.31 = (bf16[504,512]{1,0:T(8,128)(2,1)S(1)}, bf16[504,512]{1,0:T(8,128)(2,1)S(1)}, u32[]{:S(2)}, u32[]{:S(2)}) collective-permute-start(bf16[504,512]{1,0:T(8,128)(2,1)S(1)} %get-tuple-element.61.refs_0_), channel_id=1, source_target_pairs={{192,0},{0,64},{64,128},{128,192},{193,1},{1,65},{65,129},{129,193... | collective-permute-start | bytes 1548296 | tf_op jit(solution)/shard_map/ppermute | solution.py:40
  152.3 24.2 %collective-permute-start.30 = (bf16[504,512]{1,0:T(8,128)(2,1)S(1)}, bf16[504,512]{1,0:T(8,128)(2,1)S(1)}, u32[]{:S(2)}, u32[]{:S(2)}) collective-permute-start(bf16[504,512]{1,0:T(8,128)(2,1)S(1)} %get-tuple-element.61.refs_0_), channel_id=1, source_target_pairs={{64,0},{128,64},{192,128},{0,192},{65,1},{129,65},{193,129},{1,193... | collective-permute-start | bytes 1548296 | tf_op jit(solution)/shard_map/ppermute | solution.py:40
  155.7 24.3 %collective-permute-start.33 = (bf16[504,512]{1,0:T(8,128)(2,1)S(1)}, bf16[504,512]{1,0:T(8,128)(2,1)S(1)}, u32[]{:S(2)}, u32[]{:S(2)}) collective-permute-start(bf16[504,512]{1,0:T(8,128)(2,1)S(1)} %get-tuple-element.61.refs_0_), channel_id=1, source_target_pairs={{128,0},{192,64},{0,128},{64,192},{129,1},{193,65},{1,129},{65,193... | collective-permute-start | bytes 1548296 | tf_op jit(solution)/shard_map/ppermute | solution.py:40
  176.5 13.6 %collective-permute-start.35 = (bf16[504,512]{1,0:T(8,128)(2,1)S(1)}, bf16[504,512]{1,0:T(8,128)(2,1)S(1)}, u32[]{:S(2)}, u32[]{:S(2)}) collective-permute-start(bf16[504,512]{1,0:T(8,128)(2,1)S(1)} %collective-permute-done.32.refs_3_), channel_id=1, source_target_pairs={{192,0},{0,64},{64,128},{128,192},{193,1},{1,65},{65,129},{129,193... | collective-permute-start | bytes 1548296 | tf_op jit(solution)/shard_map/ppermute | solution.py:40
  176.5 13.6 %collective-permute-start.34 = (bf16[504,512]{1,0:T(8,128)(2,1)S(1)}, bf16[504,512]{1,0:T(8,128)(2,1)S(1)}, u32[]{:S(2)}, u32[]{:S(2)}) collective-permute-start(bf16[504,512]{1,0:T(8,128)(2,1)S(1)} %collective-permute-done.32.refs_3_), channel_id=1, source_target_pairs={{64,0},{128,64},{192,128},{0,192},{65,1},{129,65},{193,129},{1,193... | collective-permute-start | bytes 1548296 | tf_op jit(solution)/shard_map/ppermute | solution.py:40
  180.1 11.5 %collective-permute-start.36 = (bf16[504,512]{1,0:T(8,128)(2,1)S(1)}, bf16[504,512]{1,0:T(8,128)(2,1)S(1)}, u32[]{:S(2)}, u32[]{:S(2)}) collective-permute-start(bf16[504,512]{1,0:T(8,128)(2,1)S(1)} %collective-permute-done.33.block), channel_id=1, source_target_pairs={{32,0},{0,32},{33,1},{1,33},{34,2},{2,34},{35,3},{3,35},{36,4},{4,... | collective-permute-start | bytes 1548296 | tf_op jit(solution)/shard_map/ppermute | solution.py:40
